TPU v7x, 256 devices: a whole 4x4x8 slice. The times are simulated.
256 devices in a mesh: fsdp: 32 (over z, x_hi, core), tp: 8 (over x_lo, y).
Axes of the slice: x: 4 (x_hi: 2, x_lo: 2; x = x_hi * 2 + x_lo), y: 4, z: 8, core: 2. Of those that a mesh axis runs over, the one named last changes fastest.
Arguments:
- grad_iterate: bfloat16 [3584, 18432], P('tp', 'fsdp'), may hold values from -0.036828478 to 0.036828478
Outputs:
- update: float32 [3584, 18432], P('tp', 'fsdp')
All inputs are finite; a program needn't handle non-finite values.
Results may differ from a plain program's by a relative error of at most 0.0031.
Values may be sent and summed in bfloat16 or wider, within the bound.
No kernel may reach another device: no remote copies, remote signals or barrier semaphores. Data moves between devices by JAX's collectives and lax.ppermute only.
A program may use at most 64 MiB of HBM per device.

v0:
```python
import math

import jax
import jax.numpy as jnp
from jax import lax
from jax.sharding import Mesh, PartitionSpec as P

C = 18432


quintic_one = 3.4445
quintic_three = -4.775
quintic_five = 2.0315

TP = ("x_lo", "y")
SWAP = [(0, 1), (1, 0)]


def dot(a, b, dims):
    return lax.dot_general(a, b, (dims, ((), ())), preferred_element_type=jnp.float32)


def shift(v, axis, size, by):
    return lax.ppermute(v, axis, [(i, (i + by) % size) for i in range(size)])


def swap(v, axis):
    return lax.ppermute(v, axis, SWAP)


def gather_tp(first, second, early_work=None):
    n = first.shape[0]
    h = n // 2
    whole = jnp.concatenate([first, second], axis=0)
    wave = (swap(whole, "x_lo"), shift(whole, "y", 4, 1), shift(whole, "y", 4, -1))
    (f_x, s_x), (f_left, s_left), (f_right, s_right) = (
        (v[:n], v[n:]) for v in lax.optimization_barrier(wave)
    )
    early = (
        jnp.concatenate([first, f_x, f_left, f_right], axis=0),
        jnp.concatenate([second, s_x, s_left, s_right], axis=0),
    )
    wave = (
        shift(jnp.concatenate([f_x, s_left[:h]], axis=0), "y", 4, 1),
        shift(jnp.concatenate([f_x, s_right[h:]], axis=0), "y", 4, -1),
        swap(s_left, "x_lo"),
    )
    done = early_work(early) if early_work is not None else early
    (to_right, to_left, sx_left), done = lax.optimization_barrier((wave, done))
    fx_left, far_low = to_right[:n], to_right[n:]
    fx_right, far_high = to_left[:n], to_left[n:]
    sx_right = swap(s_right, "x_lo")
    s_far = jnp.concatenate([far_low, far_high], axis=0)
    f_far = shift(f_left, "y", 4, 1)
    fx_far = shift(fx_right, "y", 4, -1)
    sx_far = swap(s_far, "x_lo")
    late = (
        jnp.concatenate([fx_left, fx_right, f_far, fx_far], axis=0),
        jnp.concatenate([sx_left, sx_right, s_far, sx_far], axis=0),
    )
    return early, late, done


def gather_z(v, base):
    rows, columns = v.shape
    h = columns // 2
    z = lax.axis_index("z")
    r1 = shift(v, "z", 8, 1)
    l1 = shift(v, "z", 8, -1)
    r2 = shift(r1, "z", 8, 1)
    l2 = shift(l1, "z", 8, -1)
    r3 = shift(r1, "z", 8, 2)
    l3 = shift(l1, "z", 8, -2)
    far = jnp.concatenate([shift(r2[:, :h], "z", 8, 2), shift(l2[:, h:], "z", 8, -2)], axis=1)
    out = base
    for by, piece in ((0, v), (-1, r1), (1, l1), (-2, r2), (2, l2), (-3, r3), (3, l3), (4, far)):
        out = lax.dynamic_update_slice_in_dim(out, piece, lax.rem(z + by + 8, 8) * rows, 0)
    return out


def halves(v, core):
    half = v.shape[0] // 2
    return (
        lax.dynamic_slice_in_dim(v, core * half, half, 0),
        lax.dynamic_slice_in_dim(v, (1 - core) * half, half, 0),
    )


def low(v):
    return v.astype(jnp.bfloat16)


def wide(v):
    return v.astype(jnp.float32)


def local(x):
    core = lax.axis_index("core")

    def pair_sum(blocks):
        mine, other = blocks
        got = swap(low(dot(x, other, ((1,), (1,)))), "core")
        pair = low(dot(x, mine, ((1,), (1,))) + wide(got))
        return pair.reshape(8, pair.shape[0] // 8, pair.shape[1])

    def exchange_z(pair):
        return lax.all_to_all(pair, "z", 0, 0)

    def finish(split):
        plane = low(jnp.sum(wide(split), axis=0))
        return low(wide(plane) + wide(swap(plane, "x_hi")))

    *parts, pair = gather_tp(*halves(x, core), pair_sum)
    sent = exchange_z(pair)
    sent, pair = lax.optimization_barrier((sent, pair_sum(parts[1])))
    rows = [finish(sent), finish(exchange_z(pair))]
    rows = jnp.concatenate(rows, axis=1)
    gram_mine = gather_z(rows, jnp.zeros((8 * rows.shape[0], rows.shape[1]), rows.dtype))
    gram_other = swap(gram_mine, "core")
    n = rows.shape[1] // 2
    grams = [(gram_mine[:, :n], gram_other[:, :n]), (gram_mine[:, n:], gram_other[:, n:])]

    def apply(blocks):
        total = 0
        for gram, block in zip(grams, blocks):
            for g, b in zip(gram, block):
                total = total + dot(g, b, ((1,), (0,)))
        return total

    applied = apply(parts)
    twice_applied = apply(gather_tp(*halves(low(applied), core))[:2])
    mixed = (
        quintic_one * x.astype(jnp.float32)
        + quintic_three * applied
        + quintic_five * twice_applied
    )
    return mixed * math.sqrt(C)


def solution(mesh):
    grid = Mesh(mesh.devices.reshape(8, 2, 2, 2, 4), ("z", "x_hi", "core", "x_lo", "y"))
    spec = P(TP, ("z", "x_hi", "core"))
    return jax.shard_map(local, mesh=grid, in_specs=(spec,), out_specs=spec, check_vma=False)
```

profile of v0, /device:TPU:32, one launch (start us, length us, event | category | flops | bytes accessed | tf_op | source)
XLA Modules:
  0.0 186.2 jit_solution(6573665768878814701)
XLA Ops:
  6.0 10.0 %collective-permute-done = bf16[448,576]{1,0:T(8,128)(2,1)S(1)} collective-permute-done((bf16[448,576]{1,0:T(8,128)(2,1)S(1)}, bf16[448,576]{1,0:T(8,128)(2,1)S(1)}, u32[]{:S(2)}, u32[]{:S(2)}) %collective-permute-start) | collective-permute-done | bytes 516128 | tf_op jit(solution)/shard_map/ppermute | solution.py:28
  28.3 5.9 %collective-permute-done.5 = bf16[224,576]{1,0:T(8,128)(2,1)S(1)} collective-permute-done((bf16[224,576]{1,0:T(8,128)(2,1)S(1)}, bf16[224,576]{1,0:T(8,128)(2,1)S(1)}, u32[]{:S(2)}, u32[]{:S(2)}) %collective-permute-start.5) | collective-permute-done | bytes 258080 | tf_op jit(solution)/shard_map/ppermute | solution.py:28
  34.8 4.5 %collective-permute-done.9 = bf16[224,576]{1,0:T(8,128)(2,1)S(1)} collective-permute-done((bf16[224,576]{1,0:T(8,128)(2,1)S(1)}, bf16[224,576]{1,0:T(8,128)(2,1)S(1)}, u32[]{:S(2)}, u32[]{:S(2)}) %collective-permute-start.9) | collective-permute-done | bytes 258080 | tf_op jit(solution)/shard_map/ppermute | solution.py:28
  41.1 8.6 %all-to-all-start = ((bf16[8,56,896]{2,1,0:T(8,128)(2,1)}), bf16[8,56,896]{2,1,0:T(8,128)(2,1)S(1)}, u32[]{:S(2)}, u32[]{:S(2)}) async-start(bf16[8,56,896]{2,1,0:T(8,128)(2,1)} %bitcast.2), calls=%async_computation | async-start | bytes 1605632 | tf_op jit(solution)/shard_map/all_to_all | solution.py:107
  53.1 3.0 %collective-permute-start.8 = (bf16[224,576]{1,0:T(8,128)(2,1)S(1)}, bf16[224,576]{1,0:T(8,128)(2,1)S(1)}, u32[]{:S(2)}, u32[]{:S(2)}) collective-permute-start(bf16[224,576]{1,0:T(8,128)(2,1)S(1)} %slice.103), channel_id=1, source_target_pairs={{0,3},{1,0},{2,1},{3,2},{4,7},{5,4},{6,5},{7,6},{8,11},{9,8},{10,9... | collective-permute-start | bytes 774152 | tf_op jit(solution)/shard_map/ppermute | solution.py:24
  56.1 7.0 %collective-permute-done.7 = bf16[224,576]{1,0:T(8,128)(2,1)S(1)} collective-permute-done((bf16[224,576]{1,0:T(8,128)(2,1)S(1)}, bf16[224,576]{1,0:T(8,128)(2,1)S(1)}, u32[]{:S(2)}, u32[]{:S(2)}) %collective-permute-start.7) | collective-permute-done | bytes 258080 | tf_op jit(solution)/shard_map/ppermute | solution.py:24
  65.7 5.0 %all-to-all-done = bf16[8,56,896]{2,1,0:T(8,128)(2,1)S(1)} async-done(((bf16[8,56,896]{2,1,0:T(8,128)(2,1)}), bf16[8,56,896]{2,1,0:T(8,128)(2,1)S(1)}, u32[]{:S(2)}, u32[]{:S(2)}) %all-to-all-start) | async-done | bytes 802848 | tf_op jit(solution)/shard_map/all_to_all | solution.py:107
  70.7 4.9 %all-to-all-start.1 = ((bf16[8,56,896]{2,1,0:T(8,128)(2,1)}), bf16[8,56,896]{2,1,0:T(8,128)(2,1)S(1)}, u32[]{:S(2)}, u32[]{:S(2)}) async-start(bf16[8,56,896]{2,1,0:T(8,128)(2,1)} %bitcast.21), calls=%async_computation.1 | async-start | bytes 1605632 | tf_op jit(solution)/shard_map/all_to_all | solution.py:107
  75.7 3.3 %collective-permute-start.12 = (bf16[56,896]{1,0:T(8,128)(2,1)S(1)}, bf16[56,896]{1,0:T(8,128)(2,1)S(1)}, u32[]{:S(2)}, u32[]{:S(2)}) collective-permute-start(bf16[56,896]{1,0:T(8,128)(2,1)S(1)} %reduce_sum.24), channel_id=1, source_target_pairs={{0,16},{16,0},{1,17},{17,1},{2,18},{18,2},{3,19},{19,3},{4,20},{20... | collective-permute-start | bytes 301064 | tf_op jit(solution)/shard_map/ppermute | solution.py:28
  79.0 17.8 %all-to-all-done.1 = bf16[8,56,896]{2,1,0:T(8,128)(2,1)S(1)} async-done(((bf16[8,56,896]{2,1,0:T(8,128)(2,1)}), bf16[8,56,896]{2,1,0:T(8,128)(2,1)S(1)}, u32[]{:S(2)}, u32[]{:S(2)}) %all-to-all-start.1) | async-done | bytes 802848 | tf_op jit(solution)/shard_map/all_to_all | solution.py:107
  96.9 3.0 %collective-permute-start.13 = (bf16[56,896]{1,0:T(8,128)(2,1)S(1)}, bf16[56,896]{1,0:T(8,128)(2,1)S(1)}, u32[]{:S(2)}, u32[]{:S(2)}) collective-permute-start(bf16[56,896]{1,0:T(8,128)(2,1)S(1)} %reduce_sum.25), channel_id=1, source_target_pairs={{0,16},{16,0},{1,17},{17,1},{2,18},{18,2},{3,19},{19,3},{4,20},{20... | collective-permute-start | bytes 301064 | tf_op jit(solution)/shard_map/ppermute | solution.py:28
  99.9 3.2 %collective-permute-done.13 = bf16[56,896]{1,0:T(8,128)(2,1)S(1)} collective-permute-done((bf16[56,896]{1,0:T(8,128)(2,1)S(1)}, bf16[56,896]{1,0:T(8,128)(2,1)S(1)}, u32[]{:S(2)}, u32[]{:S(2)}) %collective-permute-start.13) | collective-permute-done | bytes 100384 | tf_op jit(solution)/shard_map/ppermute | solution.py:28
  106.0 4.0 %collective-permute-done.14 = bf16[56,1792]{1,0:T(8,128)(2,1)} collective-permute-done((bf16[56,1792]{1,0:T(8,128)(2,1)}, bf16[56,1792]{1,0:T(8,128)(2,1)}, u32[]{:S(2)}, u32[]{:S(2)}) %collective-permute-start.14) | collective-permute-done | bytes 200736 | tf_op jit(solution)/shard_map/ppermute | solution.py:24
  110.2 2.6 %collective-permute-start.18 = (bf16[56,1792]{1,0:T(8,128)(2,1)}, bf16[56,1792]{1,0:T(8,128)(2,1)S(1)}, u32[]{:S(2)}, u32[]{:S(2)}) collective-permute-start(bf16[56,1792]{1,0:T(8,128)(2,1)} %collective-permute-done.14), channel_id=1, source_target_pairs={{0,64},{32,96},{64,128},{96,160},{128,192},{160,224},{192,0},{224,... | collective-permute-start | bytes 602120 | tf_op jit(solution)/shard_map/ppermute | solution.py:24
  113.6 3.2 %collective-permute-start.19 = (bf16[56,1792]{1,0:T(8,128)(2,1)S(1)}, bf16[56,1792]{1,0:T(8,128)(2,1)S(1)}, u32[]{:S(2)}, u32[]{:S(2)}) collective-permute-start(bf16[56,1792]{1,0:T(8,128)(2,1)S(1)} %collective-permute-done.15), channel_id=1, source_target_pairs={{0,192},{32,224},{64,0},{96,32},{128,64},{160,96},{192,128},{224,1... | collective-permute-start | bytes 602120 | tf_op jit(solution)/shard_map/ppermute | solution.py:24
  117.8 3.7 %collective-permute-done.17 = bf16[56,1792]{1,0:T(8,128)(2,1)S(1)} collective-permute-done((bf16[56,1792]{1,0:T(8,128)(2,1)S(1)}, bf16[56,1792]{1,0:T(8,128)(2,1)S(1)}, u32[]{:S(2)}, u32[]{:S(2)}) %collective-permute-start.17) | collective-permute-done | bytes 200736 | tf_op jit(solution)/shard_map/ppermute | solution.py:24
  121.5 4.5 %collective-permute-start.21 = (bf16[56,896]{1,0:T(8,128)(2,1)S(1)}, bf16[56,896]{1,0:T(8,128)(2,1)S(1)}, u32[]{:S(2)}, u32[]{:S(2)}) collective-permute-start(bf16[56,896]{1,0:T(8,128)(2,1)S(1)} %slice.125), channel_id=1, source_target_pairs={{0,192},{32,224},{64,0},{96,32},{128,64},{160,96},{192,128},{224,1... | collective-permute-start | bytes 301064 | tf_op jit(solution)/shard_map/ppermute | solution.py:24
  128.4 5.5 %collective-permute-done.20 = bf16[56,896]{1,0:T(8,128)(2,1)S(1)} collective-permute-done((bf16[56,896]{1,0:T(8,128)(2,1)S(1)}, bf16[56,896]{1,0:T(8,128)(2,1)S(1)}, u32[]{:S(2)}, u32[]{:S(2)}) %collective-permute-start.20) | collective-permute-done | bytes 100384 | tf_op jit(solution)/shard_map/ppermute | solution.py:24
  141.7 3.2 %collective-permute-start.25 = (bf16[448,576]{1,0:T(8,128)(2,1)S(1)}, bf16[448,576]{1,0:T(8,128)(2,1)S(1)}, u32[]{:S(2)}, u32[]{:S(2)}) collective-permute-start(bf16[448,576]{1,0:T(8,128)(2,1)S(1)} %pad_maximum_fusion.6), channel_id=1, source_target_pairs={{0,3},{1,0},{2,1},{3,2},{4,7},{5,4},{6,5},{7,6},{8,11},{9,8},{10,9... | collective-permute-start | bytes 1548296 | tf_op jit(solution)/shard_map/ppermute | solution.py:24
  145.0 10.6 %collective-permute-done.23 = bf16[448,576]{1,0:T(8,128)(2,1)S(1)} collective-permute-done((bf16[448,576]{1,0:T(8,128)(2,1)S(1)}, bf16[448,576]{1,0:T(8,128)(2,1)S(1)}, u32[]{:S(2)}, u32[]{:S(2)}) %collective-permute-start.23) | collective-permute-done | bytes 516128 | tf_op jit(solution)/shard_map/ppermute | solution.py:28
  158.0 3.2 %collective-permute-start.27 = (bf16[336,576]{1,0:T(8,128)(2,1)S(1)}, bf16[336,576]{1,0:T(8,128)(2,1)S(1)}, u32[]{:S(2)}, u32[]{:S(2)}) collective-permute-start(bf16[336,576]{1,0:T(8,128)(2,1)S(1)} %get-tuple-element.59), channel_id=1, source_target_pairs={{0,3},{1,0},{2,1},{3,2},{4,7},{5,4},{6,5},{7,6},{8,11},{9,8},{10,9... | collective-permute-start | bytes 1161224 | tf_op jit(solution)/shard_map/ppermute | solution.py:24
  163.5 7.6 %collective-permute-done.28 = bf16[224,576]{1,0:T(8,128)(2,1)S(1)} collective-permute-done((bf16[224,576]{1,0:T(8,128)(2,1)S(1)}, bf16[224,576]{1,0:T(8,128)(2,1)S(1)}, u32[]{:S(2)}, u32[]{:S(2)}) %collective-permute-start.28) | collective-permute-done | bytes 258080 | tf_op jit(solution)/shard_map/ppermute | solution.py:28
  172.0 2.6 %collective-permute-done.31 = bf16[224,576]{1,0:T(8,128)(2,1)S(1)} collective-permute-done((bf16[224,576]{1,0:T(8,128)(2,1)S(1)}, bf16[224,576]{1,0:T(8,128)(2,1)S(1)}, u32[]{:S(2)}, u32[]{:S(2)}) %collective-permute-start.31) | collective-permute-done | bytes 258080 | tf_op jit(solution)/shard_map/ppermute | solution.py:28
  178.1 3.4 %collective-permute-done.32 = bf16[224,576]{1,0:T(8,128)(2,1)S(1)} collective-permute-done((bf16[224,576]{1,0:T(8,128)(2,1)S(1)}, bf16[224,576]{1,0:T(8,128)(2,1)S(1)}, u32[]{:S(2)}, u32[]{:S(2)}) %collective-permute-start.32) | collective-permute-done | bytes 258080 | tf_op jit(solution)/shard_map/ppermute | solution.py:28
  (150 shorter events, 55.4 us)
Async XLA Ops:
  1.2 14.8 %collective-permute-start = (bf16[448,576]{1,0:T(8,128)(2,1)S(1)}, bf16[448,576]{1,0:T(8,128)(2,1)S(1)}, u32[]{:S(2)}, u32[]{:S(2)}) collective-permute-start(bf16[448,576]{1,0:T(8,128)(2,1)S(1)} %pad_maximum_fusion.5), channel_id=1, source_target_pairs={{0,4},{4,0},{1,5},{5,1},{2,6},{6,2},{3,7},{7,3},{8,12},{12,8},{9,1... | collective-permute-start | bytes 1548296 | tf_op jit(solution)/shard_map/ppermute | solution.py:28
  2.7 15.7 %collective-permute-start.1 = (bf16[448,576]{1,0:T(8,128)(2,1)S(1)}, bf16[448,576]{1,0:T(8,128)(2,1)S(1)}, u32[]{:S(2)}, u32[]{:S(2)}) collective-permute-start(bf16[448,576]{1,0:T(8,128)(2,1)S(1)} %pad_maximum_fusion.5), channel_id=1, source_target_pairs={{0,1},{1,2},{2,3},{3,0},{4,5},{5,6},{6,7},{7,4},{8,9},{9,10},{10,1... | collective-permute-start | bytes 1548296 | tf_op jit(solution)/shard_map/ppermute | solution.py:24
  4.3 14.2 %collective-permute-start.2 = (bf16[448,576]{1,0:T(8,128)(2,1)S(1)}, bf16[448,576]{1,0:T(8,128)(2,1)S(1)}, u32[]{:S(2)}, u32[]{:S(2)}) collective-permute-start(bf16[448,576]{1,0:T(8,128)(2,1)S(1)} %pad_maximum_fusion.5), channel_id=1, source_target_pairs={{0,3},{1,0},{2,1},{3,2},{4,7},{5,4},{6,5},{7,6},{8,11},{9,8},{10,9... | collective-permute-start | bytes 1548296 | tf_op jit(solution)/shard_map/ppermute | solution.py:24
  21.1 13.6 %collective-permute-start.3 = (bf16[336,576]{1,0:T(8,128)(2,1)S(1)}, bf16[336,576]{1,0:T(8,128)(2,1)S(1)}, u32[]{:S(2)}, u32[]{:S(2)}) collective-permute-start(bf16[336,576]{1,0:T(8,128)(2,1)S(1)} %get-tuple-element.62), channel_id=1, source_target_pairs={{0,1},{1,2},{2,3},{3,0},{4,5},{5,6},{6,7},{7,4},{8,9},{9,10},{10,1... | collective-permute-start | bytes 1161224 | tf_op jit(solution)/shard_map/ppermute | solution.py:24
  22.8 12.0 %collective-permute-start.4 = (bf16[336,576]{1,0:T(8,128)(2,1)S(1)}, bf16[336,576]{1,0:T(8,128)(2,1)S(1)}, u32[]{:S(2)}, u32[]{:S(2)}) collective-permute-start(bf16[336,576]{1,0:T(8,128)(2,1)S(1)} %get-tuple-element.61), channel_id=1, source_target_pairs={{0,3},{1,0},{2,1},{3,2},{4,7},{5,4},{6,5},{7,6},{8,11},{9,8},{10,9... | collective-permute-start | bytes 1161224 | tf_op jit(solution)/shard_map/ppermute | solution.py:24
  24.4 9.7 %collective-permute-start.5 = (bf16[224,576]{1,0:T(8,128)(2,1)S(1)}, bf16[224,576]{1,0:T(8,128)(2,1)S(1)}, u32[]{:S(2)}, u32[]{:S(2)}) collective-permute-start(bf16[224,576]{1,0:T(8,128)(2,1)S(1)} %get-tuple-element.44), channel_id=1, source_target_pairs={{0,4},{4,0},{1,5},{5,1},{2,6},{6,2},{3,7},{7,3},{8,12},{12,8},{9,1... | collective-permute-start | bytes 774152 | tf_op jit(solution)/shard_map/ppermute | solution.py:28
  25.0 14.3 %collective-permute-start.9 = (bf16[224,576]{1,0:T(8,128)(2,1)S(1)}, bf16[224,576]{1,0:T(8,128)(2,1)S(1)}, u32[]{:S(2)}, u32[]{:S(2)}) collective-permute-start(bf16[224,576]{1,0:T(8,128)(2,1)S(1)} %get-tuple-element.46), channel_id=1, source_target_pairs={{0,4},{4,0},{1,5},{5,1},{2,6},{6,2},{3,7},{7,3},{8,12},{12,8},{9,1... | collective-permute-start | bytes 774152 | tf_op jit(solution)/shard_map/ppermute | solution.py:28
  41.1 29.6 %all-to-all-start = ((bf16[8,56,896]{2,1,0:T(8,128)(2,1)}), bf16[8,56,896]{2,1,0:T(8,128)(2,1)S(1)}, u32[]{:S(2)}, u32[]{:S(2)}) async-start(bf16[8,56,896]{2,1,0:T(8,128)(2,1)} %bitcast.2), calls=%async_computation | async-start | bytes 1605632 | tf_op jit(solution)/shard_map/all_to_all | solution.py:107
  52.6 10.6 %collective-permute-start.11 = (bf16[448,896]{1,0:T(8,128)(2,1)S(1)}, bf16[448,896]{1,0:T(8,128)(2,1)S(1)}, u32[]{:S(2)}, u32[]{:S(2)}) collective-permute-start(bf16[448,896]{1,0:T(8,128)(2,1)S(1)} %fusion.10), channel_id=1, source_target_pairs={{0,8},{8,0},{1,9},{9,1},{2,10},{10,2},{3,11},{11,3},{4,12},{12,4},... | collective-permute-start | bytes 2408456 | tf_op jit(solution)/shard_map/ppermute | solution.py:28
  52.7 10.5 %collective-permute-start.7 = (bf16[224,576]{1,0:T(8,128)(2,1)S(1)}, bf16[224,576]{1,0:T(8,128)(2,1)S(1)}, u32[]{:S(2)}, u32[]{:S(2)}) collective-permute-start(bf16[224,576]{1,0:T(8,128)(2,1)S(1)} %get-tuple-element.43), channel_id=1, source_target_pairs={{0,1},{1,2},{2,3},{3,0},{4,5},{5,6},{6,7},{7,4},{8,9},{9,10},{10,1... | collective-permute-start | bytes 774152 | tf_op jit(solution)/shard_map/ppermute | solution.py:24
  53.1 10.0 %collective-permute-start.8 = (bf16[224,576]{1,0:T(8,128)(2,1)S(1)}, bf16[224,576]{1,0:T(8,128)(2,1)S(1)}, u32[]{:S(2)}, u32[]{:S(2)}) collective-permute-start(bf16[224,576]{1,0:T(8,128)(2,1)S(1)} %slice.103), channel_id=1, source_target_pairs={{0,3},{1,0},{2,1},{3,2},{4,7},{5,4},{6,5},{7,6},{8,11},{9,8},{10,9... | collective-permute-start | bytes 774152 | tf_op jit(solution)/shard_map/ppermute | solution.py:24
  70.7 26.1 %all-to-all-start.1 = ((bf16[8,56,896]{2,1,0:T(8,128)(2,1)}), bf16[8,56,896]{2,1,0:T(8,128)(2,1)S(1)}, u32[]{:S(2)}, u32[]{:S(2)}) async-start(bf16[8,56,896]{2,1,0:T(8,128)(2,1)} %bitcast.21), calls=%async_computation.1 | async-start | bytes 1605632 | tf_op jit(solution)/shard_map/all_to_all | solution.py:107
  75.7 24.2 %collective-permute-start.12 = (bf16[56,896]{1,0:T(8,128)(2,1)S(1)}, bf16[56,896]{1,0:T(8,128)(2,1)S(1)}, u32[]{:S(2)}, u32[]{:S(2)}) collective-permute-start(bf16[56,896]{1,0:T(8,128)(2,1)S(1)} %reduce_sum.24), channel_id=1, source_target_pairs={{0,16},{16,0},{1,17},{17,1},{2,18},{18,2},{3,19},{19,3},{4,20},{20... | collective-permute-start | bytes 301064 | tf_op jit(solution)/shard_map/ppermute | solution.py:28
  110.0 16.0 %collective-permute-start.16 = (bf16[56,1792]{1,0:T(8,128)(2,1)}, bf16[56,1792]{1,0:T(8,128)(2,1)S(1)}, u32[]{:S(2)}, u32[]{:S(2)}) collective-permute-start(bf16[56,1792]{1,0:T(8,128)(2,1)} %collective-permute-done.14), channel_id=1, source_target_pairs={{0,32},{32,64},{64,96},{96,128},{128,160},{160,192},{192,224},{224... | collective-permute-start | bytes 602120 | tf_op jit(solution)/shard_map/ppermute | solution.py:24
  110.2 17.8 %collective-permute-start.18 = (bf16[56,1792]{1,0:T(8,128)(2,1)}, bf16[56,1792]{1,0:T(8,128)(2,1)S(1)}, u32[]{:S(2)}, u32[]{:S(2)}) collective-permute-start(bf16[56,1792]{1,0:T(8,128)(2,1)} %collective-permute-done.14), channel_id=1, source_target_pairs={{0,64},{32,96},{64,128},{96,160},{128,192},{160,224},{192,0},{224,... | collective-permute-start | bytes 602120 | tf_op jit(solution)/shard_map/ppermute | solution.py:24
  113.6 14.5 %collective-permute-start.19 = (bf16[56,1792]{1,0:T(8,128)(2,1)S(1)}, bf16[56,1792]{1,0:T(8,128)(2,1)S(1)}, u32[]{:S(2)}, u32[]{:S(2)}) collective-permute-start(bf16[56,1792]{1,0:T(8,128)(2,1)S(1)} %collective-permute-done.15), channel_id=1, source_target_pairs={{0,192},{32,224},{64,0},{96,32},{128,64},{160,96},{192,128},{224,1... | collective-permute-start | bytes 602120 | tf_op jit(solution)/shard_map/ppermute | solution.py:24
  140.5 15.1 %collective-permute-start.23 = (bf16[448,576]{1,0:T(8,128)(2,1)S(1)}, bf16[448,576]{1,0:T(8,128)(2,1)S(1)}, u32[]{:S(2)}, u32[]{:S(2)}) collective-permute-start(bf16[448,576]{1,0:T(8,128)(2,1)S(1)} %pad_maximum_fusion.6), channel_id=1, source_target_pairs={{0,4},{4,0},{1,5},{5,1},{2,6},{6,2},{3,7},{7,3},{8,12},{12,8},{9,1... | collective-permute-start | bytes 1548296 | tf_op jit(solution)/shard_map/ppermute | solution.py:28
  141.7 16.0 %collective-permute-start.24 = (bf16[448,576]{1,0:T(8,128)(2,1)S(1)}, bf16[448,576]{1,0:T(8,128)(2,1)S(1)}, u32[]{:S(2)}, u32[]{:S(2)}) collective-permute-start(bf16[448,576]{1,0:T(8,128)(2,1)S(1)} %pad_maximum_fusion.6), channel_id=1, source_target_pairs={{0,1},{1,2},{2,3},{3,0},{4,5},{5,6},{6,7},{7,4},{8,9},{9,10},{10,1... | collective-permute-start | bytes 1548296 | tf_op jit(solution)/shard_map/ppermute | solution.py:24
  141.7 16.0 %collective-permute-start.25 = (bf16[448,576]{1,0:T(8,128)(2,1)S(1)}, bf16[448,576]{1,0:T(8,128)(2,1)S(1)}, u32[]{:S(2)}, u32[]{:S(2)}) collective-permute-start(bf16[448,576]{1,0:T(8,128)(2,1)S(1)} %pad_maximum_fusion.6), channel_id=1, source_target_pairs={{0,3},{1,0},{2,1},{3,2},{4,7},{5,4},{6,5},{7,6},{8,11},{9,8},{10,9... | collective-permute-start | bytes 1548296 | tf_op jit(solution)/shard_map/ppermute | solution.py:24
  157.9 14.1 %collective-permute-start.26 = (bf16[336,576]{1,0:T(8,128)(2,1)S(1)}, bf16[336,576]{1,0:T(8,128)(2,1)S(1)}, u32[]{:S(2)}, u32[]{:S(2)}) collective-permute-start(bf16[336,576]{1,0:T(8,128)(2,1)S(1)} %get-tuple-element.60), channel_id=1, source_target_pairs={{0,1},{1,2},{2,3},{3,0},{4,5},{5,6},{6,7},{7,4},{8,9},{9,10},{10,1... | collective-permute-start | bytes 1161224 | tf_op jit(solution)/shard_map/ppermute | solution.py:24
  158.0 14.0 %collective-permute-start.27 = (bf16[336,576]{1,0:T(8,128)(2,1)S(1)}, bf16[336,576]{1,0:T(8,128)(2,1)S(1)}, u32[]{:S(2)}, u32[]{:S(2)}) collective-permute-start(bf16[336,576]{1,0:T(8,128)(2,1)S(1)} %get-tuple-element.59), channel_id=1, source_target_pairs={{0,3},{1,0},{2,1},{3,2},{4,7},{5,4},{6,5},{7,6},{8,11},{9,8},{10,9... | collective-permute-start | bytes 1161224 | tf_op jit(solution)/shard_map/ppermute | solution.py:24
  161.2 9.9 %collective-permute-start.28 = (bf16[224,576]{1,0:T(8,128)(2,1)S(1)}, bf16[224,576]{1,0:T(8,128)(2,1)S(1)}, u32[]{:S(2)}, u32[]{:S(2)}) collective-permute-start(bf16[224,576]{1,0:T(8,128)(2,1)S(1)} %get-tuple-element.40), channel_id=1, source_target_pairs={{0,4},{4,0},{1,5},{5,1},{2,6},{6,2},{3,7},{7,3},{8,12},{12,8},{9,1... | collective-permute-start | bytes 774152 | tf_op jit(solution)/shard_map/ppermute | solution.py:28
  162.2 12.4 %collective-permute-start.31 = (bf16[224,576]{1,0:T(8,128)(2,1)S(1)}, bf16[224,576]{1,0:T(8,128)(2,1)S(1)}, u32[]{:S(2)}, u32[]{:S(2)}) collective-permute-start(bf16[224,576]{1,0:T(8,128)(2,1)S(1)} %get-tuple-element.36), channel_id=1, source_target_pairs={{0,4},{4,0},{1,5},{5,1},{2,6},{6,2},{3,7},{7,3},{8,12},{12,8},{9,1... | collective-permute-start | bytes 774152 | tf_op jit(solution)/shard_map/ppermute | solution.py:28
  163.5 19.0 %collective-permute-start.29 = (bf16[224,576]{1,0:T(8,128)(2,1)S(1)}, bf16[224,576]{1,0:T(8,128)(2,1)S(1)}, u32[]{:S(2)}, u32[]{:S(2)}) collective-permute-start(bf16[224,576]{1,0:T(8,128)(2,1)S(1)} %get-tuple-element.39), channel_id=1, source_target_pairs={{0,1},{1,2},{2,3},{3,0},{4,5},{5,6},{6,7},{7,4},{8,9},{9,10},{10,1... | collective-permute-start | bytes 774152 | tf_op jit(solution)/shard_map/ppermute | solution.py:24
  (34 other events, 200.2 us)
where the time goes:
time: 187 us; the launch traced here: 186 us
  waiting for transfers between devices  102 us (55%)
  starting transfers between devices  60 us (32%)
  matrix products  14.8 us (8%)
  local copies, waits for them, and re-layouts  6.35 us (3%)
  other arithmetic  2.11 us (1%)
    ppermute x13, waiting for transfers between devices, swap(): return lax.ppermute(v, axis, SWAP)  50.2 us
    ppermute x20, starting transfers between devices, shift(): return lax.ppermute(v, axis, [(i, (i + by) % size) for i in range(size)])  31.4 us
    ppermute x20, waiting for transfers between devices, shift(): return lax.ppermute(v, axis, [(i, (i + by) % size) for i in range(size)])  29.5 us
    all_to_all x2, waiting for transfers between devices, exchange_z(): return lax.all_to_all(pair, 'z', 0, 0)  22.7 us
    ppermute x13, starting transfers between devices, swap(): return lax.ppermute(v, axis, SWAP)  15.1 us
    dot_general x12, matrix products, dot(): lax.dot_general(a, b, (dims, ((), ())), preferred_element_type=jnp.float32)  14.8 us
    all_to_all x2, starting transfers between devices, exchange_z(): return lax.all_to_all(pair, 'z', 0, 0)  13.5 us
  transfers between devices with their start and end apart: 35, of which 23 were waited for; matrix products, arithmetic and copies ran while one was open for 6% of the time, Pallas kernels for 0%

commit v1 on v0

--- a/solution.py
+++ b/solution.py
@@ -40,23 +40,27 @@
         jnp.concatenate([first, f_x, f_left, f_right], axis=0),
         jnp.concatenate([second, s_x, s_left, s_right], axis=0),
     )
-    wave = (
-        shift(jnp.concatenate([f_x, s_left[:h]], axis=0), "y", 4, 1),
-        shift(jnp.concatenate([f_x, s_right[h:]], axis=0), "y", 4, -1),
-        swap(s_left, "x_lo"),
-    )
+    right = jnp.concatenate([f_x, s_left[:h]], axis=0)
+    left = jnp.concatenate([f_x, s_right[h:]], axis=0)
+    across = s_left if early_work is not None else jnp.concatenate([s_left, s_right], axis=0)
+    wave = (shift(right, "y", 4, 1), shift(left, "y", 4, -1), swap(across, "x_lo"))
     done = early_work(early) if early_work is not None else early
-    (to_right, to_left, sx_left), done = lax.optimization_barrier((wave, done))
+    (to_right, to_left, across), done = lax.optimization_barrier((wave, done))
     fx_left, far_low = to_right[:n], to_right[n:]
     fx_right, far_high = to_left[:n], to_left[n:]
-    sx_right = swap(s_right, "x_lo")
-    s_far = jnp.concatenate([far_low, far_high], axis=0)
-    f_far = shift(f_left, "y", 4, 1)
-    fx_far = shift(fx_right, "y", 4, -1)
-    sx_far = swap(s_far, "x_lo")
+    far = [far_low, far_high]
+    if early_work is not None:
+        last = swap(jnp.concatenate([s_right] + far, axis=0), "x_lo")
+    else:
+        last = swap(jnp.concatenate(far, axis=0), "x_lo")
+    wave = (last, shift(f_left, "y", 4, 1), shift(fx_right, "y", 4, -1))
+    last, f_far, fx_far = lax.optimization_barrier(wave)
+    s_late = [across, far_low, far_high, last]
+    if early_work is not None:
+        s_late = [across, last[:n], far_low, far_high, last[n:]]
     late = (
         jnp.concatenate([fx_left, fx_right, f_far, fx_far], axis=0),
-        jnp.concatenate([sx_left, sx_right, s_far, sx_far], axis=0),
+        jnp.concatenate(s_late, axis=0),
     )
     return early, late, done
 
@@ -118,17 +122,17 @@
     gram_mine = gather_z(rows, jnp.zeros((8 * rows.shape[0], rows.shape[1]), rows.dtype))
     gram_other = swap(gram_mine, "core")
     n = rows.shape[1] // 2
-    grams = [(gram_mine[:, :n], gram_other[:, :n]), (gram_mine[:, n:], gram_other[:, n:])]
+    grams = [g[:, i : i + n] for i in (0, n) for g in (gram_mine, gram_other)]
 
-    def apply(blocks):
+    def apply(blocks, order):
+        flat = [b for part in blocks for b in part]
         total = 0
-        for gram, block in zip(grams, blocks):
-            for g, b in zip(gram, block):
-                total = total + dot(g, b, ((1,), (0,)))
+        for i in order:
+            total = total + dot(grams[i], flat[i], ((1,), (0,)))
         return total
 
-    applied = apply(parts)
-    twice_applied = apply(gather_tp(*halves(low(applied), core))[:2])
+    applied = apply(parts, (0, 2, 1, 3))
+    twice_applied = apply(gather_tp(*halves(low(applied), core))[:2], (0, 1, 2, 3))
     mixed = (
         quintic_one * x.astype(jnp.float32)
         + quintic_three * applied

time: 187 us -> 191 us (1.021)
  local copies, waits for them, and re-layouts: 6.35 us -> 9.98 us
    ppermute x13 -> x11, waiting for transfers between devices: 50.2 us -> 15.5 us  [swap(): return lax.ppermute(v, axis, SWAP)]
    ppermute x20, waiting for transfers between devices: 29.5 us -> 58.4 us  [shift(): return lax.ppermute(v, axis, [(i, (i + by) % size) for i in range(size)])]
    all_to_all x2, waiting for transfers between devices: 22.7 us -> 28.2 us  [exchange_z(): return lax.all_to_all(pair, 'z', 0, 0)]
    unnamed x48 -> x38, local copies, waits for them, and re-layouts: 2.65 us -> 5.15 us
    ppermute x13 -> x11, starting transfers between devices: 15.1 us -> 12.9 us  [swap(): return lax.ppermute(v, axis, SWAP)]
  transfers between devices with their start and end apart: 35 -> 33, of which waited for: 23 -> 22; matrix products, arithmetic and copies ran while one was open for 6% -> 8% of each run, Pallas kernels for 0% -> 0%
where the time goes in v1:
time: 191 us; the launch traced here: 189 us
  waiting for transfers between devices  102 us (53%)
  starting transfers between devices  58.1 us (30%)
  matrix products  15.8 us (8%)
  local copies, waits for them, and re-layouts  9.98 us (5%)
  other arithmetic  2.22 us (1%)
    ppermute x20, waiting for transfers between devices, shift(): return lax.ppermute(v, axis, [(i, (i + by) % size) for i in range(size)])  58.4 us
    ppermute x20, starting transfers between devices, shift(): return lax.ppermute(v, axis, [(i, (i + by) % size) for i in range(size)])  31.7 us
    all_to_all x2, waiting for transfers between devices, exchange_z(): return lax.all_to_all(pair, 'z', 0, 0)  28.2 us
    dot_general x12, matrix products, dot(): lax.dot_general(a, b, (dims, ((), ())), preferred_element_type=jnp.float32)  15.8 us
    ppermute x11, waiting for transfers between devices, swap(): return lax.ppermute(v, axis, SWAP)  15.5 us
    all_to_all x2, starting transfers between devices, exchange_z(): return lax.all_to_all(pair, 'z', 0, 0)  13.5 us
    ppermute x11, starting transfers between devices, swap(): return lax.ppermute(v, axis, SWAP)  12.9 us
    unnamed x38, local copies, waits for them, and re-layouts  5.15 us
  transfers between devices with their start and end apart: 33, of which 22 were waited for; matrix products, arithmetic and copies ran while one was open for 8% of the time, Pallas kernels for 0%

profile of v1, /device:TPU:32, one launch (start us, length us, event | category | flops | bytes accessed | tf_op | source)
XLA Modules:
  0.0 188.9 jit_solution(9564230651824981528)
XLA Ops:
  1.2 3.1 %collective-permute-start.2 = (bf16[448,576]{1,0:T(8,128)(2,1)S(1)}, bf16[448,576]{1,0:T(8,128)(2,1)S(1)}, u32[]{:S(2)}, u32[]{:S(2)}) collective-permute-start(bf16[448,576]{1,0:T(8,128)(2,1)S(1)} %pad_maximum_fusion.5), channel_id=1, source_target_pairs={{0,3},{1,0},{2,1},{3,2},{4,7},{5,4},{6,5},{7,6},{8,11},{9,8},{10,9... | collective-permute-start | bytes 1548296 | tf_op jit(solution)/shard_map/ppermute | solution.py:24
  5.7 10.7 %collective-permute-done.2 = bf16[448,576]{1,0:T(8,128)(2,1)S(1)} collective-permute-done((bf16[448,576]{1,0:T(8,128)(2,1)S(1)}, bf16[448,576]{1,0:T(8,128)(2,1)S(1)}, u32[]{:S(2)}, u32[]{:S(2)}) %collective-permute-start.2) | collective-permute-done | bytes 516128 | tf_op jit(solution)/shard_map/ppermute | solution.py:24
  16.5 3.4 %collective-permute-done.1 = bf16[448,576]{1,0:T(8,128)(2,1)S(1)} collective-permute-done((bf16[448,576]{1,0:T(8,128)(2,1)S(1)}, bf16[448,576]{1,0:T(8,128)(2,1)S(1)}, u32[]{:S(2)}, u32[]{:S(2)}) %collective-permute-start.1) | collective-permute-done | bytes 516128 | tf_op jit(solution)/shard_map/ppermute | solution.py:24
  28.0 5.3 %collective-permute-done.5 = bf16[224,576]{1,0:T(8,128)(2,1)S(1)} collective-permute-done((bf16[224,576]{1,0:T(8,128)(2,1)S(1)}, bf16[224,576]{1,0:T(8,128)(2,1)S(1)}, u32[]{:S(2)}, u32[]{:S(2)}) %collective-permute-start.5) | collective-permute-done | bytes 258080 | tf_op jit(solution)/shard_map/ppermute | solution.py:28
  34.9 2.7 %collective-permute-done.3 = bf16[336,576]{1,0:T(8,128)(2,1)S(1)} collective-permute-done((bf16[336,576]{1,0:T(8,128)(2,1)S(1)}, bf16[336,576]{1,0:T(8,128)(2,1)S(1)}, u32[]{:S(2)}, u32[]{:S(2)}) %collective-permute-start.3) | collective-permute-done | bytes 387104 | tf_op jit(solution)/shard_map/ppermute | solution.py:24
  40.8 3.2 %collective-permute-start.9 = (bf16[224,576]{1,0:T(8,128)(2,1)}, bf16[224,576]{1,0:T(8,128)(2,1)}, u32[]{:S(2)}, u32[]{:S(2)}) collective-permute-start(bf16[224,576]{1,0:T(8,128)(2,1)} %slice.109), channel_id=1, source_target_pairs={{0,3},{1,0},{2,1},{3,2},{4,7},{5,4},{6,5},{7,6},{8,11},{9,8},{10,9... | collective-permute-start | bytes 774152 | tf_op jit(solution)/shard_map/ppermute | solution.py:24
  44.0 8.6 %all-to-all-start = ((bf16[8,56,896]{2,1,0:T(8,128)(2,1)}), bf16[8,56,896]{2,1,0:T(8,128)(2,1)S(1)}, u32[]{:S(2)}, u32[]{:S(2)}) async-start(bf16[8,56,896]{2,1,0:T(8,128)(2,1)} %bitcast.20), calls=%async_computation | async-start | bytes 1605632 | tf_op jit(solution)/shard_map/all_to_all | solution.py:111
  57.6 2.3 %collective-permute-done.10 = bf16[448,896]{1,0:T(8,128)(2,1)S(1)} collective-permute-done((bf16[448,896]{1,0:T(8,128)(2,1)S(1)}, bf16[448,896]{1,0:T(8,128)(2,1)S(1)}, u32[]{:S(2)}, u32[]{:S(2)}) %collective-permute-start.10) | collective-permute-done | bytes 802848 | tf_op jit(solution)/shard_map/ppermute | solution.py:28
  59.9 2.9 %fusion = bf16[448,896]{1,0:T(8,128)(2,1)} fusion(bf16[448,896]{1,0:T(8,128)(2,1)S(1)} %collective-permute-done.10, bf16[448,576]{1,0:T(8,128)(2,1)S(1)} %copy-done, bf16[224,576]{1,0:T(8,128)(2,1)} %collective-permute-done.9, bf16[224,576]{1,0:T(8,128)(2,1)} %collective-permute-done.8, bf16[224,576]{1,0:T(8,128)(2,1)} %slice.109, ...), kind=kOutput, calls=%fused_computation.1 | convolution fusion | flops 467755008 | bytes 3153920 | tf_op jit(solution)/shard_map/dot_general | solution.py:20
  62.8 10.5 %all-to-all-done = bf16[8,56,896]{2,1,0:T(8,128)(2,1)S(1)} async-done(((bf16[8,56,896]{2,1,0:T(8,128)(2,1)}), bf16[8,56,896]{2,1,0:T(8,128)(2,1)S(1)}, u32[]{:S(2)}, u32[]{:S(2)}) %all-to-all-start) | async-done | bytes 802848 | tf_op jit(solution)/shard_map/all_to_all | solution.py:111
  73.3 4.9 %all-to-all-start.1 = ((bf16[8,56,896]{2,1,0:T(8,128)(2,1)}), bf16[8,56,896]{2,1,0:T(8,128)(2,1)S(1)}, u32[]{:S(2)}, u32[]{:S(2)}) async-start(bf16[8,56,896]{2,1,0:T(8,128)(2,1)} %bitcast.21), calls=%async_computation.1 | async-start | bytes 1605632 | tf_op jit(solution)/shard_map/all_to_all | solution.py:111
  78.3 2.8 %collective-permute-start.11 = (bf16[56,896]{1,0:T(8,128)(2,1)S(1)}, bf16[56,896]{1,0:T(8,128)(2,1)S(1)}, u32[]{:S(2)}, u32[]{:S(2)}) collective-permute-start(bf16[56,896]{1,0:T(8,128)(2,1)S(1)} %reduce_sum.24), channel_id=1, source_target_pairs={{0,16},{16,0},{1,17},{17,1},{2,18},{18,2},{3,19},{19,3},{4,20},{20... | collective-permute-start | bytes 301064 | tf_op jit(solution)/shard_map/ppermute | solution.py:28
  81.1 17.7 %all-to-all-done.1 = bf16[8,56,896]{2,1,0:T(8,128)(2,1)S(1)} async-done(((bf16[8,56,896]{2,1,0:T(8,128)(2,1)}), bf16[8,56,896]{2,1,0:T(8,128)(2,1)S(1)}, u32[]{:S(2)}, u32[]{:S(2)}) %all-to-all-start.1) | async-done | bytes 802848 | tf_op jit(solution)/shard_map/all_to_all | solution.py:111
  98.9 3.0 %collective-permute-start.12 = (bf16[56,896]{1,0:T(8,128)(2,1)S(1)}, bf16[56,896]{1,0:T(8,128)(2,1)S(1)}, u32[]{:S(2)}, u32[]{:S(2)}) collective-permute-start(bf16[56,896]{1,0:T(8,128)(2,1)S(1)} %reduce_sum.25), channel_id=1, source_target_pairs={{0,16},{16,0},{1,17},{17,1},{2,18},{18,2},{3,19},{19,3},{4,20},{20... | collective-permute-start | bytes 301064 | tf_op jit(solution)/shard_map/ppermute | solution.py:28
  102.0 3.4 %collective-permute-done.12 = bf16[56,896]{1,0:T(8,128)(2,1)S(1)} collective-permute-done((bf16[56,896]{1,0:T(8,128)(2,1)S(1)}, bf16[56,896]{1,0:T(8,128)(2,1)S(1)}, u32[]{:S(2)}, u32[]{:S(2)}) %collective-permute-start.12) | collective-permute-done | bytes 100384 | tf_op jit(solution)/shard_map/ppermute | solution.py:28
  108.2 4.3 %collective-permute-done.13 = bf16[56,1792]{1,0:T(8,128)(2,1)} collective-permute-done((bf16[56,1792]{1,0:T(8,128)(2,1)}, bf16[56,1792]{1,0:T(8,128)(2,1)}, u32[]{:S(2)}, u32[]{:S(2)}) %collective-permute-start.13) | collective-permute-done | bytes 200736 | tf_op jit(solution)/shard_map/ppermute | solution.py:24
  112.6 2.5 %collective-permute-start.17 = (bf16[56,1792]{1,0:T(8,128)(2,1)}, bf16[56,1792]{1,0:T(8,128)(2,1)S(1)}, u32[]{:S(2)}, u32[]{:S(2)}) collective-permute-start(bf16[56,1792]{1,0:T(8,128)(2,1)} %collective-permute-done.13), channel_id=1, source_target_pairs={{0,64},{32,96},{64,128},{96,160},{128,192},{160,224},{192,0},{224,... | collective-permute-start | bytes 602120 | tf_op jit(solution)/shard_map/ppermute | solution.py:24
  115.0 3.8 %collective-permute-start.15 = (bf16[56,1792]{1,0:T(8,128)(2,1)}, bf16[56,1792]{1,0:T(8,128)(2,1)S(1)}, u32[]{:S(2)}, u32[]{:S(2)}) collective-permute-start(bf16[56,1792]{1,0:T(8,128)(2,1)} %collective-permute-done.13), channel_id=1, source_target_pairs={{0,32},{32,64},{64,96},{96,128},{128,160},{160,192},{192,224},{224... | collective-permute-start | bytes 602120 | tf_op jit(solution)/shard_map/ppermute | solution.py:24
  122.7 4.4 %collective-permute-done.15 = bf16[56,1792]{1,0:T(8,128)(2,1)S(1)} collective-permute-done((bf16[56,1792]{1,0:T(8,128)(2,1)}, bf16[56,1792]{1,0:T(8,128)(2,1)S(1)}, u32[]{:S(2)}, u32[]{:S(2)}) %collective-permute-start.15) | collective-permute-done | bytes 200736 | tf_op jit(solution)/shard_map/ppermute | solution.py:24
  128.7 5.9 %collective-permute-start.20 = (bf16[56,896]{1,0:T(8,128)(2,1)S(1)}, bf16[56,896]{1,0:T(8,128)(2,1)S(1)}, u32[]{:S(2)}, u32[]{:S(2)}) collective-permute-start(bf16[56,896]{1,0:T(8,128)(2,1)S(1)} %slice.133), channel_id=1, source_target_pairs={{0,192},{32,224},{64,0},{96,32},{128,64},{160,96},{192,128},{224,1... | collective-permute-start | bytes 301064 | tf_op jit(solution)/shard_map/ppermute | solution.py:24
  146.1 12.5 %collective-permute-done.24 = bf16[448,576]{1,0:T(8,128)(2,1)S(1)} collective-permute-done((bf16[448,576]{1,0:T(8,128)(2,1)S(1)}, bf16[448,576]{1,0:T(8,128)(2,1)S(1)}, u32[]{:S(2)}, u32[]{:S(2)}) %collective-permute-start.24) | collective-permute-done | bytes 516128 | tf_op jit(solution)/shard_map/ppermute | solution.py:24
  164.4 8.6 %collective-permute-done.26 = bf16[336,576]{1,0:T(8,128)(2,1)S(1)} collective-permute-done((bf16[336,576]{1,0:T(8,128)(2,1)S(1)}, bf16[336,576]{1,0:T(8,128)(2,1)S(1)}, u32[]{:S(2)}, u32[]{:S(2)}) %collective-permute-start.26) | collective-permute-done | bytes 387104 | tf_op jit(solution)/shard_map/ppermute | solution.py:24
  173.0 4.0 %collective-permute-done.25 = bf16[336,576]{1,0:T(8,128)(2,1)S(1)} collective-permute-done((bf16[336,576]{1,0:T(8,128)(2,1)S(1)}, bf16[336,576]{1,0:T(8,128)(2,1)S(1)}, u32[]{:S(2)}, u32[]{:S(2)}) %collective-permute-start.25) | collective-permute-done | bytes 387104 | tf_op jit(solution)/shard_map/ppermute | solution.py:24
  180.8 3.0 %collective-permute-done.28 = bf16[224,576]{1,0:T(8,128)(2,1)S(1)} collective-permute-done((bf16[224,576]{1,0:T(8,128)(2,1)S(1)}, bf16[224,576]{1,0:T(8,128)(2,1)S(1)}, u32[]{:S(2)}, u32[]{:S(2)}) %collective-permute-start.28) | collective-permute-done | bytes 258080 | tf_op jit(solution)/shard_map/ppermute | solution.py:28
  (136 shorter events, 54.8 us)
Async XLA Ops:
  1.2 15.3 %collective-permute-start.2 = (bf16[448,576]{1,0:T(8,128)(2,1)S(1)}, bf16[448,576]{1,0:T(8,128)(2,1)S(1)}, u32[]{:S(2)}, u32[]{:S(2)}) collective-permute-start(bf16[448,576]{1,0:T(8,128)(2,1)S(1)} %pad_maximum_fusion.5), channel_id=1, source_target_pairs={{0,3},{1,0},{2,1},{3,2},{4,7},{5,4},{6,5},{7,6},{8,11},{9,8},{10,9... | collective-permute-start | bytes 1548296 | tf_op jit(solution)/shard_map/ppermute | solution.py:24
  4.3 15.6 %collective-permute-start.1 = (bf16[448,576]{1,0:T(8,128)(2,1)S(1)}, bf16[448,576]{1,0:T(8,128)(2,1)S(1)}, u32[]{:S(2)}, u32[]{:S(2)}) collective-permute-start(bf16[448,576]{1,0:T(8,128)(2,1)S(1)} %pad_maximum_fusion.5), channel_id=1, source_target_pairs={{0,1},{1,2},{2,3},{3,0},{4,5},{5,6},{6,7},{7,4},{8,9},{9,10},{10,1... | collective-permute-start | bytes 1548296 | tf_op jit(solution)/shard_map/ppermute | solution.py:24
  4.3 15.6 %collective-permute-start = (bf16[448,576]{1,0:T(8,128)(2,1)S(1)}, bf16[448,576]{1,0:T(8,128)(2,1)S(1)}, u32[]{:S(2)}, u32[]{:S(2)}) collective-permute-start(bf16[448,576]{1,0:T(8,128)(2,1)S(1)} %pad_maximum_fusion.5), channel_id=1, source_target_pairs={{0,4},{4,0},{1,5},{5,1},{2,6},{6,2},{3,7},{7,3},{8,12},{12,8},{9,1... | collective-permute-start | bytes 1548296 | tf_op jit(solution)/shard_map/ppermute | solution.py:28
  22.6 12.4 %collective-permute-start.4 = (bf16[336,576]{1,0:T(8,128)(2,1)S(1)}, bf16[336,576]{1,0:T(8,128)(2,1)S(1)}, u32[]{:S(2)}, u32[]{:S(2)}) collective-permute-start(bf16[336,576]{1,0:T(8,128)(2,1)S(1)} %get-tuple-element.65), channel_id=1, source_target_pairs={{0,3},{1,0},{2,1},{3,2},{4,7},{5,4},{6,5},{7,6},{8,11},{9,8},{10,9... | collective-permute-start | bytes 1161224 | tf_op jit(solution)/shard_map/ppermute | solution.py:24
  24.4 13.2 %collective-permute-start.3 = (bf16[336,576]{1,0:T(8,128)(2,1)S(1)}, bf16[336,576]{1,0:T(8,128)(2,1)S(1)}, u32[]{:S(2)}, u32[]{:S(2)}) collective-permute-start(bf16[336,576]{1,0:T(8,128)(2,1)S(1)} %get-tuple-element.66), channel_id=1, source_target_pairs={{0,1},{1,2},{2,3},{3,0},{4,5},{5,6},{6,7},{7,4},{8,9},{9,10},{10,1... | collective-permute-start | bytes 1161224 | tf_op jit(solution)/shard_map/ppermute | solution.py:24
  24.7 8.7 %collective-permute-start.5 = (bf16[224,576]{1,0:T(8,128)(2,1)S(1)}, bf16[224,576]{1,0:T(8,128)(2,1)S(1)}, u32[]{:S(2)}, u32[]{:S(2)}) collective-permute-start(bf16[224,576]{1,0:T(8,128)(2,1)S(1)} %get-tuple-element.56), channel_id=1, source_target_pairs={{0,4},{4,0},{1,5},{5,1},{2,6},{6,2},{3,7},{7,3},{8,12},{12,8},{9,1... | collective-permute-start | bytes 774152 | tf_op jit(solution)/shard_map/ppermute | solution.py:28
  38.5 15.1 %collective-permute-start.7 = (bf16[448,576]{1,0:T(8,128)(2,1)}, bf16[448,576]{1,0:T(8,128)(2,1)}, u32[]{:S(2)}, u32[]{:S(2)}) collective-permute-start(bf16[448,576]{1,0:T(8,128)(2,1)} %pad_maximum_fusion.6), channel_id=1, source_target_pairs={{0,4},{4,0},{1,5},{5,1},{2,6},{6,2},{3,7},{7,3},{8,12},{12,8},{9,1... | collective-permute-start | bytes 1548296 | tf_op jit(solution)/shard_map/ppermute | solution.py:28
  40.0 13.5 %collective-permute-start.8 = (bf16[224,576]{1,0:T(8,128)(2,1)S(1)}, bf16[224,576]{1,0:T(8,128)(2,1)}, u32[]{:S(2)}, u32[]{:S(2)}) collective-permute-start(bf16[224,576]{1,0:T(8,128)(2,1)S(1)} %get-tuple-element.55), channel_id=1, source_target_pairs={{0,1},{1,2},{2,3},{3,0},{4,5},{5,6},{6,7},{7,4},{8,9},{9,10},{10,1... | collective-permute-start | bytes 774152 | tf_op jit(solution)/shard_map/ppermute | solution.py:24
  40.8 12.8 %collective-permute-start.9 = (bf16[224,576]{1,0:T(8,128)(2,1)}, bf16[224,576]{1,0:T(8,128)(2,1)}, u32[]{:S(2)}, u32[]{:S(2)}) collective-permute-start(bf16[224,576]{1,0:T(8,128)(2,1)} %slice.109), channel_id=1, source_target_pairs={{0,3},{1,0},{2,1},{3,2},{4,7},{5,4},{6,5},{7,6},{8,11},{9,8},{10,9... | collective-permute-start | bytes 774152 | tf_op jit(solution)/shard_map/ppermute | solution.py:24
  44.0 29.3 %all-to-all-start = ((bf16[8,56,896]{2,1,0:T(8,128)(2,1)}), bf16[8,56,896]{2,1,0:T(8,128)(2,1)S(1)}, u32[]{:S(2)}, u32[]{:S(2)}) async-start(bf16[8,56,896]{2,1,0:T(8,128)(2,1)} %bitcast.20), calls=%async_computation | async-start | bytes 1605632 | tf_op jit(solution)/shard_map/all_to_all | solution.py:111
  73.3 25.5 %all-to-all-start.1 = ((bf16[8,56,896]{2,1,0:T(8,128)(2,1)}), bf16[8,56,896]{2,1,0:T(8,128)(2,1)S(1)}, u32[]{:S(2)}, u32[]{:S(2)}) async-start(bf16[8,56,896]{2,1,0:T(8,128)(2,1)} %bitcast.21), calls=%async_computation.1 | async-start | bytes 1605632 | tf_op jit(solution)/shard_map/all_to_all | solution.py:111
  78.3 23.6 %collective-permute-start.11 = (bf16[56,896]{1,0:T(8,128)(2,1)S(1)}, bf16[56,896]{1,0:T(8,128)(2,1)S(1)}, u32[]{:S(2)}, u32[]{:S(2)}) collective-permute-start(bf16[56,896]{1,0:T(8,128)(2,1)S(1)} %reduce_sum.24), channel_id=1, source_target_pairs={{0,16},{16,0},{1,17},{17,1},{2,18},{18,2},{3,19},{19,3},{4,20},{20... | collective-permute-start | bytes 301064 | tf_op jit(solution)/shard_map/ppermute | solution.py:28
  106.2 12.7 %collective-permute-start.14 = (bf16[56,1792]{1,0:T(8,128)(2,1)}, bf16[56,1792]{1,0:T(8,128)(2,1)S(1)}, u32[]{:S(2)}, u32[]{:S(2)}) collective-permute-start(bf16[56,1792]{1,0:T(8,128)(2,1)} %get-tuple-element.67), channel_id=1, source_target_pairs={{0,224},{32,0},{64,32},{96,64},{128,96},{160,128},{192,160},{224,1... | collective-permute-start | bytes 602120 | tf_op jit(solution)/shard_map/ppermute | solution.py:24
  112.6 22.1 %collective-permute-start.17 = (bf16[56,1792]{1,0:T(8,128)(2,1)}, bf16[56,1792]{1,0:T(8,128)(2,1)S(1)}, u32[]{:S(2)}, u32[]{:S(2)}) collective-permute-start(bf16[56,1792]{1,0:T(8,128)(2,1)} %collective-permute-done.13), channel_id=1, source_target_pairs={{0,64},{32,96},{64,128},{96,160},{128,192},{160,224},{192,0},{224,... | collective-permute-start | bytes 602120 | tf_op jit(solution)/shard_map/ppermute | solution.py:24
  115.0 12.1 %collective-permute-start.15 = (bf16[56,1792]{1,0:T(8,128)(2,1)}, bf16[56,1792]{1,0:T(8,128)(2,1)S(1)}, u32[]{:S(2)}, u32[]{:S(2)}) collective-permute-start(bf16[56,1792]{1,0:T(8,128)(2,1)} %collective-permute-done.13), channel_id=1, source_target_pairs={{0,32},{32,64},{64,96},{96,128},{128,160},{160,192},{192,224},{224... | collective-permute-start | bytes 602120 | tf_op jit(solution)/shard_map/ppermute | solution.py:24
  118.9 15.9 %collective-permute-start.18 = (bf16[56,1792]{1,0:T(8,128)(2,1)S(1)}, bf16[56,1792]{1,0:T(8,128)(2,1)S(1)}, u32[]{:S(2)}, u32[]{:S(2)}) collective-permute-start(bf16[56,1792]{1,0:T(8,128)(2,1)S(1)} %collective-permute-done.14), channel_id=1, source_target_pairs={{0,192},{32,224},{64,0},{96,32},{128,64},{160,96},{192,128},{224,1... | collective-permute-start | bytes 602120 | tf_op jit(solution)/shard_map/ppermute | solution.py:24
  120.3 8.5 %collective-permute-start.16 = (bf16[56,1792]{1,0:T(8,128)(2,1)S(1)}, bf16[56,1792]{1,0:T(8,128)(2,1)S(1)}, u32[]{:S(2)}, u32[]{:S(2)}) collective-permute-start(bf16[56,1792]{1,0:T(8,128)(2,1)S(1)} %collective-permute-done.14), channel_id=1, source_target_pairs={{0,224},{32,0},{64,32},{96,64},{128,96},{160,128},{192,160},{224,1... | collective-permute-start | bytes 602120 | tf_op jit(solution)/shard_map/ppermute | solution.py:24
  143.5 15.1 %collective-permute-start.24 = (bf16[448,576]{1,0:T(8,128)(2,1)S(1)}, bf16[448,576]{1,0:T(8,128)(2,1)S(1)}, u32[]{:S(2)}, u32[]{:S(2)}) collective-permute-start(bf16[448,576]{1,0:T(8,128)(2,1)S(1)} %pad_maximum_fusion.7), channel_id=1, source_target_pairs={{0,3},{1,0},{2,1},{3,2},{4,7},{5,4},{6,5},{7,6},{8,11},{9,8},{10,9... | collective-permute-start | bytes 1548296 | tf_op jit(solution)/shard_map/ppermute | solution.py:24
  143.6 16.3 %collective-permute-start.23 = (bf16[448,576]{1,0:T(8,128)(2,1)S(1)}, bf16[448,576]{1,0:T(8,128)(2,1)S(1)}, u32[]{:S(2)}, u32[]{:S(2)}) collective-permute-start(bf16[448,576]{1,0:T(8,128)(2,1)S(1)} %pad_maximum_fusion.7), channel_id=1, source_target_pairs={{0,1},{1,2},{2,3},{3,0},{4,5},{5,6},{6,7},{7,4},{8,9},{9,10},{10,1... | collective-permute-start | bytes 1548296 | tf_op jit(solution)/shard_map/ppermute | solution.py:24
  145.6 14.5 %collective-permute-start.22 = (bf16[448,576]{1,0:T(8,128)(2,1)S(1)}, bf16[448,576]{1,0:T(8,128)(2,1)S(1)}, u32[]{:S(2)}, u32[]{:S(2)}) collective-permute-start(bf16[448,576]{1,0:T(8,128)(2,1)S(1)} %pad_maximum_fusion.7), channel_id=1, source_target_pairs={{0,4},{4,0},{1,5},{5,1},{2,6},{6,2},{3,7},{7,3},{8,12},{12,8},{9,1... | collective-permute-start | bytes 1548296 | tf_op jit(solution)/shard_map/ppermute | solution.py:28
  160.9 16.2 %collective-permute-start.27 = (bf16[448,576]{1,0:T(8,128)(2,1)S(1)}, bf16[448,576]{1,0:T(8,128)(2,1)S(1)}, u32[]{:S(2)}, u32[]{:S(2)}) collective-permute-start(bf16[448,576]{1,0:T(8,128)(2,1)S(1)} %pad_maximum_fusion.8), channel_id=1, source_target_pairs={{0,4},{4,0},{1,5},{5,1},{2,6},{6,2},{3,7},{7,3},{8,12},{12,8},{9,1... | collective-permute-start | bytes 1548296 | tf_op jit(solution)/shard_map/ppermute | solution.py:28
  161.8 11.2 %collective-permute-start.26 = (bf16[336,576]{1,0:T(8,128)(2,1)S(1)}, bf16[336,576]{1,0:T(8,128)(2,1)S(1)}, u32[]{:S(2)}, u32[]{:S(2)}) collective-permute-start(bf16[336,576]{1,0:T(8,128)(2,1)S(1)} %get-tuple-element.63), channel_id=1, source_target_pairs={{0,3},{1,0},{2,1},{3,2},{4,7},{5,4},{6,5},{7,6},{8,11},{9,8},{10,9... | collective-permute-start | bytes 1161224 | tf_op jit(solution)/shard_map/ppermute | solution.py:24
  163.0 14.1 %collective-permute-start.25 = (bf16[336,576]{1,0:T(8,128)(2,1)S(1)}, bf16[336,576]{1,0:T(8,128)(2,1)S(1)}, u32[]{:S(2)}, u32[]{:S(2)}) collective-permute-start(bf16[336,576]{1,0:T(8,128)(2,1)S(1)} %get-tuple-element.64), channel_id=1, source_target_pairs={{0,1},{1,2},{2,3},{3,0},{4,5},{5,6},{6,7},{7,4},{8,9},{9,10},{10,1... | collective-permute-start | bytes 1161224 | tf_op jit(solution)/shard_map/ppermute | solution.py:24
  163.9 16.9 %collective-permute-start.29 = (bf16[224,576]{1,0:T(8,128)(2,1)S(1)}, bf16[224,576]{1,0:T(8,128)(2,1)S(1)}, u32[]{:S(2)}, u32[]{:S(2)}) collective-permute-start(bf16[224,576]{1,0:T(8,128)(2,1)S(1)} %get-tuple-element.51), channel_id=1, source_target_pairs={{0,1},{1,2},{2,3},{3,0},{4,5},{5,6},{6,7},{7,4},{8,9},{9,10},{10,1... | collective-permute-start | bytes 774152 | tf_op jit(solution)/shard_map/ppermute | solution.py:24
  (28 other events, 129.8 us)

commit v2 on v1

--- a/solution.py
+++ b/solution.py
@@ -42,22 +42,22 @@
     )
     right = jnp.concatenate([f_x, s_left[:h]], axis=0)
     left = jnp.concatenate([f_x, s_right[h:]], axis=0)
-    across = s_left if early_work is not None else jnp.concatenate([s_left, s_right], axis=0)
-    wave = (shift(right, "y", 4, 1), shift(left, "y", 4, -1), swap(across, "x_lo"))
-    done = early_work(early) if early_work is not None else early
-    (to_right, to_left, across), done = lax.optimization_barrier((wave, done))
-    fx_left, far_low = to_right[:n], to_right[n:]
-    fx_right, far_high = to_left[:n], to_left[n:]
-    far = [far_low, far_high]
+    h_right = shift(right, "y", 4, 1)
+    h_left = shift(left, "y", 4, -1)
     if early_work is not None:
+        wave = (h_right, h_left, swap(s_left, "x_lo"))
+        (h_right, h_left, sx_left), done = lax.optimization_barrier((wave, early_work(early)))
+        far = [h_right[n:], h_left[n:]]
         last = swap(jnp.concatenate([s_right] + far, axis=0), "x_lo")
+        s_late = [sx_left, last[:n]] + far + [last[n:]]
     else:
-        last = swap(jnp.concatenate(far, axis=0), "x_lo")
-    wave = (last, shift(f_left, "y", 4, 1), shift(fx_right, "y", 4, -1))
-    last, f_far, fx_far = lax.optimization_barrier(wave)
-    s_late = [across, far_low, far_high, last]
-    if early_work is not None:
-        s_late = [across, last[:n], far_low, far_high, last[n:]]
+        done = early
+        across = swap(jnp.concatenate([s_left, s_right], axis=0), "x_lo")
+        far = [h_right[n:], h_left[n:]]
+        s_late = [across] + far + [swap(jnp.concatenate(far, axis=0), "x_lo")]
+    fx_left, fx_right = h_right[:n], h_left[:n]
+    f_far = shift(f_left, "y", 4, 1)
+    fx_far = shift(fx_right, "y", 4, -1)
     late = (
         jnp.concatenate([fx_left, fx_right, f_far, fx_far], axis=0),
         jnp.concatenate(s_late, axis=0),

time: 191 us -> 191 us (level)
  starting transfers between devices: 58.1 us -> 62.7 us
  matrix products: 15.8 us -> 13.5 us
    all_to_all x2, waiting for transfers between devices: 28.2 us -> 19 us  [exchange_z(): return lax.all_to_all(pair, 'z', 0, 0)]
    ppermute x11, waiting for transfers between devices: 15.5 us -> 19.8 us  [swap(): return lax.ppermute(v, axis, SWAP)]
    ppermute x20, waiting for transfers between devices: 58.4 us -> 62.7 us  [shift(): return lax.ppermute(v, axis, [(i, (i + by) % size) for i in range(size)])]
    all_to_all x2, starting transfers between devices: 13.5 us -> 16.5 us  [exchange_z(): return lax.all_to_all(pair, 'z', 0, 0)]
    ppermute x11, starting transfers between devices: 12.9 us -> 15.7 us  [swap(): return lax.ppermute(v, axis, SWAP)]
    dot_general x12, matrix products: 15.8 us -> 13.5 us  [dot(): lax.dot_general(a, b, (dims, ((), ())), preferred_element_type=jnp.float32)]
    unnamed x38 -> x50, local copies, waits for them, and re-layouts: 5.15 us -> 4.55 us
  transfers between devices with their start and end apart: 33 -> 33, of which waited for: 22 -> 20; matrix products, arithmetic and copies ran while one was open for 8% -> 6% of each run, Pallas kernels for 0% -> 0%
where the time goes in v2:
time: 191 us; the launch traced here: 189 us
  waiting for transfers between devices  102 us (53%)
  starting transfers between devices  62.7 us (33%)
  matrix products  13.5 us (7%)
  local copies, waits for them, and re-layouts  8.4 us (4%)
  other arithmetic  2.22 us (1%)
    ppermute x20, waiting for transfers between devices, shift(): return lax.ppermute(v, axis, [(i, (i + by) % size) for i in range(size)])  62.7 us
    ppermute x20, starting transfers between devices, shift(): return lax.ppermute(v, axis, [(i, (i + by) % size) for i in range(size)])  30.5 us
    ppermute x11, waiting for transfers between devices, swap(): return lax.ppermute(v, axis, SWAP)  19.8 us
    all_to_all x2, waiting for transfers between devices, exchange_z(): return lax.all_to_all(pair, 'z', 0, 0)  19 us
    all_to_all x2, starting transfers between devices, exchange_z(): return lax.all_to_all(pair, 'z', 0, 0)  16.5 us
    ppermute x11, starting transfers between devices, swap(): return lax.ppermute(v, axis, SWAP)  15.7 us
    dot_general x12, matrix products, dot(): lax.dot_general(a, b, (dims, ((), ())), preferred_element_type=jnp.float32)  13.5 us
    unnamed x50, local copies, waits for them, and re-layouts  4.55 us
  transfers between devices with their start and end apart: 33, of which 20 were waited for; matrix products, arithmetic and copies ran while one was open for 6% of the time, Pallas kernels for 0%

profile of v2, /device:TPU:32, one launch (start us, length us, event | category | flops | bytes accessed | tf_op | source)
XLA Modules:
  0.0 189.0 jit_solution(4167011330747066161)
XLA Ops:
  1.2 3.1 %collective-permute-start.2 = (bf16[448,576]{1,0:T(8,128)(2,1)S(1)}, bf16[448,576]{1,0:T(8,128)(2,1)S(1)}, u32[]{:S(2)}, u32[]{:S(2)}) collective-permute-start(bf16[448,576]{1,0:T(8,128)(2,1)S(1)} %pad_maximum_fusion.3), channel_id=1, source_target_pairs={{0,3},{1,0},{2,1},{3,2},{4,7},{5,4},{6,5},{7,6},{8,11},{9,8},{10,9... | collective-permute-start | bytes 1548296 | tf_op jit(solution)/shard_map/ppermute | solution.py:24
  5.7 10.7 %collective-permute-done.2 = bf16[448,576]{1,0:T(8,128)(2,1)S(1)} collective-permute-done((bf16[448,576]{1,0:T(8,128)(2,1)S(1)}, bf16[448,576]{1,0:T(8,128)(2,1)S(1)}, u32[]{:S(2)}, u32[]{:S(2)}) %collective-permute-start.2) | collective-permute-done | bytes 516128 | tf_op jit(solution)/shard_map/ppermute | solution.py:24
  16.5 3.4 %collective-permute-done.1 = bf16[448,576]{1,0:T(8,128)(2,1)S(1)} collective-permute-done((bf16[448,576]{1,0:T(8,128)(2,1)S(1)}, bf16[448,576]{1,0:T(8,128)(2,1)S(1)}, u32[]{:S(2)}, u32[]{:S(2)}) %collective-permute-start.1) | collective-permute-done | bytes 516128 | tf_op jit(solution)/shard_map/ppermute | solution.py:24
  28.0 5.4 %collective-permute-done.5 = bf16[224,576]{1,0:T(8,128)(2,1)S(1)} collective-permute-done((bf16[224,576]{1,0:T(8,128)(2,1)S(1)}, bf16[224,576]{1,0:T(8,128)(2,1)S(1)}, u32[]{:S(2)}, u32[]{:S(2)}) %collective-permute-start.5) | collective-permute-done | bytes 258080 | tf_op jit(solution)/shard_map/ppermute | solution.py:28
  34.9 2.7 %collective-permute-done.3 = bf16[336,576]{1,0:T(8,128)(2,1)S(1)} collective-permute-done((bf16[336,576]{1,0:T(8,128)(2,1)S(1)}, bf16[336,576]{1,0:T(8,128)(2,1)S(1)}, u32[]{:S(2)}, u32[]{:S(2)}) %collective-permute-start.3) | collective-permute-done | bytes 387104 | tf_op jit(solution)/shard_map/ppermute | solution.py:24
  40.0 8.6 %all-to-all-start = ((bf16[8,56,896]{2,1,0:T(8,128)(2,1)}), bf16[8,56,896]{2,1,0:T(8,128)(2,1)S(1)}, u32[]{:S(2)}, u32[]{:S(2)}) async-start(bf16[8,56,896]{2,1,0:T(8,128)(2,1)} %bitcast.20), calls=%async_computation | async-start | bytes 1605632 | tf_op jit(solution)/shard_map/all_to_all | solution.py:111
  49.6 3.5 %collective-permute-done.9 = bf16[448,576]{1,0:T(8,128)(2,1)} collective-permute-done((bf16[448,576]{1,0:T(8,128)(2,1)}, bf16[448,576]{1,0:T(8,128)(2,1)}, u32[]{:S(2)}, u32[]{:S(2)}) %collective-permute-start.9) | collective-permute-done | bytes 516128 | tf_op jit(solution)/shard_map/ppermute | solution.py:28
  56.3 3.3 %collective-permute-start.8 = (bf16[224,576]{1,0:T(8,128)(2,1)S(1)}, bf16[224,576]{1,0:T(8,128)(2,1)S(1)}, u32[]{:S(2)}, u32[]{:S(2)}) collective-permute-start(bf16[224,576]{1,0:T(8,128)(2,1)S(1)} %slice.109), channel_id=1, source_target_pairs={{0,3},{1,0},{2,1},{3,2},{4,7},{5,4},{6,5},{7,6},{8,11},{9,8},{10,9... | collective-permute-start | bytes 774152 | tf_op jit(solution)/shard_map/ppermute | solution.py:24
  59.7 7.0 %collective-permute-done.7 = bf16[224,576]{1,0:T(8,128)(2,1)S(1)} collective-permute-done((bf16[224,576]{1,0:T(8,128)(2,1)S(1)}, bf16[224,576]{1,0:T(8,128)(2,1)S(1)}, u32[]{:S(2)}, u32[]{:S(2)}) %collective-permute-start.7) | collective-permute-done | bytes 258080 | tf_op jit(solution)/shard_map/ppermute | solution.py:24
  69.9 8.0 %all-to-all-start.1 = ((bf16[8,56,896]{2,1,0:T(8,128)(2,1)}), bf16[8,56,896]{2,1,0:T(8,128)(2,1)S(1)}, u32[]{:S(2)}, u32[]{:S(2)}) async-start(bf16[8,56,896]{2,1,0:T(8,128)(2,1)} %bitcast.21), calls=%async_computation.1 | async-start | bytes 1605632 | tf_op jit(solution)/shard_map/all_to_all | solution.py:111
  78.0 3.3 %collective-permute-start.11 = (bf16[56,896]{1,0:T(8,128)(2,1)S(1)}, bf16[56,896]{1,0:T(8,128)(2,1)S(1)}, u32[]{:S(2)}, u32[]{:S(2)}) collective-permute-start(bf16[56,896]{1,0:T(8,128)(2,1)S(1)} %reduce_sum.24), channel_id=1, source_target_pairs={{0,16},{16,0},{1,17},{17,1},{2,18},{18,2},{3,19},{19,3},{4,20},{20... | collective-permute-start | bytes 301064 | tf_op jit(solution)/shard_map/ppermute | solution.py:28
  81.3 18.4 %all-to-all-done.1 = bf16[8,56,896]{2,1,0:T(8,128)(2,1)S(1)} async-done(((bf16[8,56,896]{2,1,0:T(8,128)(2,1)}), bf16[8,56,896]{2,1,0:T(8,128)(2,1)S(1)}, u32[]{:S(2)}, u32[]{:S(2)}) %all-to-all-start.1) | async-done | bytes 802848 | tf_op jit(solution)/shard_map/all_to_all | solution.py:111
  99.8 3.1 %collective-permute-start.12 = (bf16[56,896]{1,0:T(8,128)(2,1)S(1)}, bf16[56,896]{1,0:T(8,128)(2,1)S(1)}, u32[]{:S(2)}, u32[]{:S(2)}) collective-permute-start(bf16[56,896]{1,0:T(8,128)(2,1)S(1)} %reduce_sum.25), channel_id=1, source_target_pairs={{0,16},{16,0},{1,17},{17,1},{2,18},{18,2},{3,19},{19,3},{4,20},{20... | collective-permute-start | bytes 301064 | tf_op jit(solution)/shard_map/ppermute | solution.py:28
  102.9 3.1 %collective-permute-done.12 = bf16[56,896]{1,0:T(8,128)(2,1)S(1)} collective-permute-done((bf16[56,896]{1,0:T(8,128)(2,1)S(1)}, bf16[56,896]{1,0:T(8,128)(2,1)S(1)}, u32[]{:S(2)}, u32[]{:S(2)}) %collective-permute-start.12) | collective-permute-done | bytes 100384 | tf_op jit(solution)/shard_map/ppermute | solution.py:28
  108.9 4.2 %collective-permute-done.13 = bf16[56,1792]{1,0:T(8,128)(2,1)} collective-permute-done((bf16[56,1792]{1,0:T(8,128)(2,1)}, bf16[56,1792]{1,0:T(8,128)(2,1)}, u32[]{:S(2)}, u32[]{:S(2)}) %collective-permute-start.13) | collective-permute-done | bytes 200736 | tf_op jit(solution)/shard_map/ppermute | solution.py:24
  115.2 3.5 %collective-permute-start.18 = (bf16[56,1792]{1,0:T(8,128)(2,1)S(1)}, bf16[56,1792]{1,0:T(8,128)(2,1)S(1)}, u32[]{:S(2)}, u32[]{:S(2)}) collective-permute-start(bf16[56,1792]{1,0:T(8,128)(2,1)S(1)} %collective-permute-done.14), channel_id=1, source_target_pairs={{0,192},{32,224},{64,0},{96,32},{128,64},{160,96},{192,128},{224,1... | collective-permute-start | bytes 602120 | tf_op jit(solution)/shard_map/ppermute | solution.py:24
  121.2 7.4 %collective-permute-done.15 = bf16[56,1792]{1,0:T(8,128)(2,1)S(1)} collective-permute-done((bf16[56,1792]{1,0:T(8,128)(2,1)}, bf16[56,1792]{1,0:T(8,128)(2,1)S(1)}, u32[]{:S(2)}, u32[]{:S(2)}) %collective-permute-start.15) | collective-permute-done | bytes 200736 | tf_op jit(solution)/shard_map/ppermute | solution.py:24
  128.7 5.7 %collective-permute-start.20 = (bf16[56,896]{1,0:T(8,128)(2,1)S(1)}, bf16[56,896]{1,0:T(8,128)(2,1)S(1)}, u32[]{:S(2)}, u32[]{:S(2)}) collective-permute-start(bf16[56,896]{1,0:T(8,128)(2,1)S(1)} %slice.135), channel_id=1, source_target_pairs={{0,192},{32,224},{64,0},{96,32},{128,64},{160,96},{192,128},{224,1... | collective-permute-start | bytes 301064 | tf_op jit(solution)/shard_map/ppermute | solution.py:24
  143.2 2.7 %collective-permute-start.24 = (bf16[448,576]{1,0:T(8,128)(2,1)S(1)}, bf16[448,576]{1,0:T(8,128)(2,1)S(1)}, u32[]{:S(2)}, u32[]{:S(2)}) collective-permute-start(bf16[448,576]{1,0:T(8,128)(2,1)S(1)} %pad_maximum_fusion.5), channel_id=1, source_target_pairs={{0,3},{1,0},{2,1},{3,2},{4,7},{5,4},{6,5},{7,6},{8,11},{9,8},{10,9... | collective-permute-start | bytes 1548296 | tf_op jit(solution)/shard_map/ppermute | solution.py:24
  147.4 11.0 %collective-permute-done.24 = bf16[448,576]{1,0:T(8,128)(2,1)S(1)} collective-permute-done((bf16[448,576]{1,0:T(8,128)(2,1)S(1)}, bf16[448,576]{1,0:T(8,128)(2,1)S(1)}, u32[]{:S(2)}, u32[]{:S(2)}) %collective-permute-start.24) | collective-permute-done | bytes 516128 | tf_op jit(solution)/shard_map/ppermute | solution.py:24
  158.5 3.4 %collective-permute-done.23 = bf16[448,576]{1,0:T(8,128)(2,1)S(1)} collective-permute-done((bf16[448,576]{1,0:T(8,128)(2,1)S(1)}, bf16[448,576]{1,0:T(8,128)(2,1)S(1)}, u32[]{:S(2)}, u32[]{:S(2)}) %collective-permute-start.23) | collective-permute-done | bytes 516128 | tf_op jit(solution)/shard_map/ppermute | solution.py:24
  162.2 3.2 %collective-permute-start.26 = (bf16[336,576]{1,0:T(8,128)(2,1)S(1)}, bf16[336,576]{1,0:T(8,128)(2,1)S(1)}, u32[]{:S(2)}, u32[]{:S(2)}) collective-permute-start(bf16[336,576]{1,0:T(8,128)(2,1)S(1)} %get-tuple-element.46), channel_id=1, source_target_pairs={{0,3},{1,0},{2,1},{3,2},{4,7},{5,4},{6,5},{7,6},{8,11},{9,8},{10,9... | collective-permute-start | bytes 1161224 | tf_op jit(solution)/shard_map/ppermute | solution.py:24
  167.2 9.1 %collective-permute-done.25 = bf16[336,576]{1,0:T(8,128)(2,1)S(1)} collective-permute-done((bf16[336,576]{1,0:T(8,128)(2,1)S(1)}, bf16[336,576]{1,0:T(8,128)(2,1)S(1)}, u32[]{:S(2)}, u32[]{:S(2)}) %collective-permute-start.25) | collective-permute-done | bytes 387104 | tf_op jit(solution)/shard_map/ppermute | solution.py:24
  181.6 3.5 %collective-permute-done.30 = bf16[224,576]{1,0:T(8,128)(2,1)S(1)} collective-permute-done((bf16[224,576]{1,0:T(8,128)(2,1)S(1)}, bf16[224,576]{1,0:T(8,128)(2,1)S(1)}, u32[]{:S(2)}, u32[]{:S(2)}) %collective-permute-start.30) | collective-permute-done | bytes 258080 | tf_op jit(solution)/shard_map/ppermute | solution.py:28
  (147 shorter events, 51.0 us)
Async XLA Ops:
  1.2 15.3 %collective-permute-start.2 = (bf16[448,576]{1,0:T(8,128)(2,1)S(1)}, bf16[448,576]{1,0:T(8,128)(2,1)S(1)}, u32[]{:S(2)}, u32[]{:S(2)}) collective-permute-start(bf16[448,576]{1,0:T(8,128)(2,1)S(1)} %pad_maximum_fusion.3), channel_id=1, source_target_pairs={{0,3},{1,0},{2,1},{3,2},{4,7},{5,4},{6,5},{7,6},{8,11},{9,8},{10,9... | collective-permute-start | bytes 1548296 | tf_op jit(solution)/shard_map/ppermute | solution.py:24
  4.3 15.6 %collective-permute-start.1 = (bf16[448,576]{1,0:T(8,128)(2,1)S(1)}, bf16[448,576]{1,0:T(8,128)(2,1)S(1)}, u32[]{:S(2)}, u32[]{:S(2)}) collective-permute-start(bf16[448,576]{1,0:T(8,128)(2,1)S(1)} %pad_maximum_fusion.3), channel_id=1, source_target_pairs={{0,1},{1,2},{2,3},{3,0},{4,5},{5,6},{6,7},{7,4},{8,9},{9,10},{10,1... | collective-permute-start | bytes 1548296 | tf_op jit(solution)/shard_map/ppermute | solution.py:24
  4.3 15.6 %collective-permute-start = (bf16[448,576]{1,0:T(8,128)(2,1)S(1)}, bf16[448,576]{1,0:T(8,128)(2,1)S(1)}, u32[]{:S(2)}, u32[]{:S(2)}) collective-permute-start(bf16[448,576]{1,0:T(8,128)(2,1)S(1)} %pad_maximum_fusion.3), channel_id=1, source_target_pairs={{0,4},{4,0},{1,5},{5,1},{2,6},{6,2},{3,7},{7,3},{8,12},{12,8},{9,1... | collective-permute-start | bytes 1548296 | tf_op jit(solution)/shard_map/ppermute | solution.py:28
  22.6 12.4 %collective-permute-start.4 = (bf16[336,576]{1,0:T(8,128)(2,1)S(1)}, bf16[336,576]{1,0:T(8,128)(2,1)S(1)}, u32[]{:S(2)}, u32[]{:S(2)}) collective-permute-start(bf16[336,576]{1,0:T(8,128)(2,1)S(1)} %get-tuple-element.47), channel_id=1, source_target_pairs={{0,3},{1,0},{2,1},{3,2},{4,7},{5,4},{6,5},{7,6},{8,11},{9,8},{10,9... | collective-permute-start | bytes 1161224 | tf_op jit(solution)/shard_map/ppermute | solution.py:24
  24.4 13.2 %collective-permute-start.3 = (bf16[336,576]{1,0:T(8,128)(2,1)S(1)}, bf16[336,576]{1,0:T(8,128)(2,1)S(1)}, u32[]{:S(2)}, u32[]{:S(2)}) collective-permute-start(bf16[336,576]{1,0:T(8,128)(2,1)S(1)} %get-tuple-element.48), channel_id=1, source_target_pairs={{0,1},{1,2},{2,3},{3,0},{4,5},{5,6},{6,7},{7,4},{8,9},{9,10},{10,1... | collective-permute-start | bytes 1161224 | tf_op jit(solution)/shard_map/ppermute | solution.py:24
  38.5 14.6 %collective-permute-start.9 = (bf16[448,576]{1,0:T(8,128)(2,1)}, bf16[448,576]{1,0:T(8,128)(2,1)}, u32[]{:S(2)}, u32[]{:S(2)}) collective-permute-start(bf16[448,576]{1,0:T(8,128)(2,1)} %pad_maximum_fusion.4), channel_id=1, source_target_pairs={{0,4},{4,0},{1,5},{5,1},{2,6},{6,2},{3,7},{7,3},{8,12},{12,8},{9,1... | collective-permute-start | bytes 1548296 | tf_op jit(solution)/shard_map/ppermute | solution.py:28
  40.0 29.9 %all-to-all-start = ((bf16[8,56,896]{2,1,0:T(8,128)(2,1)}), bf16[8,56,896]{2,1,0:T(8,128)(2,1)S(1)}, u32[]{:S(2)}, u32[]{:S(2)}) async-start(bf16[8,56,896]{2,1,0:T(8,128)(2,1)} %bitcast.20), calls=%async_computation | async-start | bytes 1605632 | tf_op jit(solution)/shard_map/all_to_all | solution.py:111
  56.2 10.5 %collective-permute-start.10 = (bf16[448,896]{1,0:T(8,128)(2,1)S(1)}, bf16[448,896]{1,0:T(8,128)(2,1)S(1)}, u32[]{:S(2)}, u32[]{:S(2)}) collective-permute-start(bf16[448,896]{1,0:T(8,128)(2,1)S(1)} %fusion.10), channel_id=1, source_target_pairs={{0,8},{8,0},{1,9},{9,1},{2,10},{10,2},{3,11},{11,3},{4,12},{12,4},... | collective-permute-start | bytes 2408456 | tf_op jit(solution)/shard_map/ppermute | solution.py:28
  56.2 10.5 %collective-permute-start.7 = (bf16[224,576]{1,0:T(8,128)(2,1)S(1)}, bf16[224,576]{1,0:T(8,128)(2,1)S(1)}, u32[]{:S(2)}, u32[]{:S(2)}) collective-permute-start(bf16[224,576]{1,0:T(8,128)(2,1)S(1)} %get-tuple-element.37), channel_id=1, source_target_pairs={{0,1},{1,2},{2,3},{3,0},{4,5},{5,6},{6,7},{7,4},{8,9},{9,10},{10,1... | collective-permute-start | bytes 774152 | tf_op jit(solution)/shard_map/ppermute | solution.py:24
  56.3 10.3 %collective-permute-start.8 = (bf16[224,576]{1,0:T(8,128)(2,1)S(1)}, bf16[224,576]{1,0:T(8,128)(2,1)S(1)}, u32[]{:S(2)}, u32[]{:S(2)}) collective-permute-start(bf16[224,576]{1,0:T(8,128)(2,1)S(1)} %slice.109), channel_id=1, source_target_pairs={{0,3},{1,0},{2,1},{3,2},{4,7},{5,4},{6,5},{7,6},{8,11},{9,8},{10,9... | collective-permute-start | bytes 774152 | tf_op jit(solution)/shard_map/ppermute | solution.py:24
  69.9 29.8 %all-to-all-start.1 = ((bf16[8,56,896]{2,1,0:T(8,128)(2,1)}), bf16[8,56,896]{2,1,0:T(8,128)(2,1)S(1)}, u32[]{:S(2)}, u32[]{:S(2)}) async-start(bf16[8,56,896]{2,1,0:T(8,128)(2,1)} %bitcast.21), calls=%async_computation.1 | async-start | bytes 1605632 | tf_op jit(solution)/shard_map/all_to_all | solution.py:111
  78.0 24.9 %collective-permute-start.11 = (bf16[56,896]{1,0:T(8,128)(2,1)S(1)}, bf16[56,896]{1,0:T(8,128)(2,1)S(1)}, u32[]{:S(2)}, u32[]{:S(2)}) collective-permute-start(bf16[56,896]{1,0:T(8,128)(2,1)S(1)} %reduce_sum.24), channel_id=1, source_target_pairs={{0,16},{16,0},{1,17},{17,1},{2,18},{18,2},{3,19},{19,3},{4,20},{20... | collective-permute-start | bytes 301064 | tf_op jit(solution)/shard_map/ppermute | solution.py:28
  113.1 21.4 %collective-permute-start.17 = (bf16[56,1792]{1,0:T(8,128)(2,1)}, bf16[56,1792]{1,0:T(8,128)(2,1)S(1)}, u32[]{:S(2)}, u32[]{:S(2)}) collective-permute-start(bf16[56,1792]{1,0:T(8,128)(2,1)} %collective-permute-done.13), channel_id=1, source_target_pairs={{0,64},{32,96},{64,128},{96,160},{128,192},{160,224},{192,0},{224,... | collective-permute-start | bytes 602120 | tf_op jit(solution)/shard_map/ppermute | solution.py:24
  113.1 15.4 %collective-permute-start.15 = (bf16[56,1792]{1,0:T(8,128)(2,1)}, bf16[56,1792]{1,0:T(8,128)(2,1)S(1)}, u32[]{:S(2)}, u32[]{:S(2)}) collective-permute-start(bf16[56,1792]{1,0:T(8,128)(2,1)} %collective-permute-done.13), channel_id=1, source_target_pairs={{0,32},{32,64},{64,96},{96,128},{128,160},{160,192},{192,224},{224... | collective-permute-start | bytes 602120 | tf_op jit(solution)/shard_map/ppermute | solution.py:24
  115.2 19.2 %collective-permute-start.18 = (bf16[56,1792]{1,0:T(8,128)(2,1)S(1)}, bf16[56,1792]{1,0:T(8,128)(2,1)S(1)}, u32[]{:S(2)}, u32[]{:S(2)}) collective-permute-start(bf16[56,1792]{1,0:T(8,128)(2,1)S(1)} %collective-permute-done.14), channel_id=1, source_target_pairs={{0,192},{32,224},{64,0},{96,32},{128,64},{160,96},{192,128},{224,1... | collective-permute-start | bytes 602120 | tf_op jit(solution)/shard_map/ppermute | solution.py:24
  118.7 9.9 %collective-permute-start.16 = (bf16[56,1792]{1,0:T(8,128)(2,1)S(1)}, bf16[56,1792]{1,0:T(8,128)(2,1)S(1)}, u32[]{:S(2)}, u32[]{:S(2)}) collective-permute-start(bf16[56,1792]{1,0:T(8,128)(2,1)S(1)} %collective-permute-done.14), channel_id=1, source_target_pairs={{0,224},{32,0},{64,32},{96,64},{128,96},{160,128},{192,160},{224,1... | collective-permute-start | bytes 602120 | tf_op jit(solution)/shard_map/ppermute | solution.py:24
  143.2 15.3 %collective-permute-start.24 = (bf16[448,576]{1,0:T(8,128)(2,1)S(1)}, bf16[448,576]{1,0:T(8,128)(2,1)S(1)}, u32[]{:S(2)}, u32[]{:S(2)}) collective-permute-start(bf16[448,576]{1,0:T(8,128)(2,1)S(1)} %pad_maximum_fusion.5), channel_id=1, source_target_pairs={{0,3},{1,0},{2,1},{3,2},{4,7},{5,4},{6,5},{7,6},{8,11},{9,8},{10,9... | collective-permute-start | bytes 1548296 | tf_op jit(solution)/shard_map/ppermute | solution.py:24
  145.9 16.0 %collective-permute-start.23 = (bf16[448,576]{1,0:T(8,128)(2,1)S(1)}, bf16[448,576]{1,0:T(8,128)(2,1)S(1)}, u32[]{:S(2)}, u32[]{:S(2)}) collective-permute-start(bf16[448,576]{1,0:T(8,128)(2,1)S(1)} %pad_maximum_fusion.5), channel_id=1, source_target_pairs={{0,1},{1,2},{2,3},{3,0},{4,5},{5,6},{6,7},{7,4},{8,9},{9,10},{10,1... | collective-permute-start | bytes 1548296 | tf_op jit(solution)/shard_map/ppermute | solution.py:24
  146.0 16.0 %collective-permute-start.22 = (bf16[448,576]{1,0:T(8,128)(2,1)S(1)}, bf16[448,576]{1,0:T(8,128)(2,1)S(1)}, u32[]{:S(2)}, u32[]{:S(2)}) collective-permute-start(bf16[448,576]{1,0:T(8,128)(2,1)S(1)} %pad_maximum_fusion.5), channel_id=1, source_target_pairs={{0,4},{4,0},{1,5},{5,1},{2,6},{6,2},{3,7},{7,3},{8,12},{12,8},{9,1... | collective-permute-start | bytes 1548296 | tf_op jit(solution)/shard_map/ppermute | solution.py:28
  162.2 14.1 %collective-permute-start.25 = (bf16[336,576]{1,0:T(8,128)(2,1)S(1)}, bf16[336,576]{1,0:T(8,128)(2,1)S(1)}, u32[]{:S(2)}, u32[]{:S(2)}) collective-permute-start(bf16[336,576]{1,0:T(8,128)(2,1)S(1)} %get-tuple-element.45), channel_id=1, source_target_pairs={{0,1},{1,2},{2,3},{3,0},{4,5},{5,6},{6,7},{7,4},{8,9},{9,10},{10,1... | collective-permute-start | bytes 1161224 | tf_op jit(solution)/shard_map/ppermute | solution.py:24
  162.2 14.1 %collective-permute-start.26 = (bf16[336,576]{1,0:T(8,128)(2,1)S(1)}, bf16[336,576]{1,0:T(8,128)(2,1)S(1)}, u32[]{:S(2)}, u32[]{:S(2)}) collective-permute-start(bf16[336,576]{1,0:T(8,128)(2,1)S(1)} %get-tuple-element.46), channel_id=1, source_target_pairs={{0,3},{1,0},{2,1},{3,2},{4,7},{5,4},{6,5},{7,6},{8,11},{9,8},{10,9... | collective-permute-start | bytes 1161224 | tf_op jit(solution)/shard_map/ppermute | solution.py:24
  165.6 16.0 %collective-permute-start.29 = (bf16[448,576]{1,0:T(8,128)(2,1)S(1)}, bf16[448,576]{1,0:T(8,128)(2,1)S(1)}, u32[]{:S(2)}, u32[]{:S(2)}) collective-permute-start(bf16[448,576]{1,0:T(8,128)(2,1)S(1)} %pad_maximum_fusion.6), channel_id=1, source_target_pairs={{0,4},{4,0},{1,5},{5,1},{2,6},{6,2},{3,7},{7,3},{8,12},{12,8},{9,1... | collective-permute-start | bytes 1548296 | tf_op jit(solution)/shard_map/ppermute | solution.py:28
  167.2 18.8 %collective-permute-start.27 = (bf16[224,576]{1,0:T(8,128)(2,1)S(1)}, bf16[224,576]{1,0:T(8,128)(2,1)S(1)}, u32[]{:S(2)}, u32[]{:S(2)}) collective-permute-start(bf16[224,576]{1,0:T(8,128)(2,1)S(1)} %get-tuple-element.33), channel_id=1, source_target_pairs={{0,1},{1,2},{2,3},{3,0},{4,5},{5,6},{6,7},{7,4},{8,9},{9,10},{10,1... | collective-permute-start | bytes 774152 | tf_op jit(solution)/shard_map/ppermute | solution.py:24
  176.4 8.8 %collective-permute-start.30 = (bf16[224,576]{1,0:T(8,128)(2,1)S(1)}, bf16[224,576]{1,0:T(8,128)(2,1)S(1)}, u32[]{:S(2)}, u32[]{:S(2)}) collective-permute-start(bf16[224,576]{1,0:T(8,128)(2,1)S(1)} %pad_maximum_fusion.11), channel_id=1, source_target_pairs={{0,4},{4,0},{1,5},{5,1},{2,6},{6,2},{3,7},{7,3},{8,12},{12,8},{9,1... | collective-permute-start | bytes 774152 | tf_op jit(solution)/shard_map/ppermute | solution.py:28
  (33 other events, 198.0 us)

commit v3 on v0

--- a/solution.py
+++ b/solution.py
@@ -55,8 +55,8 @@
     fx_far = shift(fx_right, "y", 4, -1)
     sx_far = swap(s_far, "x_lo")
     late = (
-        jnp.concatenate([fx_left, fx_right, f_far, fx_far], axis=0),
-        jnp.concatenate([sx_left, sx_right, s_far, sx_far], axis=0),
+        jnp.concatenate([fx_left, f_far, fx_right, fx_far], axis=0),
+        jnp.concatenate([sx_left, s_far, sx_right, sx_far], axis=0),
     )
     return early, late, done
 
@@ -118,17 +118,17 @@
     gram_mine = gather_z(rows, jnp.zeros((8 * rows.shape[0], rows.shape[1]), rows.dtype))
     gram_other = swap(gram_mine, "core")
     n = rows.shape[1] // 2
-    grams = [(gram_mine[:, :n], gram_other[:, :n]), (gram_mine[:, n:], gram_other[:, n:])]
+    grams = [g[:, i : i + n] for i in (0, n) for g in (gram_mine, gram_other)]
 
-    def apply(blocks):
+    def apply(blocks, order):
+        flat = [b for part in blocks for b in part]
         total = 0
-        for gram, block in zip(grams, blocks):
-            for g, b in zip(gram, block):
-                total = total + dot(g, b, ((1,), (0,)))
+        for i in order:
+            total = total + dot(grams[i], flat[i], ((1,), (0,)))
         return total
 
-    applied = apply(parts)
-    twice_applied = apply(gather_tp(*halves(low(applied), core))[:2])
+    applied = apply(parts, (0, 2, 1, 3))
+    twice_applied = apply(gather_tp(*halves(low(applied), core))[:2], (0, 1, 2, 3))
     mixed = (
         quintic_one * x.astype(jnp.float32)
         + quintic_three * applied

time: 187 us -> 186 us (level)
  waiting for transfers between devices: 102 us -> 96.7 us
  matrix products: 14.8 us -> 16.7 us
    ppermute x13, waiting for transfers between devices: 50.2 us -> 44.6 us  [swap(): return lax.ppermute(v, axis, SWAP)]
    dot_general x12, matrix products: 14.8 us -> 16.7 us  [dot(): lax.dot_general(a, b, (dims, ((), ())), preferred_element_type=jnp.float32)]
  transfers between devices with their start and end apart: 35 -> 35, of which waited for: 23 -> 21; matrix products, arithmetic and copies ran while one was open for 6% -> 7% of each run, Pallas kernels for 0% -> 0%
where the time goes in v3:
time: 186 us; the launch traced here: 185 us
  waiting for transfers between devices  96.7 us (52%)
  starting transfers between devices  61 us (33%)
  matrix products  16.7 us (9%)
  local copies, waits for them, and re-layouts  7.92 us (4%)
  other arithmetic  2.14 us (1%)
    ppermute x13, waiting for transfers between devices, swap(): return lax.ppermute(v, axis, SWAP)  44.6 us
    ppermute x20, starting transfers between devices, shift(): return lax.ppermute(v, axis, [(i, (i + by) % size) for i in range(size)])  32.3 us
    ppermute x20, waiting for transfers between devices, shift(): return lax.ppermute(v, axis, [(i, (i + by) % size) for i in range(size)])  29.4 us
    all_to_all x2, waiting for transfers between devices, exchange_z(): return lax.all_to_all(pair, 'z', 0, 0)  22.8 us
    dot_general x12, matrix products, dot(): lax.dot_general(a, b, (dims, ((), ())), preferred_element_type=jnp.float32)  16.7 us
    ppermute x13, starting transfers between devices, swap(): return lax.ppermute(v, axis, SWAP)  15.2 us
    all_to_all x2, starting transfers between devices, exchange_z(): return lax.all_to_all(pair, 'z', 0, 0)  13.5 us
  transfers between devices with their start and end apart: 35, of which 21 were waited for; matrix products, arithmetic and copies ran while one was open for 7% of the time, Pallas kernels for 0%

profile of v3, /device:TPU:32, one launch (start us, length us, event | category | flops | bytes accessed | tf_op | source)
XLA Modules:
  0.0 185.1 jit_solution(4080361708782521067)
XLA Ops:
  6.0 10.0 %collective-permute-done = bf16[448,576]{1,0:T(8,128)(2,1)S(1)} collective-permute-done((bf16[448,576]{1,0:T(8,128)(2,1)S(1)}, bf16[448,576]{1,0:T(8,128)(2,1)S(1)}, u32[]{:S(2)}, u32[]{:S(2)}) %collective-permute-start) | collective-permute-done | bytes 516128 | tf_op jit(solution)/shard_map/ppermute | solution.py:28
  16.0 2.5 %collective-permute-done.1 = bf16[448,576]{1,0:T(8,128)(2,1)S(1)} collective-permute-done((bf16[448,576]{1,0:T(8,128)(2,1)S(1)}, bf16[448,576]{1,0:T(8,128)(2,1)S(1)}, u32[]{:S(2)}, u32[]{:S(2)}) %collective-permute-start.1) | collective-permute-done | bytes 516128 | tf_op jit(solution)/shard_map/ppermute | solution.py:24
  29.1 5.9 %collective-permute-done.5 = bf16[224,576]{1,0:T(8,128)(2,1)S(1)} collective-permute-done((bf16[224,576]{1,0:T(8,128)(2,1)S(1)}, bf16[224,576]{1,0:T(8,128)(2,1)S(1)}, u32[]{:S(2)}, u32[]{:S(2)}) %collective-permute-start.5) | collective-permute-done | bytes 258080 | tf_op jit(solution)/shard_map/ppermute | solution.py:28
  37.4 8.6 %all-to-all-start = ((bf16[8,56,896]{2,1,0:T(8,128)(2,1)}), bf16[8,56,896]{2,1,0:T(8,128)(2,1)S(1)}, u32[]{:S(2)}, u32[]{:S(2)}) async-start(bf16[8,56,896]{2,1,0:T(8,128)(2,1)} %bitcast.2), calls=%async_computation | async-start | bytes 1605632 | tf_op jit(solution)/shard_map/all_to_all | solution.py:107
  54.2 7.0 %collective-permute-done.7 = bf16[224,576]{1,0:T(8,128)(2,1)S(1)} collective-permute-done((bf16[224,576]{1,0:T(8,128)(2,1)S(1)}, bf16[224,576]{1,0:T(8,128)(2,1)S(1)}, u32[]{:S(2)}, u32[]{:S(2)}) %collective-permute-start.7) | collective-permute-done | bytes 258080 | tf_op jit(solution)/shard_map/ppermute | solution.py:24
  63.8 3.7 %all-to-all-done = bf16[8,56,896]{2,1,0:T(8,128)(2,1)S(1)} async-done(((bf16[8,56,896]{2,1,0:T(8,128)(2,1)}), bf16[8,56,896]{2,1,0:T(8,128)(2,1)S(1)}, u32[]{:S(2)}, u32[]{:S(2)}) %all-to-all-start) | async-done | bytes 802848 | tf_op jit(solution)/shard_map/all_to_all | solution.py:107
  67.5 4.9 %all-to-all-start.1 = ((bf16[8,56,896]{2,1,0:T(8,128)(2,1)}), bf16[8,56,896]{2,1,0:T(8,128)(2,1)S(1)}, u32[]{:S(2)}, u32[]{:S(2)}) async-start(bf16[8,56,896]{2,1,0:T(8,128)(2,1)} %bitcast.21), calls=%async_computation.1 | async-start | bytes 1605632 | tf_op jit(solution)/shard_map/all_to_all | solution.py:107
  72.5 3.3 %collective-permute-start.12 = (bf16[56,896]{1,0:T(8,128)(2,1)S(1)}, bf16[56,896]{1,0:T(8,128)(2,1)S(1)}, u32[]{:S(2)}, u32[]{:S(2)}) collective-permute-start(bf16[56,896]{1,0:T(8,128)(2,1)S(1)} %reduce_sum.24), channel_id=1, source_target_pairs={{0,16},{16,0},{1,17},{17,1},{2,18},{18,2},{3,19},{19,3},{4,20},{20... | collective-permute-start | bytes 301064 | tf_op jit(solution)/shard_map/ppermute | solution.py:28
  75.8 19.1 %all-to-all-done.1 = bf16[8,56,896]{2,1,0:T(8,128)(2,1)S(1)} async-done(((bf16[8,56,896]{2,1,0:T(8,128)(2,1)}), bf16[8,56,896]{2,1,0:T(8,128)(2,1)S(1)}, u32[]{:S(2)}, u32[]{:S(2)}) %all-to-all-start.1) | async-done | bytes 802848 | tf_op jit(solution)/shard_map/all_to_all | solution.py:107
  95.0 3.1 %collective-permute-start.13 = (bf16[56,896]{1,0:T(8,128)(2,1)S(1)}, bf16[56,896]{1,0:T(8,128)(2,1)S(1)}, u32[]{:S(2)}, u32[]{:S(2)}) collective-permute-start(bf16[56,896]{1,0:T(8,128)(2,1)S(1)} %reduce_sum.25), channel_id=1, source_target_pairs={{0,16},{16,0},{1,17},{17,1},{2,18},{18,2},{3,19},{19,3},{4,20},{20... | collective-permute-start | bytes 301064 | tf_op jit(solution)/shard_map/ppermute | solution.py:28
  98.2 3.1 %collective-permute-done.13 = bf16[56,896]{1,0:T(8,128)(2,1)S(1)} collective-permute-done((bf16[56,896]{1,0:T(8,128)(2,1)S(1)}, bf16[56,896]{1,0:T(8,128)(2,1)S(1)}, u32[]{:S(2)}, u32[]{:S(2)}) %collective-permute-start.13) | collective-permute-done | bytes 100384 | tf_op jit(solution)/shard_map/ppermute | solution.py:28
  104.2 4.2 %collective-permute-done.14 = bf16[56,1792]{1,0:T(8,128)(2,1)} collective-permute-done((bf16[56,1792]{1,0:T(8,128)(2,1)}, bf16[56,1792]{1,0:T(8,128)(2,1)}, u32[]{:S(2)}, u32[]{:S(2)}) %collective-permute-start.14) | collective-permute-done | bytes 200736 | tf_op jit(solution)/shard_map/ppermute | solution.py:24
  108.6 2.8 %collective-permute-start.18 = (bf16[56,1792]{1,0:T(8,128)(2,1)}, bf16[56,1792]{1,0:T(8,128)(2,1)S(1)}, u32[]{:S(2)}, u32[]{:S(2)}) collective-permute-start(bf16[56,1792]{1,0:T(8,128)(2,1)} %collective-permute-done.14), channel_id=1, source_target_pairs={{0,64},{32,96},{64,128},{96,160},{128,192},{160,224},{192,0},{224,... | collective-permute-start | bytes 602120 | tf_op jit(solution)/shard_map/ppermute | solution.py:24
  111.5 4.0 %collective-permute-start.19 = (bf16[56,1792]{1,0:T(8,128)(2,1)S(1)}, bf16[56,1792]{1,0:T(8,128)(2,1)S(1)}, u32[]{:S(2)}, u32[]{:S(2)}) collective-permute-start(bf16[56,1792]{1,0:T(8,128)(2,1)S(1)} %collective-permute-done.15), channel_id=1, source_target_pairs={{0,192},{32,224},{64,0},{96,32},{128,64},{160,96},{192,128},{224,1... | collective-permute-start | bytes 602120 | tf_op jit(solution)/shard_map/ppermute | solution.py:24
  116.5 5.0 %collective-permute-done.17 = bf16[56,1792]{1,0:T(8,128)(2,1)S(1)} collective-permute-done((bf16[56,1792]{1,0:T(8,128)(2,1)S(1)}, bf16[56,1792]{1,0:T(8,128)(2,1)S(1)}, u32[]{:S(2)}, u32[]{:S(2)}) %collective-permute-start.17) | collective-permute-done | bytes 200736 | tf_op jit(solution)/shard_map/ppermute | solution.py:24
  121.5 4.8 %collective-permute-start.21 = (bf16[56,896]{1,0:T(8,128)(2,1)S(1)}, bf16[56,896]{1,0:T(8,128)(2,1)S(1)}, u32[]{:S(2)}, u32[]{:S(2)}) collective-permute-start(bf16[56,896]{1,0:T(8,128)(2,1)S(1)} %slice.125), channel_id=1, source_target_pairs={{0,192},{32,224},{64,0},{96,32},{128,64},{160,96},{192,128},{224,1... | collective-permute-start | bytes 301064 | tf_op jit(solution)/shard_map/ppermute | solution.py:24
  128.6 4.6 %collective-permute-done.20 = bf16[56,896]{1,0:T(8,128)(2,1)S(1)} collective-permute-done((bf16[56,896]{1,0:T(8,128)(2,1)S(1)}, bf16[56,896]{1,0:T(8,128)(2,1)S(1)}, u32[]{:S(2)}, u32[]{:S(2)}) %collective-permute-start.20) | collective-permute-done | bytes 100384 | tf_op jit(solution)/shard_map/ppermute | solution.py:24
  134.3 2.5 %collective-permute-done.22 = bf16[448,1792]{1,0:T(8,128)(2,1)S(1)} collective-permute-done((bf16[448,1792]{1,0:T(8,128)(2,1)S(1)}, bf16[448,1792]{1,0:T(8,128)(2,1)S(1)}, u32[]{:S(2)}, u32[]{:S(2)}) %collective-permute-start.22) | collective-permute-done | bytes 1605664 | tf_op jit(solution)/shard_map/ppermute | solution.py:28
  143.3 2.2 %collective-permute-start.25 = (bf16[448,576]{1,0:T(8,128)(2,1)S(1)}, bf16[448,576]{1,0:T(8,128)(2,1)S(1)}, u32[]{:S(2)}, u32[]{:S(2)}) collective-permute-start(bf16[448,576]{1,0:T(8,128)(2,1)S(1)} %pad_maximum_fusion.6), channel_id=1, source_target_pairs={{0,3},{1,0},{2,1},{3,2},{4,7},{5,4},{6,5},{7,6},{8,11},{9,8},{10,9... | collective-permute-start | bytes 1548296 | tf_op jit(solution)/shard_map/ppermute | solution.py:24
  145.5 10.3 %collective-permute-done.23 = bf16[448,576]{1,0:T(8,128)(2,1)S(1)} collective-permute-done((bf16[448,576]{1,0:T(8,128)(2,1)S(1)}, bf16[448,576]{1,0:T(8,128)(2,1)S(1)}, u32[]{:S(2)}, u32[]{:S(2)}) %collective-permute-start.23) | collective-permute-done | bytes 516128 | tf_op jit(solution)/shard_map/ppermute | solution.py:28
  155.7 2.4 %collective-permute-done.24 = bf16[448,576]{1,0:T(8,128)(2,1)S(1)} collective-permute-done((bf16[448,576]{1,0:T(8,128)(2,1)S(1)}, bf16[448,576]{1,0:T(8,128)(2,1)S(1)}, u32[]{:S(2)}, u32[]{:S(2)}) %collective-permute-start.24) | collective-permute-done | bytes 516128 | tf_op jit(solution)/shard_map/ppermute | solution.py:24
  159.5 2.2 %collective-permute-start.27 = (bf16[336,576]{1,0:T(8,128)(2,1)S(1)}, bf16[336,576]{1,0:T(8,128)(2,1)S(1)}, u32[]{:S(2)}, u32[]{:S(2)}) collective-permute-start(bf16[336,576]{1,0:T(8,128)(2,1)S(1)} %get-tuple-element.59), channel_id=1, source_target_pairs={{0,3},{1,0},{2,1},{3,2},{4,7},{5,4},{6,5},{7,6},{8,11},{9,8},{10,9... | collective-permute-start | bytes 1161224 | tf_op jit(solution)/shard_map/ppermute | solution.py:24
  164.0 7.6 %collective-permute-done.28 = bf16[224,576]{1,0:T(8,128)(2,1)S(1)} collective-permute-done((bf16[224,576]{1,0:T(8,128)(2,1)S(1)}, bf16[224,576]{1,0:T(8,128)(2,1)S(1)}, u32[]{:S(2)}, u32[]{:S(2)}) %collective-permute-start.28) | collective-permute-done | bytes 258080 | tf_op jit(solution)/shard_map/ppermute | solution.py:28
  177.8 3.5 %collective-permute-done.32 = bf16[224,576]{1,0:T(8,128)(2,1)S(1)} collective-permute-done((bf16[224,576]{1,0:T(8,128)(2,1)S(1)}, bf16[224,576]{1,0:T(8,128)(2,1)S(1)}, u32[]{:S(2)}, u32[]{:S(2)}) %collective-permute-start.32) | collective-permute-done | bytes 258080 | tf_op jit(solution)/shard_map/ppermute | solution.py:28
  (146 shorter events, 57.2 us)
Async XLA Ops:
  1.2 14.8 %collective-permute-start = (bf16[448,576]{1,0:T(8,128)(2,1)S(1)}, bf16[448,576]{1,0:T(8,128)(2,1)S(1)}, u32[]{:S(2)}, u32[]{:S(2)}) collective-permute-start(bf16[448,576]{1,0:T(8,128)(2,1)S(1)} %pad_maximum_fusion.5), channel_id=1, source_target_pairs={{0,4},{4,0},{1,5},{5,1},{2,6},{6,2},{3,7},{7,3},{8,12},{12,8},{9,1... | collective-permute-start | bytes 1548296 | tf_op jit(solution)/shard_map/ppermute | solution.py:28
  2.7 15.7 %collective-permute-start.1 = (bf16[448,576]{1,0:T(8,128)(2,1)S(1)}, bf16[448,576]{1,0:T(8,128)(2,1)S(1)}, u32[]{:S(2)}, u32[]{:S(2)}) collective-permute-start(bf16[448,576]{1,0:T(8,128)(2,1)S(1)} %pad_maximum_fusion.5), channel_id=1, source_target_pairs={{0,1},{1,2},{2,3},{3,0},{4,5},{5,6},{6,7},{7,4},{8,9},{9,10},{10,1... | collective-permute-start | bytes 1548296 | tf_op jit(solution)/shard_map/ppermute | solution.py:24
  4.3 14.2 %collective-permute-start.2 = (bf16[448,576]{1,0:T(8,128)(2,1)S(1)}, bf16[448,576]{1,0:T(8,128)(2,1)S(1)}, u32[]{:S(2)}, u32[]{:S(2)}) collective-permute-start(bf16[448,576]{1,0:T(8,128)(2,1)S(1)} %pad_maximum_fusion.5), channel_id=1, source_target_pairs={{0,3},{1,0},{2,1},{3,2},{4,7},{5,4},{6,5},{7,6},{8,11},{9,8},{10,9... | collective-permute-start | bytes 1548296 | tf_op jit(solution)/shard_map/ppermute | solution.py:24
  22.0 13.6 %collective-permute-start.3 = (bf16[336,576]{1,0:T(8,128)(2,1)S(1)}, bf16[336,576]{1,0:T(8,128)(2,1)S(1)}, u32[]{:S(2)}, u32[]{:S(2)}) collective-permute-start(bf16[336,576]{1,0:T(8,128)(2,1)S(1)} %get-tuple-element.62), channel_id=1, source_target_pairs={{0,1},{1,2},{2,3},{3,0},{4,5},{5,6},{6,7},{7,4},{8,9},{9,10},{10,1... | collective-permute-start | bytes 1161224 | tf_op jit(solution)/shard_map/ppermute | solution.py:24
  23.6 12.0 %collective-permute-start.4 = (bf16[336,576]{1,0:T(8,128)(2,1)S(1)}, bf16[336,576]{1,0:T(8,128)(2,1)S(1)}, u32[]{:S(2)}, u32[]{:S(2)}) collective-permute-start(bf16[336,576]{1,0:T(8,128)(2,1)S(1)} %get-tuple-element.61), channel_id=1, source_target_pairs={{0,3},{1,0},{2,1},{3,2},{4,7},{5,4},{6,5},{7,6},{8,11},{9,8},{10,9... | collective-permute-start | bytes 1161224 | tf_op jit(solution)/shard_map/ppermute | solution.py:24
  25.8 20.2 %collective-permute-start.9 = (bf16[224,576]{1,0:T(8,128)(2,1)}, bf16[224,576]{1,0:T(8,128)(2,1)S(1)}, u32[]{:S(2)}, u32[]{:S(2)}) collective-permute-start(bf16[224,576]{1,0:T(8,128)(2,1)} %get-tuple-element.46), channel_id=1, source_target_pairs={{0,4},{4,0},{1,5},{5,1},{2,6},{6,2},{3,7},{7,3},{8,12},{12,8},{9,1... | collective-permute-start | bytes 774152 | tf_op jit(solution)/shard_map/ppermute | solution.py:28
  36.9 9.9 %collective-permute-start.10 = (bf16[224,576]{1,0:T(8,128)(2,1)}, bf16[224,576]{1,0:T(8,128)(2,1)}, u32[]{:S(2)}, u32[]{:S(2)}) collective-permute-start(bf16[224,576]{1,0:T(8,128)(2,1)} %pad_maximum_fusion.11), channel_id=1, source_target_pairs={{0,4},{4,0},{1,5},{5,1},{2,6},{6,2},{3,7},{7,3},{8,12},{12,8},{9,1... | collective-permute-start | bytes 774152 | tf_op jit(solution)/shard_map/ppermute | solution.py:28
  37.4 30.1 %all-to-all-start = ((bf16[8,56,896]{2,1,0:T(8,128)(2,1)}), bf16[8,56,896]{2,1,0:T(8,128)(2,1)S(1)}, u32[]{:S(2)}, u32[]{:S(2)}) async-start(bf16[8,56,896]{2,1,0:T(8,128)(2,1)} %bitcast.2), calls=%async_computation | async-start | bytes 1605632 | tf_op jit(solution)/shard_map/all_to_all | solution.py:107
  50.6 10.6 %collective-permute-start.11 = (bf16[448,896]{1,0:T(8,128)(2,1)S(1)}, bf16[448,896]{1,0:T(8,128)(2,1)S(1)}, u32[]{:S(2)}, u32[]{:S(2)}) collective-permute-start(bf16[448,896]{1,0:T(8,128)(2,1)S(1)} %fusion.10), channel_id=1, source_target_pairs={{0,8},{8,0},{1,9},{9,1},{2,10},{10,2},{3,11},{11,3},{4,12},{12,4},... | collective-permute-start | bytes 2408456 | tf_op jit(solution)/shard_map/ppermute | solution.py:28
  50.7 10.5 %collective-permute-start.7 = (bf16[224,576]{1,0:T(8,128)(2,1)S(1)}, bf16[224,576]{1,0:T(8,128)(2,1)S(1)}, u32[]{:S(2)}, u32[]{:S(2)}) collective-permute-start(bf16[224,576]{1,0:T(8,128)(2,1)S(1)} %get-tuple-element.43), channel_id=1, source_target_pairs={{0,1},{1,2},{2,3},{3,0},{4,5},{5,6},{6,7},{7,4},{8,9},{9,10},{10,1... | collective-permute-start | bytes 774152 | tf_op jit(solution)/shard_map/ppermute | solution.py:24
  67.5 27.4 %all-to-all-start.1 = ((bf16[8,56,896]{2,1,0:T(8,128)(2,1)}), bf16[8,56,896]{2,1,0:T(8,128)(2,1)S(1)}, u32[]{:S(2)}, u32[]{:S(2)}) async-start(bf16[8,56,896]{2,1,0:T(8,128)(2,1)} %bitcast.21), calls=%async_computation.1 | async-start | bytes 1605632 | tf_op jit(solution)/shard_map/all_to_all | solution.py:107
  72.5 25.6 %collective-permute-start.12 = (bf16[56,896]{1,0:T(8,128)(2,1)S(1)}, bf16[56,896]{1,0:T(8,128)(2,1)S(1)}, u32[]{:S(2)}, u32[]{:S(2)}) collective-permute-start(bf16[56,896]{1,0:T(8,128)(2,1)S(1)} %reduce_sum.24), channel_id=1, source_target_pairs={{0,16},{16,0},{1,17},{17,1},{2,18},{18,2},{3,19},{19,3},{4,20},{20... | collective-permute-start | bytes 301064 | tf_op jit(solution)/shard_map/ppermute | solution.py:28
  108.4 18.0 %collective-permute-start.16 = (bf16[56,1792]{1,0:T(8,128)(2,1)}, bf16[56,1792]{1,0:T(8,128)(2,1)S(1)}, u32[]{:S(2)}, u32[]{:S(2)}) collective-permute-start(bf16[56,1792]{1,0:T(8,128)(2,1)} %collective-permute-done.14), channel_id=1, source_target_pairs={{0,32},{32,64},{64,96},{96,128},{128,160},{160,192},{192,224},{224... | collective-permute-start | bytes 602120 | tf_op jit(solution)/shard_map/ppermute | solution.py:24
  108.6 19.5 %collective-permute-start.18 = (bf16[56,1792]{1,0:T(8,128)(2,1)}, bf16[56,1792]{1,0:T(8,128)(2,1)S(1)}, u32[]{:S(2)}, u32[]{:S(2)}) collective-permute-start(bf16[56,1792]{1,0:T(8,128)(2,1)} %collective-permute-done.14), channel_id=1, source_target_pairs={{0,64},{32,96},{64,128},{96,160},{128,192},{160,224},{192,0},{224,... | collective-permute-start | bytes 602120 | tf_op jit(solution)/shard_map/ppermute | solution.py:24
  111.5 10.0 %collective-permute-start.17 = (bf16[56,1792]{1,0:T(8,128)(2,1)S(1)}, bf16[56,1792]{1,0:T(8,128)(2,1)S(1)}, u32[]{:S(2)}, u32[]{:S(2)}) collective-permute-start(bf16[56,1792]{1,0:T(8,128)(2,1)S(1)} %collective-permute-done.15), channel_id=1, source_target_pairs={{0,224},{32,0},{64,32},{96,64},{128,96},{160,128},{192,160},{224,1... | collective-permute-start | bytes 602120 | tf_op jit(solution)/shard_map/ppermute | solution.py:24
  111.5 16.7 %collective-permute-start.19 = (bf16[56,1792]{1,0:T(8,128)(2,1)S(1)}, bf16[56,1792]{1,0:T(8,128)(2,1)S(1)}, u32[]{:S(2)}, u32[]{:S(2)}) collective-permute-start(bf16[56,1792]{1,0:T(8,128)(2,1)S(1)} %collective-permute-done.15), channel_id=1, source_target_pairs={{0,192},{32,224},{64,0},{96,32},{128,64},{160,96},{192,128},{224,1... | collective-permute-start | bytes 602120 | tf_op jit(solution)/shard_map/ppermute | solution.py:24
  140.6 15.1 %collective-permute-start.23 = (bf16[448,576]{1,0:T(8,128)(2,1)S(1)}, bf16[448,576]{1,0:T(8,128)(2,1)S(1)}, u32[]{:S(2)}, u32[]{:S(2)}) collective-permute-start(bf16[448,576]{1,0:T(8,128)(2,1)S(1)} %pad_maximum_fusion.6), channel_id=1, source_target_pairs={{0,4},{4,0},{1,5},{5,1},{2,6},{6,2},{3,7},{7,3},{8,12},{12,8},{9,1... | collective-permute-start | bytes 1548296 | tf_op jit(solution)/shard_map/ppermute | solution.py:28
  142.2 16.0 %collective-permute-start.24 = (bf16[448,576]{1,0:T(8,128)(2,1)S(1)}, bf16[448,576]{1,0:T(8,128)(2,1)S(1)}, u32[]{:S(2)}, u32[]{:S(2)}) collective-permute-start(bf16[448,576]{1,0:T(8,128)(2,1)S(1)} %pad_maximum_fusion.6), channel_id=1, source_target_pairs={{0,1},{1,2},{2,3},{3,0},{4,5},{5,6},{6,7},{7,4},{8,9},{9,10},{10,1... | collective-permute-start | bytes 1548296 | tf_op jit(solution)/shard_map/ppermute | solution.py:24
  143.3 14.9 %collective-permute-start.25 = (bf16[448,576]{1,0:T(8,128)(2,1)S(1)}, bf16[448,576]{1,0:T(8,128)(2,1)S(1)}, u32[]{:S(2)}, u32[]{:S(2)}) collective-permute-start(bf16[448,576]{1,0:T(8,128)(2,1)S(1)} %pad_maximum_fusion.6), channel_id=1, source_target_pairs={{0,3},{1,0},{2,1},{3,2},{4,7},{5,4},{6,5},{7,6},{8,11},{9,8},{10,9... | collective-permute-start | bytes 1548296 | tf_op jit(solution)/shard_map/ppermute | solution.py:24
  158.4 14.1 %collective-permute-start.26 = (bf16[336,576]{1,0:T(8,128)(2,1)S(1)}, bf16[336,576]{1,0:T(8,128)(2,1)S(1)}, u32[]{:S(2)}, u32[]{:S(2)}) collective-permute-start(bf16[336,576]{1,0:T(8,128)(2,1)S(1)} %get-tuple-element.60), channel_id=1, source_target_pairs={{0,1},{1,2},{2,3},{3,0},{4,5},{5,6},{6,7},{7,4},{8,9},{9,10},{10,1... | collective-permute-start | bytes 1161224 | tf_op jit(solution)/shard_map/ppermute | solution.py:24
  159.5 13.0 %collective-permute-start.27 = (bf16[336,576]{1,0:T(8,128)(2,1)S(1)}, bf16[336,576]{1,0:T(8,128)(2,1)S(1)}, u32[]{:S(2)}, u32[]{:S(2)}) collective-permute-start(bf16[336,576]{1,0:T(8,128)(2,1)S(1)} %get-tuple-element.59), channel_id=1, source_target_pairs={{0,3},{1,0},{2,1},{3,2},{4,7},{5,4},{6,5},{7,6},{8,11},{9,8},{10,9... | collective-permute-start | bytes 1161224 | tf_op jit(solution)/shard_map/ppermute | solution.py:24
  161.7 9.9 %collective-permute-start.28 = (bf16[224,576]{1,0:T(8,128)(2,1)S(1)}, bf16[224,576]{1,0:T(8,128)(2,1)S(1)}, u32[]{:S(2)}, u32[]{:S(2)}) collective-permute-start(bf16[224,576]{1,0:T(8,128)(2,1)S(1)} %get-tuple-element.40), channel_id=1, source_target_pairs={{0,4},{4,0},{1,5},{5,1},{2,6},{6,2},{3,7},{7,3},{8,12},{12,8},{9,1... | collective-permute-start | bytes 774152 | tf_op jit(solution)/shard_map/ppermute | solution.py:28
  162.4 15.3 %collective-permute-start.31 = (bf16[224,576]{1,0:T(8,128)(2,1)S(1)}, bf16[224,576]{1,0:T(8,128)(2,1)S(1)}, u32[]{:S(2)}, u32[]{:S(2)}) collective-permute-start(bf16[224,576]{1,0:T(8,128)(2,1)S(1)} %get-tuple-element.36), channel_id=1, source_target_pairs={{0,4},{4,0},{1,5},{5,1},{2,6},{6,2},{3,7},{7,3},{8,12},{12,8},{9,1... | collective-permute-start | bytes 774152 | tf_op jit(solution)/shard_map/ppermute | solution.py:28
  164.0 18.2 %collective-permute-start.29 = (bf16[224,576]{1,0:T(8,128)(2,1)S(1)}, bf16[224,576]{1,0:T(8,128)(2,1)S(1)}, u32[]{:S(2)}, u32[]{:S(2)}) collective-permute-start(bf16[224,576]{1,0:T(8,128)(2,1)S(1)} %get-tuple-element.39), channel_id=1, source_target_pairs={{0,1},{1,2},{2,3},{3,0},{4,5},{5,6},{6,7},{7,4},{8,9},{9,10},{10,1... | collective-permute-start | bytes 774152 | tf_op jit(solution)/shard_map/ppermute | solution.py:24
  (32 other events, 185.8 us)

commit v4 on v3

--- a/solution.py
+++ b/solution.py
@@ -28,14 +28,17 @@
     return lax.ppermute(v, axis, SWAP)
 
 
-def gather_tp(first, second, early_work=None):
-    n = first.shape[0]
+def rows_of(v, start, size):
+    return lax.dynamic_slice_in_dim(v, start, size, 0)
+
+
+def gather_tp(v, core, early_work=None):
+    n = v.shape[0] // 2
     h = n // 2
-    whole = jnp.concatenate([first, second], axis=0)
-    wave = (swap(whole, "x_lo"), shift(whole, "y", 4, 1), shift(whole, "y", 4, -1))
-    (f_x, s_x), (f_left, s_left), (f_right, s_right) = (
-        (v[:n], v[n:]) for v in lax.optimization_barrier(wave)
-    )
+    wave = (swap(v, "x_lo"), shift(v, "y", 4, 1), shift(v, "y", 4, -1))
+    blocks = (v,) + lax.optimization_barrier(wave)
+    first, f_x, f_left, f_right = (rows_of(w, core * n, n) for w in blocks)
+    second, s_x, s_left, s_right = (rows_of(w, (1 - core) * n, n) for w in blocks)
     early = (
         jnp.concatenate([first, f_x, f_left, f_right], axis=0),
         jnp.concatenate([second, s_x, s_left, s_right], axis=0),
@@ -78,14 +81,6 @@
     return out
 
 
-def halves(v, core):
-    half = v.shape[0] // 2
-    return (
-        lax.dynamic_slice_in_dim(v, core * half, half, 0),
-        lax.dynamic_slice_in_dim(v, (1 - core) * half, half, 0),
-    )
-
-
 def low(v):
     return v.astype(jnp.bfloat16)
 
@@ -110,7 +105,7 @@
         plane = low(jnp.sum(wide(split), axis=0))
         return low(wide(plane) + wide(swap(plane, "x_hi")))
 
-    *parts, pair = gather_tp(*halves(x, core), pair_sum)
+    *parts, pair = gather_tp(x, core, pair_sum)
     sent = exchange_z(pair)
     sent, pair = lax.optimization_barrier((sent, pair_sum(parts[1])))
     rows = [finish(sent), finish(exchange_z(pair))]
@@ -128,7 +123,7 @@
         return total
 
     applied = apply(parts, (0, 2, 1, 3))
-    twice_applied = apply(gather_tp(*halves(low(applied), core))[:2], (0, 1, 2, 3))
+    twice_applied = apply(gather_tp(low(applied), core)[:2], (0, 1, 2, 3))
     mixed = (
         quintic_one * x.astype(jnp.float32)
         + quintic_three * applied

time: 186 us -> 185 us (level)
  waiting for transfers between devices: 96.7 us -> 94.6 us
  matrix products: 16.7 us -> 18.8 us
    ppermute x13, waiting for transfers between devices: 44.6 us -> 42.5 us  [swap(): return lax.ppermute(v, axis, SWAP)]
    dot_general x12, matrix products: 16.7 us -> 18.8 us  [dot(): lax.dot_general(a, b, (dims, ((), ())), preferred_element_type=jnp.float32)]
  transfers between devices with their start and end apart: 35 -> 35, of which waited for: 21 -> 21; matrix products, arithmetic and copies ran while one was open for 7% -> 9% of each run, Pallas kernels for 0% -> 0%
where the time goes in v4:
time: 185 us
  waiting for transfers between devices  94.6 us (51%)
  starting transfers between devices  60.9 us (33%)
  matrix products  18.8 us (10%)
  local copies, waits for them, and re-layouts  8.1 us (4%)
  other arithmetic  2.03 us (1%)
    ppermute x13, waiting for transfers between devices, swap(): return lax.ppermute(v, axis, SWAP)  42.5 us
    ppermute x20, starting transfers between devices, shift(): return lax.ppermute(v, axis, [(i, (i + by) % size) for i in range(size)])  32.4 us
    ppermute x20, waiting for transfers between devices, shift(): return lax.ppermute(v, axis, [(i, (i + by) % size) for i in range(size)])  29.3 us
    all_to_all x2, waiting for transfers between devices, exchange_z(): return lax.all_to_all(pair, 'z', 0, 0)  22.8 us
    dot_general x12, matrix products, dot(): lax.dot_general(a, b, (dims, ((), ())), preferred_element_type=jnp.float32)  18.8 us
    ppermute x13, starting transfers between devices, swap(): return lax.ppermute(v, axis, SWAP)  15 us
    all_to_all x2, starting transfers between devices, exchange_z(): return lax.all_to_all(pair, 'z', 0, 0)  13.5 us
  transfers between devices with their start and end apart: 35, of which 21 were waited for; matrix products, arithmetic and copies ran while one was open for 9% of the time, Pallas kernels for 0%

profile of v4, /device:TPU:32, one launch (start us, length us, event | category | flops | bytes accessed | tf_op | source)
XLA Modules:
  0.0 184.9 jit_solution(2548915200133719314)
XLA Ops:
  5.8 9.1 %collective-permute-done = bf16[448,576]{1,0:T(8,128)(2,1)S(1)} collective-permute-done((bf16[448,576]{1,0:T(8,128)(2,1)}, bf16[448,576]{1,0:T(8,128)(2,1)S(1)}, u32[]{:S(2)}, u32[]{:S(2)}) %collective-permute-start) | collective-permute-done | bytes 516128 | tf_op jit(solution)/shard_map/ppermute | solution.py:28
  14.9 2.5 %collective-permute-done.1 = bf16[448,576]{1,0:T(8,128)(2,1)S(1)} collective-permute-done((bf16[448,576]{1,0:T(8,128)(2,1)}, bf16[448,576]{1,0:T(8,128)(2,1)S(1)}, u32[]{:S(2)}, u32[]{:S(2)}) %collective-permute-start.1) | collective-permute-done | bytes 516128 | tf_op jit(solution)/shard_map/ppermute | solution.py:24
  18.9 2.7 %fusion.9 = bf16[448,896]{1,0:T(8,128)(2,1)} fusion(bf16[448,576]{1,0:T(8,128)(2,1)S(1)} %copy-done, bf16[224,576]{1,0:T(8,128)(2,1)} %get-tuple-element.48, bf16[224,576]{1,0:T(8,128)(2,1)S(1)} %get-tuple-element.46, bf16[224,576]{1,0:T(8,128)(2,1)S(1)} %get-tuple-element.49, bf16[224,576]{1,0:T(8,128)(2,1)S(1)} %get-tuple-element.44), kind=kOutput, calls=%fused_computation.15 | convolution fusion | flops 466952192 | bytes 2351104 | tf_op jit(solution)/shard_map/dot_general | solution.py:20
  27.1 2.9 %fusion.1 = bf16[448,896]{1,0:T(8,128)(2,1)} fusion(bf16[448,896]{1,0:T(8,128)(2,1)} %collective-permute-done.6, bf16[448,576]{1,0:T(8,128)(2,1)S(1)} %copy-done, bf16[224,576]{1,0:T(8,128)(2,1)S(1)} %get-tuple-element.47, bf16[224,576]{1,0:T(8,128)(2,1)S(1)} %get-tuple-element.45, bf16[224,576]{1,0:T(8,128)(2,1)S(1)} %get-tuple-element.50, ...), kind=kOutput, calls=%fused_computation.3 | convolution fusion | flops 467755008 | bytes 3153920 | tf_op jit(solution)/shard_map/dot_general | solution.py:20
  30.1 4.7 %collective-permute-done.5 = bf16[224,576]{1,0:T(8,128)(2,1)S(1)} collective-permute-done((bf16[224,576]{1,0:T(8,128)(2,1)S(1)}, bf16[224,576]{1,0:T(8,128)(2,1)S(1)}, u32[]{:S(2)}, u32[]{:S(2)}) %collective-permute-start.5) | collective-permute-done | bytes 258080 | tf_op jit(solution)/shard_map/ppermute | solution.py:28
  37.2 8.6 %all-to-all-start = ((bf16[8,56,896]{2,1,0:T(8,128)(2,1)}), bf16[8,56,896]{2,1,0:T(8,128)(2,1)S(1)}, u32[]{:S(2)}, u32[]{:S(2)}) async-start(bf16[8,56,896]{2,1,0:T(8,128)(2,1)} %bitcast.2), calls=%async_computation | async-start | bytes 1605632 | tf_op jit(solution)/shard_map/all_to_all | solution.py:102
  54.0 7.0 %collective-permute-done.7 = bf16[224,576]{1,0:T(8,128)(2,1)S(1)} collective-permute-done((bf16[224,576]{1,0:T(8,128)(2,1)S(1)}, bf16[224,576]{1,0:T(8,128)(2,1)S(1)}, u32[]{:S(2)}, u32[]{:S(2)}) %collective-permute-start.7) | collective-permute-done | bytes 258080 | tf_op jit(solution)/shard_map/ppermute | solution.py:24
  63.6 3.7 %all-to-all-done = bf16[8,56,896]{2,1,0:T(8,128)(2,1)S(1)} async-done(((bf16[8,56,896]{2,1,0:T(8,128)(2,1)}), bf16[8,56,896]{2,1,0:T(8,128)(2,1)S(1)}, u32[]{:S(2)}, u32[]{:S(2)}) %all-to-all-start) | async-done | bytes 802848 | tf_op jit(solution)/shard_map/all_to_all | solution.py:102
  67.3 4.9 %all-to-all-start.1 = ((bf16[8,56,896]{2,1,0:T(8,128)(2,1)}), bf16[8,56,896]{2,1,0:T(8,128)(2,1)S(1)}, u32[]{:S(2)}, u32[]{:S(2)}) async-start(bf16[8,56,896]{2,1,0:T(8,128)(2,1)} %bitcast.21), calls=%async_computation.1 | async-start | bytes 1605632 | tf_op jit(solution)/shard_map/all_to_all | solution.py:102
  72.4 3.3 %collective-permute-start.12 = (bf16[56,896]{1,0:T(8,128)(2,1)S(1)}, bf16[56,896]{1,0:T(8,128)(2,1)S(1)}, u32[]{:S(2)}, u32[]{:S(2)}) collective-permute-start(bf16[56,896]{1,0:T(8,128)(2,1)S(1)} %reduce_sum.24), channel_id=1, source_target_pairs={{0,16},{16,0},{1,17},{17,1},{2,18},{18,2},{3,19},{19,3},{4,20},{20... | collective-permute-start | bytes 301064 | tf_op jit(solution)/shard_map/ppermute | solution.py:28
  75.6 19.1 %all-to-all-done.1 = bf16[8,56,896]{2,1,0:T(8,128)(2,1)S(1)} async-done(((bf16[8,56,896]{2,1,0:T(8,128)(2,1)}), bf16[8,56,896]{2,1,0:T(8,128)(2,1)S(1)}, u32[]{:S(2)}, u32[]{:S(2)}) %all-to-all-start.1) | async-done | bytes 802848 | tf_op jit(solution)/shard_map/all_to_all | solution.py:102
  94.8 3.1 %collective-permute-start.13 = (bf16[56,896]{1,0:T(8,128)(2,1)S(1)}, bf16[56,896]{1,0:T(8,128)(2,1)S(1)}, u32[]{:S(2)}, u32[]{:S(2)}) collective-permute-start(bf16[56,896]{1,0:T(8,128)(2,1)S(1)} %reduce_sum.25), channel_id=1, source_target_pairs={{0,16},{16,0},{1,17},{17,1},{2,18},{18,2},{3,19},{19,3},{4,20},{20... | collective-permute-start | bytes 301064 | tf_op jit(solution)/shard_map/ppermute | solution.py:28
  98.0 3.1 %collective-permute-done.13 = bf16[56,896]{1,0:T(8,128)(2,1)S(1)} collective-permute-done((bf16[56,896]{1,0:T(8,128)(2,1)S(1)}, bf16[56,896]{1,0:T(8,128)(2,1)S(1)}, u32[]{:S(2)}, u32[]{:S(2)}) %collective-permute-start.13) | collective-permute-done | bytes 100384 | tf_op jit(solution)/shard_map/ppermute | solution.py:28
  104.0 4.2 %collective-permute-done.14 = bf16[56,1792]{1,0:T(8,128)(2,1)} collective-permute-done((bf16[56,1792]{1,0:T(8,128)(2,1)}, bf16[56,1792]{1,0:T(8,128)(2,1)}, u32[]{:S(2)}, u32[]{:S(2)}) %collective-permute-start.14) | collective-permute-done | bytes 200736 | tf_op jit(solution)/shard_map/ppermute | solution.py:24
  108.5 2.8 %collective-permute-start.18 = (bf16[56,1792]{1,0:T(8,128)(2,1)}, bf16[56,1792]{1,0:T(8,128)(2,1)S(1)}, u32[]{:S(2)}, u32[]{:S(2)}) collective-permute-start(bf16[56,1792]{1,0:T(8,128)(2,1)} %collective-permute-done.14), channel_id=1, source_target_pairs={{0,64},{32,96},{64,128},{96,160},{128,192},{160,224},{192,0},{224,... | collective-permute-start | bytes 602120 | tf_op jit(solution)/shard_map/ppermute | solution.py:24
  111.3 4.0 %collective-permute-start.19 = (bf16[56,1792]{1,0:T(8,128)(2,1)S(1)}, bf16[56,1792]{1,0:T(8,128)(2,1)S(1)}, u32[]{:S(2)}, u32[]{:S(2)}) collective-permute-start(bf16[56,1792]{1,0:T(8,128)(2,1)S(1)} %collective-permute-done.15), channel_id=1, source_target_pairs={{0,192},{32,224},{64,0},{96,32},{128,64},{160,96},{192,128},{224,1... | collective-permute-start | bytes 602120 | tf_op jit(solution)/shard_map/ppermute | solution.py:24
  116.3 5.0 %collective-permute-done.17 = bf16[56,1792]{1,0:T(8,128)(2,1)S(1)} collective-permute-done((bf16[56,1792]{1,0:T(8,128)(2,1)S(1)}, bf16[56,1792]{1,0:T(8,128)(2,1)S(1)}, u32[]{:S(2)}, u32[]{:S(2)}) %collective-permute-start.17) | collective-permute-done | bytes 200736 | tf_op jit(solution)/shard_map/ppermute | solution.py:24
  121.3 4.8 %collective-permute-start.21 = (bf16[56,896]{1,0:T(8,128)(2,1)S(1)}, bf16[56,896]{1,0:T(8,128)(2,1)S(1)}, u32[]{:S(2)}, u32[]{:S(2)}) collective-permute-start(bf16[56,896]{1,0:T(8,128)(2,1)S(1)} %slice.73), channel_id=1, source_target_pairs={{0,192},{32,224},{64,0},{96,32},{128,64},{160,96},{192,128},{224,1... | collective-permute-start | bytes 301064 | tf_op jit(solution)/shard_map/ppermute | solution.py:24
  128.4 4.6 %collective-permute-done.20 = bf16[56,896]{1,0:T(8,128)(2,1)S(1)} collective-permute-done((bf16[56,896]{1,0:T(8,128)(2,1)S(1)}, bf16[56,896]{1,0:T(8,128)(2,1)S(1)}, u32[]{:S(2)}, u32[]{:S(2)}) %collective-permute-start.20) | collective-permute-done | bytes 100384 | tf_op jit(solution)/shard_map/ppermute | solution.py:24
  134.1 2.5 %collective-permute-done.22 = bf16[448,1792]{1,0:T(8,128)(2,1)S(1)} collective-permute-done((bf16[448,1792]{1,0:T(8,128)(2,1)S(1)}, bf16[448,1792]{1,0:T(8,128)(2,1)S(1)}, u32[]{:S(2)}, u32[]{:S(2)}) %collective-permute-start.22) | collective-permute-done | bytes 1605664 | tf_op jit(solution)/shard_map/ppermute | solution.py:28
  145.1 10.3 %collective-permute-done.23 = bf16[448,576]{1,0:T(8,128)(2,1)S(1)} collective-permute-done((bf16[448,576]{1,0:T(8,128)(2,1)S(1)}, bf16[448,576]{1,0:T(8,128)(2,1)S(1)}, u32[]{:S(2)}, u32[]{:S(2)}) %collective-permute-start.23) | collective-permute-done | bytes 516128 | tf_op jit(solution)/shard_map/ppermute | solution.py:28
  155.4 2.4 %collective-permute-done.24 = bf16[448,576]{1,0:T(8,128)(2,1)S(1)} collective-permute-done((bf16[448,576]{1,0:T(8,128)(2,1)S(1)}, bf16[448,576]{1,0:T(8,128)(2,1)S(1)}, u32[]{:S(2)}, u32[]{:S(2)}) %collective-permute-start.24) | collective-permute-done | bytes 516128 | tf_op jit(solution)/shard_map/ppermute | solution.py:24
  163.8 7.5 %collective-permute-done.28 = bf16[224,576]{1,0:T(8,128)(2,1)S(1)} collective-permute-done((bf16[224,576]{1,0:T(8,128)(2,1)S(1)}, bf16[224,576]{1,0:T(8,128)(2,1)S(1)}, u32[]{:S(2)}, u32[]{:S(2)}) %collective-permute-start.28) | collective-permute-done | bytes 258080 | tf_op jit(solution)/shard_map/ppermute | solution.py:28
  177.5 3.5 %collective-permute-done.32 = bf16[224,576]{1,0:T(8,128)(2,1)S(1)} collective-permute-done((bf16[224,576]{1,0:T(8,128)(2,1)S(1)}, bf16[224,576]{1,0:T(8,128)(2,1)S(1)}, u32[]{:S(2)}, u32[]{:S(2)}) %collective-permute-start.32) | collective-permute-done | bytes 258080 | tf_op jit(solution)/shard_map/ppermute | solution.py:28
  (145 shorter events, 57.9 us)
Async XLA Ops:
  0.0 14.9 %collective-permute-start = (bf16[448,576]{1,0:T(8,128)(2,1)}, bf16[448,576]{1,0:T(8,128)(2,1)S(1)}, u32[]{:S(2)}, u32[]{:S(2)}) collective-permute-start(bf16[448,576]{1,0:T(8,128)(2,1)} %param.1), channel_id=1, source_target_pairs={{0,4},{4,0},{1,5},{5,1},{2,6},{6,2},{3,7},{7,3},{8,12},{12,8},{9,1... | collective-permute-start | bytes 1548296 | tf_op jit(solution)/shard_map/ppermute | solution.py:28
  1.5 16.0 %collective-permute-start.1 = (bf16[448,576]{1,0:T(8,128)(2,1)}, bf16[448,576]{1,0:T(8,128)(2,1)S(1)}, u32[]{:S(2)}, u32[]{:S(2)}) collective-permute-start(bf16[448,576]{1,0:T(8,128)(2,1)} %param.1), channel_id=1, source_target_pairs={{0,1},{1,2},{2,3},{3,0},{4,5},{5,6},{6,7},{7,4},{8,9},{9,10},{10,1... | collective-permute-start | bytes 1548296 | tf_op jit(solution)/shard_map/ppermute | solution.py:24
  3.1 14.4 %collective-permute-start.2 = (bf16[448,576]{1,0:T(8,128)(2,1)}, bf16[448,576]{1,0:T(8,128)(2,1)S(1)}, u32[]{:S(2)}, u32[]{:S(2)}) collective-permute-start(bf16[448,576]{1,0:T(8,128)(2,1)} %param.1), channel_id=1, source_target_pairs={{0,3},{1,0},{2,1},{3,2},{4,7},{5,4},{6,5},{7,6},{8,11},{9,8},{10,9... | collective-permute-start | bytes 1548296 | tf_op jit(solution)/shard_map/ppermute | solution.py:24
  21.8 13.6 %collective-permute-start.3 = (bf16[336,576]{1,0:T(8,128)(2,1)S(1)}, bf16[336,576]{1,0:T(8,128)(2,1)S(1)}, u32[]{:S(2)}, u32[]{:S(2)}) collective-permute-start(bf16[336,576]{1,0:T(8,128)(2,1)S(1)} %get-tuple-element.62), channel_id=1, source_target_pairs={{0,1},{1,2},{2,3},{3,0},{4,5},{5,6},{6,7},{7,4},{8,9},{9,10},{10,1... | collective-permute-start | bytes 1161224 | tf_op jit(solution)/shard_map/ppermute | solution.py:24
  23.4 12.0 %collective-permute-start.4 = (bf16[336,576]{1,0:T(8,128)(2,1)S(1)}, bf16[336,576]{1,0:T(8,128)(2,1)S(1)}, u32[]{:S(2)}, u32[]{:S(2)}) collective-permute-start(bf16[336,576]{1,0:T(8,128)(2,1)S(1)} %get-tuple-element.61), channel_id=1, source_target_pairs={{0,3},{1,0},{2,1},{3,2},{4,7},{5,4},{6,5},{7,6},{8,11},{9,8},{10,9... | collective-permute-start | bytes 1161224 | tf_op jit(solution)/shard_map/ppermute | solution.py:24
  25.6 20.2 %collective-permute-start.9 = (bf16[224,576]{1,0:T(8,128)(2,1)}, bf16[224,576]{1,0:T(8,128)(2,1)S(1)}, u32[]{:S(2)}, u32[]{:S(2)}) collective-permute-start(bf16[224,576]{1,0:T(8,128)(2,1)} %get-tuple-element.48), channel_id=1, source_target_pairs={{0,4},{4,0},{1,5},{5,1},{2,6},{6,2},{3,7},{7,3},{8,12},{12,8},{9,1... | collective-permute-start | bytes 774152 | tf_op jit(solution)/shard_map/ppermute | solution.py:28
  36.7 9.8 %collective-permute-start.10 = (bf16[224,576]{1,0:T(8,128)(2,1)}, bf16[224,576]{1,0:T(8,128)(2,1)}, u32[]{:S(2)}, u32[]{:S(2)}) collective-permute-start(bf16[224,576]{1,0:T(8,128)(2,1)} %pad_maximum_fusion.9), channel_id=1, source_target_pairs={{0,4},{4,0},{1,5},{5,1},{2,6},{6,2},{3,7},{7,3},{8,12},{12,8},{9,1... | collective-permute-start | bytes 774152 | tf_op jit(solution)/shard_map/ppermute | solution.py:28
  37.2 30.1 %all-to-all-start = ((bf16[8,56,896]{2,1,0:T(8,128)(2,1)}), bf16[8,56,896]{2,1,0:T(8,128)(2,1)S(1)}, u32[]{:S(2)}, u32[]{:S(2)}) async-start(bf16[8,56,896]{2,1,0:T(8,128)(2,1)} %bitcast.2), calls=%async_computation | async-start | bytes 1605632 | tf_op jit(solution)/shard_map/all_to_all | solution.py:102
  50.4 10.6 %collective-permute-start.11 = (bf16[448,896]{1,0:T(8,128)(2,1)S(1)}, bf16[448,896]{1,0:T(8,128)(2,1)S(1)}, u32[]{:S(2)}, u32[]{:S(2)}) collective-permute-start(bf16[448,896]{1,0:T(8,128)(2,1)S(1)} %fusion.10), channel_id=1, source_target_pairs={{0,8},{8,0},{1,9},{9,1},{2,10},{10,2},{3,11},{11,3},{4,12},{12,4},... | collective-permute-start | bytes 2408456 | tf_op jit(solution)/shard_map/ppermute | solution.py:28
  50.5 10.5 %collective-permute-start.7 = (bf16[224,576]{1,0:T(8,128)(2,1)S(1)}, bf16[224,576]{1,0:T(8,128)(2,1)S(1)}, u32[]{:S(2)}, u32[]{:S(2)}) collective-permute-start(bf16[224,576]{1,0:T(8,128)(2,1)S(1)} %get-tuple-element.45), channel_id=1, source_target_pairs={{0,1},{1,2},{2,3},{3,0},{4,5},{5,6},{6,7},{7,4},{8,9},{9,10},{10,1... | collective-permute-start | bytes 774152 | tf_op jit(solution)/shard_map/ppermute | solution.py:24
  67.3 27.4 %all-to-all-start.1 = ((bf16[8,56,896]{2,1,0:T(8,128)(2,1)}), bf16[8,56,896]{2,1,0:T(8,128)(2,1)S(1)}, u32[]{:S(2)}, u32[]{:S(2)}) async-start(bf16[8,56,896]{2,1,0:T(8,128)(2,1)} %bitcast.21), calls=%async_computation.1 | async-start | bytes 1605632 | tf_op jit(solution)/shard_map/all_to_all | solution.py:102
  72.4 25.6 %collective-permute-start.12 = (bf16[56,896]{1,0:T(8,128)(2,1)S(1)}, bf16[56,896]{1,0:T(8,128)(2,1)S(1)}, u32[]{:S(2)}, u32[]{:S(2)}) collective-permute-start(bf16[56,896]{1,0:T(8,128)(2,1)S(1)} %reduce_sum.24), channel_id=1, source_target_pairs={{0,16},{16,0},{1,17},{17,1},{2,18},{18,2},{3,19},{19,3},{4,20},{20... | collective-permute-start | bytes 301064 | tf_op jit(solution)/shard_map/ppermute | solution.py:28
  108.2 18.0 %collective-permute-start.16 = (bf16[56,1792]{1,0:T(8,128)(2,1)}, bf16[56,1792]{1,0:T(8,128)(2,1)S(1)}, u32[]{:S(2)}, u32[]{:S(2)}) collective-permute-start(bf16[56,1792]{1,0:T(8,128)(2,1)} %collective-permute-done.14), channel_id=1, source_target_pairs={{0,32},{32,64},{64,96},{96,128},{128,160},{160,192},{192,224},{224... | collective-permute-start | bytes 602120 | tf_op jit(solution)/shard_map/ppermute | solution.py:24
  108.5 19.5 %collective-permute-start.18 = (bf16[56,1792]{1,0:T(8,128)(2,1)}, bf16[56,1792]{1,0:T(8,128)(2,1)S(1)}, u32[]{:S(2)}, u32[]{:S(2)}) collective-permute-start(bf16[56,1792]{1,0:T(8,128)(2,1)} %collective-permute-done.14), channel_id=1, source_target_pairs={{0,64},{32,96},{64,128},{96,160},{128,192},{160,224},{192,0},{224,... | collective-permute-start | bytes 602120 | tf_op jit(solution)/shard_map/ppermute | solution.py:24
  111.3 10.0 %collective-permute-start.17 = (bf16[56,1792]{1,0:T(8,128)(2,1)S(1)}, bf16[56,1792]{1,0:T(8,128)(2,1)S(1)}, u32[]{:S(2)}, u32[]{:S(2)}) collective-permute-start(bf16[56,1792]{1,0:T(8,128)(2,1)S(1)} %collective-permute-done.15), channel_id=1, source_target_pairs={{0,224},{32,0},{64,32},{96,64},{128,96},{160,128},{192,160},{224,1... | collective-permute-start | bytes 602120 | tf_op jit(solution)/shard_map/ppermute | solution.py:24
  111.3 16.7 %collective-permute-start.19 = (bf16[56,1792]{1,0:T(8,128)(2,1)S(1)}, bf16[56,1792]{1,0:T(8,128)(2,1)S(1)}, u32[]{:S(2)}, u32[]{:S(2)}) collective-permute-start(bf16[56,1792]{1,0:T(8,128)(2,1)S(1)} %collective-permute-done.15), channel_id=1, source_target_pairs={{0,192},{32,224},{64,0},{96,32},{128,64},{160,96},{192,128},{224,1... | collective-permute-start | bytes 602120 | tf_op jit(solution)/shard_map/ppermute | solution.py:24
  140.3 15.1 %collective-permute-start.23 = (bf16[448,576]{1,0:T(8,128)(2,1)S(1)}, bf16[448,576]{1,0:T(8,128)(2,1)S(1)}, u32[]{:S(2)}, u32[]{:S(2)}) collective-permute-start(bf16[448,576]{1,0:T(8,128)(2,1)S(1)} %get-tuple-element.65), channel_id=1, source_target_pairs={{0,4},{4,0},{1,5},{5,1},{2,6},{6,2},{3,7},{7,3},{8,12},{12,8},{9,1... | collective-permute-start | bytes 1548296 | tf_op jit(solution)/shard_map/ppermute | solution.py:28
  141.8 16.0 %collective-permute-start.24 = (bf16[448,576]{1,0:T(8,128)(2,1)S(1)}, bf16[448,576]{1,0:T(8,128)(2,1)S(1)}, u32[]{:S(2)}, u32[]{:S(2)}) collective-permute-start(bf16[448,576]{1,0:T(8,128)(2,1)S(1)} %get-tuple-element.65), channel_id=1, source_target_pairs={{0,1},{1,2},{2,3},{3,0},{4,5},{5,6},{6,7},{7,4},{8,9},{9,10},{10,1... | collective-permute-start | bytes 1548296 | tf_op jit(solution)/shard_map/ppermute | solution.py:24
  142.9 14.9 %collective-permute-start.25 = (bf16[448,576]{1,0:T(8,128)(2,1)S(1)}, bf16[448,576]{1,0:T(8,128)(2,1)S(1)}, u32[]{:S(2)}, u32[]{:S(2)}) collective-permute-start(bf16[448,576]{1,0:T(8,128)(2,1)S(1)} %get-tuple-element.65), channel_id=1, source_target_pairs={{0,3},{1,0},{2,1},{3,2},{4,7},{5,4},{6,5},{7,6},{8,11},{9,8},{10,9... | collective-permute-start | bytes 1548296 | tf_op jit(solution)/shard_map/ppermute | solution.py:24
  158.0 14.1 %collective-permute-start.26 = (bf16[336,576]{1,0:T(8,128)(2,1)S(1)}, bf16[336,576]{1,0:T(8,128)(2,1)S(1)}, u32[]{:S(2)}, u32[]{:S(2)}) collective-permute-start(bf16[336,576]{1,0:T(8,128)(2,1)S(1)} %get-tuple-element.60), channel_id=1, source_target_pairs={{0,1},{1,2},{2,3},{3,0},{4,5},{5,6},{6,7},{7,4},{8,9},{9,10},{10,1... | collective-permute-start | bytes 1161224 | tf_op jit(solution)/shard_map/ppermute | solution.py:24
  159.1 13.0 %collective-permute-start.27 = (bf16[336,576]{1,0:T(8,128)(2,1)S(1)}, bf16[336,576]{1,0:T(8,128)(2,1)S(1)}, u32[]{:S(2)}, u32[]{:S(2)}) collective-permute-start(bf16[336,576]{1,0:T(8,128)(2,1)S(1)} %get-tuple-element.59), channel_id=1, source_target_pairs={{0,3},{1,0},{2,1},{3,2},{4,7},{5,4},{6,5},{7,6},{8,11},{9,8},{10,9... | collective-permute-start | bytes 1161224 | tf_op jit(solution)/shard_map/ppermute | solution.py:24
  161.4 9.9 %collective-permute-start.28 = (bf16[224,576]{1,0:T(8,128)(2,1)S(1)}, bf16[224,576]{1,0:T(8,128)(2,1)S(1)}, u32[]{:S(2)}, u32[]{:S(2)}) collective-permute-start(bf16[224,576]{1,0:T(8,128)(2,1)S(1)} %get-tuple-element.42), channel_id=1, source_target_pairs={{0,4},{4,0},{1,5},{5,1},{2,6},{6,2},{3,7},{7,3},{8,12},{12,8},{9,1... | collective-permute-start | bytes 774152 | tf_op jit(solution)/shard_map/ppermute | solution.py:28
  162.2 15.2 %collective-permute-start.31 = (bf16[224,576]{1,0:T(8,128)(2,1)S(1)}, bf16[224,576]{1,0:T(8,128)(2,1)S(1)}, u32[]{:S(2)}, u32[]{:S(2)}) collective-permute-start(bf16[224,576]{1,0:T(8,128)(2,1)S(1)} %get-tuple-element.38), channel_id=1, source_target_pairs={{0,4},{4,0},{1,5},{5,1},{2,6},{6,2},{3,7},{7,3},{8,12},{12,8},{9,1... | collective-permute-start | bytes 774152 | tf_op jit(solution)/shard_map/ppermute | solution.py:28
  163.8 18.1 %collective-permute-start.29 = (bf16[224,576]{1,0:T(8,128)(2,1)S(1)}, bf16[224,576]{1,0:T(8,128)(2,1)S(1)}, u32[]{:S(2)}, u32[]{:S(2)}) collective-permute-start(bf16[224,576]{1,0:T(8,128)(2,1)S(1)} %get-tuple-element.41), channel_id=1, source_target_pairs={{0,1},{1,2},{2,3},{3,0},{4,5},{5,6},{6,7},{7,4},{8,9},{9,10},{10,1... | collective-permute-start | bytes 774152 | tf_op jit(solution)/shard_map/ppermute | solution.py:24
  (33 other events, 192.8 us)

commit v5 on v3

--- a/solution.py
+++ b/solution.py
@@ -120,15 +120,16 @@
     n = rows.shape[1] // 2
     grams = [g[:, i : i + n] for i in (0, n) for g in (gram_mine, gram_other)]
 
-    def apply(blocks, order):
-        flat = [b for part in blocks for b in part]
-        total = 0
+    def apply(total, flat, order):
         for i in order:
             total = total + dot(grams[i], flat[i], ((1,), (0,)))
         return total
 
-    applied = apply(parts, (0, 2, 1, 3))
-    twice_applied = apply(gather_tp(*halves(low(applied), core))[:2], (0, 1, 2, 3))
+    applied = apply(0, parts[0] + parts[1], (0, 2, 1, 3))
+    early, late, partial_sum = gather_tp(
+        *halves(low(applied), core), lambda early: apply(0, early, (0, 1))
+    )
+    twice_applied = apply(partial_sum, early + late, (2, 3))
     mixed = (
         quintic_one * x.astype(jnp.float32)
         + quintic_three * applied

time: 186 us -> 190 us (1.022)
  waiting for transfers between devices: 96.7 us -> 99 us
    ppermute x20, waiting for transfers between devices: 29.4 us -> 50.3 us  [shift(): return lax.ppermute(v, axis, [(i, (i + by) % size) for i in range(size)])]
    ppermute x13, waiting for transfers between devices: 44.6 us -> 27.7 us  [swap(): return lax.ppermute(v, axis, SWAP)]
  transfers between devices with their start and end apart: 35 -> 35, of which waited for: 21 -> 17; matrix products, arithmetic and copies ran while one was open for 7% -> 7% of each run, Pallas kernels for 0% -> 0%
where the time goes in v5:
time: 190 us; the launch traced here: 188 us
  waiting for transfers between devices  99 us (52%)
  starting transfers between devices  61.9 us (33%)
  matrix products  16.8 us (9%)
  local copies, waits for them, and re-layouts  7.88 us (4%)
  other arithmetic  2.12 us (1%)
    ppermute x20, waiting for transfers between devices, shift(): return lax.ppermute(v, axis, [(i, (i + by) % size) for i in range(size)])  50.3 us
    ppermute x20, starting transfers between devices, shift(): return lax.ppermute(v, axis, [(i, (i + by) % size) for i in range(size)])  34 us
    ppermute x13, waiting for transfers between devices, swap(): return lax.ppermute(v, axis, SWAP)  27.7 us
    all_to_all x2, waiting for transfers between devices, exchange_z(): return lax.all_to_all(pair, 'z', 0, 0)  21 us
    dot_general x12, matrix products, dot(): lax.dot_general(a, b, (dims, ((), ())), preferred_element_type=jnp.float32)  16.8 us
    ppermute x13, starting transfers between devices, swap(): return lax.ppermute(v, axis, SWAP)  14.4 us
    all_to_all x2, starting transfers between devices, exchange_z(): return lax.all_to_all(pair, 'z', 0, 0)  13.5 us
  transfers between devices with their start and end apart: 35, of which 17 were waited for; matrix products, arithmetic and copies ran while one was open for 7% of the time, Pallas kernels for 0%

profile of v5, /device:TPU:32, one launch (start us, length us, event | category | flops | bytes accessed | tf_op | source)
XLA Modules:
  0.0 188.2 jit_solution(473311849571802030)
XLA Ops:
  1.2 3.1 %collective-permute-start.2 = (bf16[448,576]{1,0:T(8,128)(2,1)S(1)}, bf16[448,576]{1,0:T(8,128)(2,1)S(1)}, u32[]{:S(2)}, u32[]{:S(2)}) collective-permute-start(bf16[448,576]{1,0:T(8,128)(2,1)S(1)} %pad_maximum_fusion.3), channel_id=1, source_target_pairs={{0,3},{1,0},{2,1},{3,2},{4,7},{5,4},{6,5},{7,6},{8,11},{9,8},{10,9... | collective-permute-start | bytes 1548296 | tf_op jit(solution)/shard_map/ppermute | solution.py:24
  5.7 10.7 %collective-permute-done.2 = bf16[448,576]{1,0:T(8,128)(2,1)S(1)} collective-permute-done((bf16[448,576]{1,0:T(8,128)(2,1)S(1)}, bf16[448,576]{1,0:T(8,128)(2,1)S(1)}, u32[]{:S(2)}, u32[]{:S(2)}) %collective-permute-start.2) | collective-permute-done | bytes 516128 | tf_op jit(solution)/shard_map/ppermute | solution.py:24
  16.5 3.4 %collective-permute-done.1 = bf16[448,576]{1,0:T(8,128)(2,1)S(1)} collective-permute-done((bf16[448,576]{1,0:T(8,128)(2,1)S(1)}, bf16[448,576]{1,0:T(8,128)(2,1)S(1)}, u32[]{:S(2)}, u32[]{:S(2)}) %collective-permute-start.1) | collective-permute-done | bytes 516128 | tf_op jit(solution)/shard_map/ppermute | solution.py:24
  29.4 11.2 %collective-permute-done.5 = bf16[224,576]{1,0:T(8,128)(2,1)S(1)} collective-permute-done((bf16[224,576]{1,0:T(8,128)(2,1)S(1)}, bf16[224,576]{1,0:T(8,128)(2,1)S(1)}, u32[]{:S(2)}, u32[]{:S(2)}) %collective-permute-start.5) | collective-permute-done | bytes 258080 | tf_op jit(solution)/shard_map/ppermute | solution.py:28
  43.3 8.6 %all-to-all-start = ((bf16[8,56,896]{2,1,0:T(8,128)(2,1)}), bf16[8,56,896]{2,1,0:T(8,128)(2,1)S(1)}, u32[]{:S(2)}, u32[]{:S(2)}) async-start(bf16[8,56,896]{2,1,0:T(8,128)(2,1)} %bitcast.2), calls=%async_computation | async-start | bytes 1605632 | tf_op jit(solution)/shard_map/all_to_all | solution.py:107
  57.0 3.0 %collective-permute-start.8 = (bf16[224,576]{1,0:T(8,128)(2,1)S(1)}, bf16[224,576]{1,0:T(8,128)(2,1)S(1)}, u32[]{:S(2)}, u32[]{:S(2)}) collective-permute-start(bf16[224,576]{1,0:T(8,128)(2,1)S(1)} %slice.103), channel_id=1, source_target_pairs={{0,3},{1,0},{2,1},{3,2},{4,7},{5,4},{6,5},{7,6},{8,11},{9,8},{10,9... | collective-permute-start | bytes 774152 | tf_op jit(solution)/shard_map/ppermute | solution.py:24
  60.0 7.0 %collective-permute-done.7 = bf16[224,576]{1,0:T(8,128)(2,1)S(1)} collective-permute-done((bf16[224,576]{1,0:T(8,128)(2,1)S(1)}, bf16[224,576]{1,0:T(8,128)(2,1)S(1)}, u32[]{:S(2)}, u32[]{:S(2)}) %collective-permute-start.7) | collective-permute-done | bytes 258080 | tf_op jit(solution)/shard_map/ppermute | solution.py:24
  69.6 3.2 %all-to-all-done = bf16[8,56,896]{2,1,0:T(8,128)(2,1)S(1)} async-done(((bf16[8,56,896]{2,1,0:T(8,128)(2,1)}), bf16[8,56,896]{2,1,0:T(8,128)(2,1)S(1)}, u32[]{:S(2)}, u32[]{:S(2)}) %all-to-all-start) | async-done | bytes 802848 | tf_op jit(solution)/shard_map/all_to_all | solution.py:107
  72.8 4.9 %all-to-all-start.1 = ((bf16[8,56,896]{2,1,0:T(8,128)(2,1)}), bf16[8,56,896]{2,1,0:T(8,128)(2,1)S(1)}, u32[]{:S(2)}, u32[]{:S(2)}) async-start(bf16[8,56,896]{2,1,0:T(8,128)(2,1)} %bitcast.21), calls=%async_computation.1 | async-start | bytes 1605632 | tf_op jit(solution)/shard_map/all_to_all | solution.py:107
  77.8 3.0 %collective-permute-start.12 = (bf16[56,896]{1,0:T(8,128)(2,1)S(1)}, bf16[56,896]{1,0:T(8,128)(2,1)S(1)}, u32[]{:S(2)}, u32[]{:S(2)}) collective-permute-start(bf16[56,896]{1,0:T(8,128)(2,1)S(1)} %reduce_sum.24), channel_id=1, source_target_pairs={{0,16},{16,0},{1,17},{17,1},{2,18},{18,2},{3,19},{19,3},{4,20},{20... | collective-permute-start | bytes 301064 | tf_op jit(solution)/shard_map/ppermute | solution.py:28
  80.8 17.9 %all-to-all-done.1 = bf16[8,56,896]{2,1,0:T(8,128)(2,1)S(1)} async-done(((bf16[8,56,896]{2,1,0:T(8,128)(2,1)}), bf16[8,56,896]{2,1,0:T(8,128)(2,1)S(1)}, u32[]{:S(2)}, u32[]{:S(2)}) %all-to-all-start.1) | async-done | bytes 802848 | tf_op jit(solution)/shard_map/all_to_all | solution.py:107
  98.8 2.8 %collective-permute-start.13 = (bf16[56,896]{1,0:T(8,128)(2,1)S(1)}, bf16[56,896]{1,0:T(8,128)(2,1)S(1)}, u32[]{:S(2)}, u32[]{:S(2)}) collective-permute-start(bf16[56,896]{1,0:T(8,128)(2,1)S(1)} %reduce_sum.25), channel_id=1, source_target_pairs={{0,16},{16,0},{1,17},{17,1},{2,18},{18,2},{3,19},{19,3},{4,20},{20... | collective-permute-start | bytes 301064 | tf_op jit(solution)/shard_map/ppermute | solution.py:28
  101.7 3.4 %collective-permute-done.13 = bf16[56,896]{1,0:T(8,128)(2,1)S(1)} collective-permute-done((bf16[56,896]{1,0:T(8,128)(2,1)S(1)}, bf16[56,896]{1,0:T(8,128)(2,1)S(1)}, u32[]{:S(2)}, u32[]{:S(2)}) %collective-permute-start.13) | collective-permute-done | bytes 100384 | tf_op jit(solution)/shard_map/ppermute | solution.py:28
  107.9 4.0 %collective-permute-done.14 = bf16[56,1792]{1,0:T(8,128)(2,1)} collective-permute-done((bf16[56,1792]{1,0:T(8,128)(2,1)}, bf16[56,1792]{1,0:T(8,128)(2,1)}, u32[]{:S(2)}, u32[]{:S(2)}) %collective-permute-start.14) | collective-permute-done | bytes 200736 | tf_op jit(solution)/shard_map/ppermute | solution.py:24
  112.3 4.2 %collective-permute-start.16 = (bf16[56,1792]{1,0:T(8,128)(2,1)}, bf16[56,1792]{1,0:T(8,128)(2,1)S(1)}, u32[]{:S(2)}, u32[]{:S(2)}) collective-permute-start(bf16[56,1792]{1,0:T(8,128)(2,1)} %collective-permute-done.14), channel_id=1, source_target_pairs={{0,32},{32,64},{64,96},{96,128},{128,160},{160,192},{192,224},{224... | collective-permute-start | bytes 602120 | tf_op jit(solution)/shard_map/ppermute | solution.py:24
  120.8 5.0 %collective-permute-done.16 = bf16[56,1792]{1,0:T(8,128)(2,1)S(1)} collective-permute-done((bf16[56,1792]{1,0:T(8,128)(2,1)}, bf16[56,1792]{1,0:T(8,128)(2,1)S(1)}, u32[]{:S(2)}, u32[]{:S(2)}) %collective-permute-start.16) | collective-permute-done | bytes 200736 | tf_op jit(solution)/shard_map/ppermute | solution.py:24
  126.2 6.7 %collective-permute-start.21 = (bf16[56,896]{1,0:T(8,128)(2,1)S(1)}, bf16[56,896]{1,0:T(8,128)(2,1)S(1)}, u32[]{:S(2)}, u32[]{:S(2)}) collective-permute-start(bf16[56,896]{1,0:T(8,128)(2,1)S(1)} %slice.125), channel_id=1, source_target_pairs={{0,192},{32,224},{64,0},{96,32},{128,64},{160,96},{192,128},{224,1... | collective-permute-start | bytes 301064 | tf_op jit(solution)/shard_map/ppermute | solution.py:24
  136.2 2.5 %collective-permute-done.22 = bf16[448,1792]{1,0:T(8,128)(2,1)S(1)} collective-permute-done((bf16[448,1792]{1,0:T(8,128)(2,1)S(1)}, bf16[448,1792]{1,0:T(8,128)(2,1)S(1)}, u32[]{:S(2)}, u32[]{:S(2)}) %collective-permute-start.22) | collective-permute-done | bytes 1605664 | tf_op jit(solution)/shard_map/ppermute | solution.py:28
  142.6 3.0 %collective-permute-start.25 = (bf16[448,576]{1,0:T(8,128)(2,1)S(1)}, bf16[448,576]{1,0:T(8,128)(2,1)S(1)}, u32[]{:S(2)}, u32[]{:S(2)}) collective-permute-start(bf16[448,576]{1,0:T(8,128)(2,1)S(1)} %pad_maximum_fusion.4), channel_id=1, source_target_pairs={{0,3},{1,0},{2,1},{3,2},{4,7},{5,4},{6,5},{7,6},{8,11},{9,8},{10,9... | collective-permute-start | bytes 1548296 | tf_op jit(solution)/shard_map/ppermute | solution.py:24
  146.2 12.4 %collective-permute-done.25 = bf16[448,576]{1,0:T(8,128)(2,1)S(1)} collective-permute-done((bf16[448,576]{1,0:T(8,128)(2,1)S(1)}, bf16[448,576]{1,0:T(8,128)(2,1)S(1)}, u32[]{:S(2)}, u32[]{:S(2)}) %collective-permute-start.25) | collective-permute-done | bytes 516128 | tf_op jit(solution)/shard_map/ppermute | solution.py:24
  158.7 2.9 %collective-permute-done.24 = bf16[448,576]{1,0:T(8,128)(2,1)S(1)} collective-permute-done((bf16[448,576]{1,0:T(8,128)(2,1)S(1)}, bf16[448,576]{1,0:T(8,128)(2,1)S(1)}, u32[]{:S(2)}, u32[]{:S(2)}) %collective-permute-start.24) | collective-permute-done | bytes 516128 | tf_op jit(solution)/shard_map/ppermute | solution.py:24
  167.9 7.9 %collective-permute-done.28 = bf16[224,576]{1,0:T(8,128)(2,1)S(1)} collective-permute-done((bf16[224,576]{1,0:T(8,128)(2,1)S(1)}, bf16[224,576]{1,0:T(8,128)(2,1)S(1)}, u32[]{:S(2)}, u32[]{:S(2)}) %collective-permute-start.28) | collective-permute-done | bytes 258080 | tf_op jit(solution)/shard_map/ppermute | solution.py:28
  177.5 3.3 %collective-permute-start.30 = (bf16[224,576]{1,0:T(8,128)(2,1)S(1)}, bf16[224,576]{1,0:T(8,128)(2,1)S(1)}, u32[]{:S(2)}, u32[]{:S(2)}) collective-permute-start(bf16[224,576]{1,0:T(8,128)(2,1)S(1)} %slice.121), channel_id=1, source_target_pairs={{0,3},{1,0},{2,1},{3,2},{4,7},{5,4},{6,5},{7,6},{8,11},{9,8},{10,9... | collective-permute-start | bytes 774152 | tf_op jit(solution)/shard_map/ppermute | solution.py:24
  180.8 2.7 %collective-permute-done.32 = bf16[224,576]{1,0:T(8,128)(2,1)S(1)} collective-permute-done((bf16[224,576]{1,0:T(8,128)(2,1)S(1)}, bf16[224,576]{1,0:T(8,128)(2,1)S(1)}, u32[]{:S(2)}, u32[]{:S(2)}) %collective-permute-start.32) | collective-permute-done | bytes 258080 | tf_op jit(solution)/shard_map/ppermute | solution.py:28
  (146 shorter events, 50.8 us)
Async XLA Ops:
  1.2 15.3 %collective-permute-start.2 = (bf16[448,576]{1,0:T(8,128)(2,1)S(1)}, bf16[448,576]{1,0:T(8,128)(2,1)S(1)}, u32[]{:S(2)}, u32[]{:S(2)}) collective-permute-start(bf16[448,576]{1,0:T(8,128)(2,1)S(1)} %pad_maximum_fusion.3), channel_id=1, source_target_pairs={{0,3},{1,0},{2,1},{3,2},{4,7},{5,4},{6,5},{7,6},{8,11},{9,8},{10,9... | collective-permute-start | bytes 1548296 | tf_op jit(solution)/shard_map/ppermute | solution.py:24
  4.3 15.6 %collective-permute-start.1 = (bf16[448,576]{1,0:T(8,128)(2,1)S(1)}, bf16[448,576]{1,0:T(8,128)(2,1)S(1)}, u32[]{:S(2)}, u32[]{:S(2)}) collective-permute-start(bf16[448,576]{1,0:T(8,128)(2,1)S(1)} %pad_maximum_fusion.3), channel_id=1, source_target_pairs={{0,1},{1,2},{2,3},{3,0},{4,5},{5,6},{6,7},{7,4},{8,9},{9,10},{10,1... | collective-permute-start | bytes 1548296 | tf_op jit(solution)/shard_map/ppermute | solution.py:24
  4.3 15.6 %collective-permute-start = (bf16[448,576]{1,0:T(8,128)(2,1)S(1)}, bf16[448,576]{1,0:T(8,128)(2,1)S(1)}, u32[]{:S(2)}, u32[]{:S(2)}) collective-permute-start(bf16[448,576]{1,0:T(8,128)(2,1)S(1)} %pad_maximum_fusion.3), channel_id=1, source_target_pairs={{0,4},{4,0},{1,5},{5,1},{2,6},{6,2},{3,7},{7,3},{8,12},{12,8},{9,1... | collective-permute-start | bytes 1548296 | tf_op jit(solution)/shard_map/ppermute | solution.py:28
  23.4 17.1 %collective-permute-start.4 = (bf16[336,576]{1,0:T(8,128)(2,1)S(1)}, bf16[336,576]{1,0:T(8,128)(2,1)S(1)}, u32[]{:S(2)}, u32[]{:S(2)}) collective-permute-start(bf16[336,576]{1,0:T(8,128)(2,1)S(1)} %get-tuple-element.63), channel_id=1, source_target_pairs={{0,3},{1,0},{2,1},{3,2},{4,7},{5,4},{6,5},{7,6},{8,11},{9,8},{10,9... | collective-permute-start | bytes 1161224 | tf_op jit(solution)/shard_map/ppermute | solution.py:24
  25.2 15.3 %collective-permute-start.3 = (bf16[336,576]{1,0:T(8,128)(2,1)S(1)}, bf16[336,576]{1,0:T(8,128)(2,1)S(1)}, u32[]{:S(2)}, u32[]{:S(2)}) collective-permute-start(bf16[336,576]{1,0:T(8,128)(2,1)S(1)} %get-tuple-element.64), channel_id=1, source_target_pairs={{0,1},{1,2},{2,3},{3,0},{4,5},{5,6},{6,7},{7,4},{8,9},{9,10},{10,1... | collective-permute-start | bytes 1161224 | tf_op jit(solution)/shard_map/ppermute | solution.py:24
  25.5 26.3 %collective-permute-start.9 = (bf16[224,576]{1,0:T(8,128)(2,1)}, bf16[224,576]{1,0:T(8,128)(2,1)S(1)}, u32[]{:S(2)}, u32[]{:S(2)}) collective-permute-start(bf16[224,576]{1,0:T(8,128)(2,1)} %get-tuple-element.48), channel_id=1, source_target_pairs={{0,4},{4,0},{1,5},{5,1},{2,6},{6,2},{3,7},{7,3},{8,12},{12,8},{9,1... | collective-permute-start | bytes 774152 | tf_op jit(solution)/shard_map/ppermute | solution.py:28
  27.0 13.5 %collective-permute-start.5 = (bf16[224,576]{1,0:T(8,128)(2,1)S(1)}, bf16[224,576]{1,0:T(8,128)(2,1)S(1)}, u32[]{:S(2)}, u32[]{:S(2)}) collective-permute-start(bf16[224,576]{1,0:T(8,128)(2,1)S(1)} %get-tuple-element.46), channel_id=1, source_target_pairs={{0,4},{4,0},{1,5},{5,1},{2,6},{6,2},{3,7},{7,3},{8,12},{12,8},{9,1... | collective-permute-start | bytes 774152 | tf_op jit(solution)/shard_map/ppermute | solution.py:28
  41.8 10.8 %collective-permute-start.10 = (bf16[224,576]{1,0:T(8,128)(2,1)}, bf16[224,576]{1,0:T(8,128)(2,1)}, u32[]{:S(2)}, u32[]{:S(2)}) collective-permute-start(bf16[224,576]{1,0:T(8,128)(2,1)} %pad_maximum_fusion.9), channel_id=1, source_target_pairs={{0,4},{4,0},{1,5},{5,1},{2,6},{6,2},{3,7},{7,3},{8,12},{12,8},{9,1... | collective-permute-start | bytes 774152 | tf_op jit(solution)/shard_map/ppermute | solution.py:28
  43.3 29.5 %all-to-all-start = ((bf16[8,56,896]{2,1,0:T(8,128)(2,1)}), bf16[8,56,896]{2,1,0:T(8,128)(2,1)S(1)}, u32[]{:S(2)}, u32[]{:S(2)}) async-start(bf16[8,56,896]{2,1,0:T(8,128)(2,1)} %bitcast.2), calls=%async_computation | async-start | bytes 1605632 | tf_op jit(solution)/shard_map/all_to_all | solution.py:107
  56.5 10.6 %collective-permute-start.11 = (bf16[448,896]{1,0:T(8,128)(2,1)S(1)}, bf16[448,896]{1,0:T(8,128)(2,1)S(1)}, u32[]{:S(2)}, u32[]{:S(2)}) collective-permute-start(bf16[448,896]{1,0:T(8,128)(2,1)S(1)} %fusion.5), channel_id=1, source_target_pairs={{0,8},{8,0},{1,9},{9,1},{2,10},{10,2},{3,11},{11,3},{4,12},{12,4},... | collective-permute-start | bytes 2408456 | tf_op jit(solution)/shard_map/ppermute | solution.py:28
  56.6 10.5 %collective-permute-start.7 = (bf16[224,576]{1,0:T(8,128)(2,1)S(1)}, bf16[224,576]{1,0:T(8,128)(2,1)S(1)}, u32[]{:S(2)}, u32[]{:S(2)}) collective-permute-start(bf16[224,576]{1,0:T(8,128)(2,1)S(1)} %get-tuple-element.45), channel_id=1, source_target_pairs={{0,1},{1,2},{2,3},{3,0},{4,5},{5,6},{6,7},{7,4},{8,9},{9,10},{10,1... | collective-permute-start | bytes 774152 | tf_op jit(solution)/shard_map/ppermute | solution.py:24
  72.8 25.9 %all-to-all-start.1 = ((bf16[8,56,896]{2,1,0:T(8,128)(2,1)}), bf16[8,56,896]{2,1,0:T(8,128)(2,1)S(1)}, u32[]{:S(2)}, u32[]{:S(2)}) async-start(bf16[8,56,896]{2,1,0:T(8,128)(2,1)} %bitcast.21), calls=%async_computation.1 | async-start | bytes 1605632 | tf_op jit(solution)/shard_map/all_to_all | solution.py:107
  77.8 23.8 %collective-permute-start.12 = (bf16[56,896]{1,0:T(8,128)(2,1)S(1)}, bf16[56,896]{1,0:T(8,128)(2,1)S(1)}, u32[]{:S(2)}, u32[]{:S(2)}) collective-permute-start(bf16[56,896]{1,0:T(8,128)(2,1)S(1)} %reduce_sum.24), channel_id=1, source_target_pairs={{0,16},{16,0},{1,17},{17,1},{2,18},{18,2},{3,19},{19,3},{4,20},{20... | collective-permute-start | bytes 301064 | tf_op jit(solution)/shard_map/ppermute | solution.py:28
  105.9 10.6 %collective-permute-start.15 = (bf16[56,1792]{1,0:T(8,128)(2,1)}, bf16[56,1792]{1,0:T(8,128)(2,1)S(1)}, u32[]{:S(2)}, u32[]{:S(2)}) collective-permute-start(bf16[56,1792]{1,0:T(8,128)(2,1)} %get-tuple-element.65), channel_id=1, source_target_pairs={{0,224},{32,0},{64,32},{96,64},{128,96},{160,128},{192,160},{224,1... | collective-permute-start | bytes 602120 | tf_op jit(solution)/shard_map/ppermute | solution.py:24
  111.9 21.0 %collective-permute-start.18 = (bf16[56,1792]{1,0:T(8,128)(2,1)}, bf16[56,1792]{1,0:T(8,128)(2,1)S(1)}, u32[]{:S(2)}, u32[]{:S(2)}) collective-permute-start(bf16[56,1792]{1,0:T(8,128)(2,1)} %collective-permute-done.14), channel_id=1, source_target_pairs={{0,64},{32,96},{64,128},{96,160},{128,192},{160,224},{192,0},{224,... | collective-permute-start | bytes 602120 | tf_op jit(solution)/shard_map/ppermute | solution.py:24
  112.3 13.6 %collective-permute-start.16 = (bf16[56,1792]{1,0:T(8,128)(2,1)}, bf16[56,1792]{1,0:T(8,128)(2,1)S(1)}, u32[]{:S(2)}, u32[]{:S(2)}) collective-permute-start(bf16[56,1792]{1,0:T(8,128)(2,1)} %collective-permute-done.14), channel_id=1, source_target_pairs={{0,32},{32,64},{64,96},{96,128},{128,160},{160,192},{192,224},{224... | collective-permute-start | bytes 602120 | tf_op jit(solution)/shard_map/ppermute | solution.py:24
  116.5 16.5 %collective-permute-start.19 = (bf16[56,1792]{1,0:T(8,128)(2,1)S(1)}, bf16[56,1792]{1,0:T(8,128)(2,1)S(1)}, u32[]{:S(2)}, u32[]{:S(2)}) collective-permute-start(bf16[56,1792]{1,0:T(8,128)(2,1)S(1)} %collective-permute-done.15), channel_id=1, source_target_pairs={{0,192},{32,224},{64,0},{96,32},{128,64},{160,96},{192,128},{224,1... | collective-permute-start | bytes 602120 | tf_op jit(solution)/shard_map/ppermute | solution.py:24
  142.6 16.0 %collective-permute-start.25 = (bf16[448,576]{1,0:T(8,128)(2,1)S(1)}, bf16[448,576]{1,0:T(8,128)(2,1)S(1)}, u32[]{:S(2)}, u32[]{:S(2)}) collective-permute-start(bf16[448,576]{1,0:T(8,128)(2,1)S(1)} %pad_maximum_fusion.4), channel_id=1, source_target_pairs={{0,3},{1,0},{2,1},{3,2},{4,7},{5,4},{6,5},{7,6},{8,11},{9,8},{10,9... | collective-permute-start | bytes 1548296 | tf_op jit(solution)/shard_map/ppermute | solution.py:24
  145.6 15.9 %collective-permute-start.24 = (bf16[448,576]{1,0:T(8,128)(2,1)S(1)}, bf16[448,576]{1,0:T(8,128)(2,1)S(1)}, u32[]{:S(2)}, u32[]{:S(2)}) collective-permute-start(bf16[448,576]{1,0:T(8,128)(2,1)S(1)} %pad_maximum_fusion.4), channel_id=1, source_target_pairs={{0,1},{1,2},{2,3},{3,0},{4,5},{5,6},{6,7},{7,4},{8,9},{9,10},{10,1... | collective-permute-start | bytes 1548296 | tf_op jit(solution)/shard_map/ppermute | solution.py:24
  145.7 15.9 %collective-permute-start.23 = (bf16[448,576]{1,0:T(8,128)(2,1)S(1)}, bf16[448,576]{1,0:T(8,128)(2,1)S(1)}, u32[]{:S(2)}, u32[]{:S(2)}) collective-permute-start(bf16[448,576]{1,0:T(8,128)(2,1)S(1)} %pad_maximum_fusion.4), channel_id=1, source_target_pairs={{0,4},{4,0},{1,5},{5,1},{2,6},{6,2},{3,7},{7,3},{8,12},{12,8},{9,1... | collective-permute-start | bytes 1548296 | tf_op jit(solution)/shard_map/ppermute | solution.py:28
  161.8 19.0 %collective-permute-start.31 = (bf16[224,576]{1,0:T(8,128)(2,1)S(1)}, bf16[224,576]{1,0:T(8,128)(2,1)S(1)}, u32[]{:S(2)}, u32[]{:S(2)}) collective-permute-start(bf16[224,576]{1,0:T(8,128)(2,1)S(1)} %get-tuple-element.40), channel_id=1, source_target_pairs={{0,4},{4,0},{1,5},{5,1},{2,6},{6,2},{3,7},{7,3},{8,12},{12,8},{9,1... | collective-permute-start | bytes 774152 | tf_op jit(solution)/shard_map/ppermute | solution.py:28
  162.4 13.3 %collective-permute-start.28 = (bf16[224,576]{1,0:T(8,128)(2,1)S(1)}, bf16[224,576]{1,0:T(8,128)(2,1)S(1)}, u32[]{:S(2)}, u32[]{:S(2)}) collective-permute-start(bf16[224,576]{1,0:T(8,128)(2,1)S(1)} %get-tuple-element.38), channel_id=1, source_target_pairs={{0,4},{4,0},{1,5},{5,1},{2,6},{6,2},{3,7},{7,3},{8,12},{12,8},{9,1... | collective-permute-start | bytes 774152 | tf_op jit(solution)/shard_map/ppermute | solution.py:28
  164.0 11.8 %collective-permute-start.27 = (bf16[336,576]{1,0:T(8,128)(2,1)S(1)}, bf16[336,576]{1,0:T(8,128)(2,1)S(1)}, u32[]{:S(2)}, u32[]{:S(2)}) collective-permute-start(bf16[336,576]{1,0:T(8,128)(2,1)S(1)} %get-tuple-element.61), channel_id=1, source_target_pairs={{0,3},{1,0},{2,1},{3,2},{4,7},{5,4},{6,5},{7,6},{8,11},{9,8},{10,9... | collective-permute-start | bytes 1161224 | tf_op jit(solution)/shard_map/ppermute | solution.py:24
  165.8 10.8 %collective-permute-start.26 = (bf16[336,576]{1,0:T(8,128)(2,1)S(1)}, bf16[336,576]{1,0:T(8,128)(2,1)S(1)}, u32[]{:S(2)}, u32[]{:S(2)}) collective-permute-start(bf16[336,576]{1,0:T(8,128)(2,1)S(1)} %get-tuple-element.62), channel_id=1, source_target_pairs={{0,1},{1,2},{2,3},{3,0},{4,5},{5,6},{6,7},{7,4},{8,9},{9,10},{10,1... | collective-permute-start | bytes 1161224 | tf_op jit(solution)/shard_map/ppermute | solution.py:24
  (32 other events, 178.6 us)

commit v6 on v3

--- a/solution.py
+++ b/solution.py
@@ -61,12 +61,13 @@
     return early, late, done
 
 
-def gather_z(v, base):
+def gather_z(parts, base):
+    v = jnp.concatenate(parts, axis=1)
     rows, columns = v.shape
     h = columns // 2
     z = lax.axis_index("z")
-    r1 = shift(v, "z", 8, 1)
-    l1 = shift(v, "z", 8, -1)
+    r1 = jnp.concatenate([shift(p, "z", 8, 1) for p in parts], axis=1)
+    l1 = jnp.concatenate([shift(p, "z", 8, -1) for p in parts], axis=1)
     r2 = shift(r1, "z", 8, 1)
     l2 = shift(l1, "z", 8, -1)
     r3 = shift(r1, "z", 8, 2)
@@ -114,10 +115,9 @@
     sent = exchange_z(pair)
     sent, pair = lax.optimization_barrier((sent, pair_sum(parts[1])))
     rows = [finish(sent), finish(exchange_z(pair))]
-    rows = jnp.concatenate(rows, axis=1)
-    gram_mine = gather_z(rows, jnp.zeros((8 * rows.shape[0], rows.shape[1]), rows.dtype))
+    n = rows[0].shape[1]
+    gram_mine = gather_z(rows, jnp.zeros((8 * rows[0].shape[0], 2 * n), rows[0].dtype))
     gram_other = swap(gram_mine, "core")
-    n = rows.shape[1] // 2
     grams = [g[:, i : i + n] for i in (0, n) for g in (gram_mine, gram_other)]
 
     def apply(blocks, order):

time: 186 us -> 182 us (0.978)
  matrix products: 16.7 us -> 14.8 us
    all_to_all x2, waiting for transfers between devices: 22.8 us -> 6.2 us  [exchange_z(): return lax.all_to_all(pair, 'z', 0, 0)]
    ppermute x20 -> x22, waiting for transfers between devices: 29.4 us -> 41.9 us  [shift(): return lax.ppermute(v, axis, [(i, (i + by) % size) for i in range(size)])]
    ppermute x13, waiting for transfers between devices: 44.6 us -> 47.7 us  [swap(): return lax.ppermute(v, axis, SWAP)]
    dot_general x12, matrix products: 16.7 us -> 14.8 us  [dot(): lax.dot_general(a, b, (dims, ((), ())), preferred_element_type=jnp.float32)]
    unnamed x44 -> x50, local copies, waits for them, and re-layouts: 2.5 us -> 4.38 us
    ppermute x20 -> x22, starting transfers between devices: 32.3 us -> 32.2 us  [shift(): return lax.ppermute(v, axis, [(i, (i + by) % size) for i in range(size)])]
  transfers between devices with their start and end apart: 35 -> 37, of which waited for: 21 -> 23; matrix products, arithmetic and copies ran while one was open for 7% -> 8% of each run, Pallas kernels for 0% -> 0%
where the time goes in v6:
time: 182 us
  waiting for transfers between devices  95.8 us (53%)
  starting transfers between devices  61.1 us (34%)
  matrix products  14.8 us (8%)
  local copies, waits for them, and re-layouts  8.18 us (4%)
    ppermute x13, waiting for transfers between devices, swap(): return lax.ppermute(v, axis, SWAP)  47.7 us
    ppermute x22, waiting for transfers between devices, shift(): return lax.ppermute(v, axis, [(i, (i + by) % size) for i in range(size)])  41.9 us
    ppermute x22, starting transfers between devices, shift(): return lax.ppermute(v, axis, [(i, (i + by) % size) for i in range(size)])  32.2 us
    ppermute x13, starting transfers between devices, swap(): return lax.ppermute(v, axis, SWAP)  15.4 us
    dot_general x12, matrix products, dot(): lax.dot_general(a, b, (dims, ((), ())), preferred_element_type=jnp.float32)  14.8 us
    all_to_all x2, starting transfers between devices, exchange_z(): return lax.all_to_all(pair, 'z', 0, 0)  13.5 us
    all_to_all x2, waiting for transfers between devices, exchange_z(): return lax.all_to_all(pair, 'z', 0, 0)  6.2 us
    unnamed x50, local copies, waits for them, and re-layouts  4.38 us
  transfers between devices with their start and end apart: 37, of which 23 were waited for; matrix products, arithmetic and copies ran while one was open for 8% of the time, Pallas kernels for 0%

profile of v6, /device:TPU:32, one launch (start us, length us, event | category | flops | bytes accessed | tf_op | source)
XLA Modules:
  0.0 181.9 jit_solution(11277871962059378373)
XLA Ops:
  6.0 10.0 %collective-permute-done = bf16[448,576]{1,0:T(8,128)(2,1)S(1)} collective-permute-done((bf16[448,576]{1,0:T(8,128)(2,1)S(1)}, bf16[448,576]{1,0:T(8,128)(2,1)S(1)}, u32[]{:S(2)}, u32[]{:S(2)}) %collective-permute-start) | collective-permute-done | bytes 516128 | tf_op jit(solution)/shard_map/ppermute | solution.py:28
  16.0 2.5 %collective-permute-done.1 = bf16[448,576]{1,0:T(8,128)(2,1)S(1)} collective-permute-done((bf16[448,576]{1,0:T(8,128)(2,1)S(1)}, bf16[448,576]{1,0:T(8,128)(2,1)S(1)}, u32[]{:S(2)}, u32[]{:S(2)}) %collective-permute-start.1) | collective-permute-done | bytes 516128 | tf_op jit(solution)/shard_map/ppermute | solution.py:24
  28.3 5.8 %collective-permute-done.5 = bf16[224,576]{1,0:T(8,128)(2,1)S(1)} collective-permute-done((bf16[224,576]{1,0:T(8,128)(2,1)S(1)}, bf16[224,576]{1,0:T(8,128)(2,1)S(1)}, u32[]{:S(2)}, u32[]{:S(2)}) %collective-permute-start.5) | collective-permute-done | bytes 258080 | tf_op jit(solution)/shard_map/ppermute | solution.py:28
  36.6 8.6 %all-to-all-start = ((bf16[8,56,896]{2,1,0:T(8,128)(2,1)}), bf16[8,56,896]{2,1,0:T(8,128)(2,1)S(1)}, u32[]{:S(2)}, u32[]{:S(2)}) async-start(bf16[8,56,896]{2,1,0:T(8,128)(2,1)} %bitcast.2), calls=%async_computation | async-start | bytes 1605632 | tf_op jit(solution)/shard_map/all_to_all | solution.py:108
  54.3 7.0 %collective-permute-done.7 = bf16[224,576]{1,0:T(8,128)(2,1)S(1)} collective-permute-done((bf16[224,576]{1,0:T(8,128)(2,1)S(1)}, bf16[224,576]{1,0:T(8,128)(2,1)S(1)}, u32[]{:S(2)}, u32[]{:S(2)}) %collective-permute-start.7) | collective-permute-done | bytes 258080 | tf_op jit(solution)/shard_map/ppermute | solution.py:24
  63.9 2.7 %all-to-all-done = bf16[8,56,896]{2,1,0:T(8,128)(2,1)S(1)} async-done(((bf16[8,56,896]{2,1,0:T(8,128)(2,1)}), bf16[8,56,896]{2,1,0:T(8,128)(2,1)S(1)}, u32[]{:S(2)}, u32[]{:S(2)}) %all-to-all-start) | async-done | bytes 802848 | tf_op jit(solution)/shard_map/all_to_all | solution.py:108
  66.7 4.9 %all-to-all-start.1 = ((bf16[8,56,896]{2,1,0:T(8,128)(2,1)}), bf16[8,56,896]{2,1,0:T(8,128)(2,1)S(1)}, u32[]{:S(2)}, u32[]{:S(2)}) async-start(bf16[8,56,896]{2,1,0:T(8,128)(2,1)} %bitcast.21), calls=%async_computation.1 | async-start | bytes 1605632 | tf_op jit(solution)/shard_map/all_to_all | solution.py:108
  71.7 3.3 %collective-permute-start.12 = (bf16[56,896]{1,0:T(8,128)(2,1)S(1)}, bf16[56,896]{1,0:T(8,128)(2,1)S(1)}, u32[]{:S(2)}, u32[]{:S(2)}) collective-permute-start(bf16[56,896]{1,0:T(8,128)(2,1)S(1)} %reduce_sum.24), channel_id=1, source_target_pairs={{0,16},{16,0},{1,17},{17,1},{2,18},{18,2},{3,19},{19,3},{4,20},{20... | collective-permute-start | bytes 301064 | tf_op jit(solution)/shard_map/ppermute | solution.py:28
  75.0 3.1 %collective-permute-done.12 = bf16[56,896]{1,0:T(8,128)(2,1)S(1)} collective-permute-done((bf16[56,896]{1,0:T(8,128)(2,1)S(1)}, bf16[56,896]{1,0:T(8,128)(2,1)S(1)}, u32[]{:S(2)}, u32[]{:S(2)}) %collective-permute-start.12) | collective-permute-done | bytes 100384 | tf_op jit(solution)/shard_map/ppermute | solution.py:28
  80.2 11.3 %collective-permute-done.14 = bf16[56,896]{1,0:T(8,128)(2,1)S(1)} collective-permute-done((bf16[56,896]{1,0:T(8,128)(2,1)S(1)}, bf16[56,896]{1,0:T(8,128)(2,1)S(1)}, u32[]{:S(2)}, u32[]{:S(2)}) %collective-permute-start.14) | collective-permute-done | bytes 100384 | tf_op jit(solution)/shard_map/ppermute | solution.py:24
  91.6 3.5 %all-to-all-done.1 = bf16[8,56,896]{2,1,0:T(8,128)(2,1)S(1)} async-done(((bf16[8,56,896]{2,1,0:T(8,128)(2,1)}), bf16[8,56,896]{2,1,0:T(8,128)(2,1)S(1)}, u32[]{:S(2)}, u32[]{:S(2)}) %all-to-all-start.1) | async-done | bytes 802848 | tf_op jit(solution)/shard_map/all_to_all | solution.py:108
  95.1 3.1 %collective-permute-start.13 = (bf16[56,896]{1,0:T(8,128)(2,1)S(1)}, bf16[56,896]{1,0:T(8,128)(2,1)S(1)}, u32[]{:S(2)}, u32[]{:S(2)}) collective-permute-start(bf16[56,896]{1,0:T(8,128)(2,1)S(1)} %reduce_sum.25), channel_id=1, source_target_pairs={{0,16},{16,0},{1,17},{17,1},{2,18},{18,2},{3,19},{19,3},{4,20},{20... | collective-permute-start | bytes 301064 | tf_op jit(solution)/shard_map/ppermute | solution.py:28
  98.3 3.1 %collective-permute-done.13 = bf16[56,896]{1,0:T(8,128)(2,1)S(1)} collective-permute-done((bf16[56,896]{1,0:T(8,128)(2,1)S(1)}, bf16[56,896]{1,0:T(8,128)(2,1)S(1)}, u32[]{:S(2)}, u32[]{:S(2)}) %collective-permute-start.13) | collective-permute-done | bytes 100384 | tf_op jit(solution)/shard_map/ppermute | solution.py:28
  103.6 2.5 %collective-permute-done.15 = bf16[56,896]{1,0:T(8,128)(2,1)S(1)} collective-permute-done((bf16[56,896]{1,0:T(8,128)(2,1)S(1)}, bf16[56,896]{1,0:T(8,128)(2,1)S(1)}, u32[]{:S(2)}, u32[]{:S(2)}) %collective-permute-start.15) | collective-permute-done | bytes 100384 | tf_op jit(solution)/shard_map/ppermute | solution.py:24
  109.9 2.6 %collective-permute-start.21 = (bf16[56,1792]{1,0:T(8,128)(2,1)S(1)}, bf16[56,1792]{1,0:T(8,128)(2,1)S(1)}, u32[]{:S(2)}, u32[]{:S(2)}) collective-permute-start(bf16[56,1792]{1,0:T(8,128)(2,1)S(1)} %constant_dynamic-update-slice_fusion.7), channel_id=1, source_target_pairs={{0,192},{32,224},{64,0},{96,32},{128,64},{160,96},{192,128},{224,1... | collective-permute-start | bytes 602120 | tf_op jit(solution)/shard_map/ppermute | solution.py:24
  112.5 7.3 %collective-permute-done.19 = bf16[56,1792]{1,0:T(8,128)(2,1)S(1)} collective-permute-done((bf16[56,1792]{1,0:T(8,128)(2,1)S(1)}, bf16[56,1792]{1,0:T(8,128)(2,1)S(1)}, u32[]{:S(2)}, u32[]{:S(2)}) %collective-permute-start.19) | collective-permute-done | bytes 200736 | tf_op jit(solution)/shard_map/ppermute | solution.py:24
  119.9 3.2 %collective-permute-start.23 = (bf16[56,896]{1,0:T(8,128)(2,1)S(1)}, bf16[56,896]{1,0:T(8,128)(2,1)S(1)}, u32[]{:S(2)}, u32[]{:S(2)}) collective-permute-start(bf16[56,896]{1,0:T(8,128)(2,1)S(1)} %slice.125), channel_id=1, source_target_pairs={{0,192},{32,224},{64,0},{96,32},{128,64},{160,96},{192,128},{224,1... | collective-permute-start | bytes 301064 | tf_op jit(solution)/shard_map/ppermute | solution.py:24
  124.1 4.0 %collective-permute-done.23 = bf16[56,896]{1,0:T(8,128)(2,1)S(1)} collective-permute-done((bf16[56,896]{1,0:T(8,128)(2,1)S(1)}, bf16[56,896]{1,0:T(8,128)(2,1)S(1)}, u32[]{:S(2)}, u32[]{:S(2)}) %collective-permute-start.23) | collective-permute-done | bytes 100384 | tf_op jit(solution)/shard_map/ppermute | solution.py:24
  128.0 2.7 %collective-permute-done.22 = bf16[56,896]{1,0:T(8,128)(2,1)S(1)} collective-permute-done((bf16[56,896]{1,0:T(8,128)(2,1)S(1)}, bf16[56,896]{1,0:T(8,128)(2,1)S(1)}, u32[]{:S(2)}, u32[]{:S(2)}) %collective-permute-start.22) | collective-permute-done | bytes 100384 | tf_op jit(solution)/shard_map/ppermute | solution.py:24
  132.0 2.5 %collective-permute-done.24 = bf16[448,1792]{1,0:T(8,128)(2,1)S(1)} collective-permute-done((bf16[448,1792]{1,0:T(8,128)(2,1)S(1)}, bf16[448,1792]{1,0:T(8,128)(2,1)S(1)}, u32[]{:S(2)}, u32[]{:S(2)}) %collective-permute-start.24) | collective-permute-done | bytes 1605664 | tf_op jit(solution)/shard_map/ppermute | solution.py:28
  142.2 10.3 %collective-permute-done.25 = bf16[448,576]{1,0:T(8,128)(2,1)S(1)} collective-permute-done((bf16[448,576]{1,0:T(8,128)(2,1)S(1)}, bf16[448,576]{1,0:T(8,128)(2,1)S(1)}, u32[]{:S(2)}, u32[]{:S(2)}) %collective-permute-start.25) | collective-permute-done | bytes 516128 | tf_op jit(solution)/shard_map/ppermute | solution.py:28
  152.5 2.4 %collective-permute-done.26 = bf16[448,576]{1,0:T(8,128)(2,1)S(1)} collective-permute-done((bf16[448,576]{1,0:T(8,128)(2,1)S(1)}, bf16[448,576]{1,0:T(8,128)(2,1)S(1)}, u32[]{:S(2)}, u32[]{:S(2)}) %collective-permute-start.26) | collective-permute-done | bytes 516128 | tf_op jit(solution)/shard_map/ppermute | solution.py:24
  160.7 7.6 %collective-permute-done.30 = bf16[224,576]{1,0:T(8,128)(2,1)S(1)} collective-permute-done((bf16[224,576]{1,0:T(8,128)(2,1)S(1)}, bf16[224,576]{1,0:T(8,128)(2,1)S(1)}, u32[]{:S(2)}, u32[]{:S(2)}) %collective-permute-start.30) | collective-permute-done | bytes 258080 | tf_op jit(solution)/shard_map/ppermute | solution.py:28
  174.5 3.5 %collective-permute-done.34 = bf16[224,576]{1,0:T(8,128)(2,1)S(1)} collective-permute-done((bf16[224,576]{1,0:T(8,128)(2,1)S(1)}, bf16[224,576]{1,0:T(8,128)(2,1)S(1)}, u32[]{:S(2)}, u32[]{:S(2)}) %collective-permute-start.34) | collective-permute-done | bytes 258080 | tf_op jit(solution)/shard_map/ppermute | solution.py:28
  (158 shorter events, 63.8 us)
Async XLA Ops:
  1.2 14.8 %collective-permute-start = (bf16[448,576]{1,0:T(8,128)(2,1)S(1)}, bf16[448,576]{1,0:T(8,128)(2,1)S(1)}, u32[]{:S(2)}, u32[]{:S(2)}) collective-permute-start(bf16[448,576]{1,0:T(8,128)(2,1)S(1)} %pad_maximum_fusion.5), channel_id=1, source_target_pairs={{0,4},{4,0},{1,5},{5,1},{2,6},{6,2},{3,7},{7,3},{8,12},{12,8},{9,1... | collective-permute-start | bytes 1548296 | tf_op jit(solution)/shard_map/ppermute | solution.py:28
  2.7 15.7 %collective-permute-start.1 = (bf16[448,576]{1,0:T(8,128)(2,1)S(1)}, bf16[448,576]{1,0:T(8,128)(2,1)S(1)}, u32[]{:S(2)}, u32[]{:S(2)}) collective-permute-start(bf16[448,576]{1,0:T(8,128)(2,1)S(1)} %pad_maximum_fusion.5), channel_id=1, source_target_pairs={{0,1},{1,2},{2,3},{3,0},{4,5},{5,6},{6,7},{7,4},{8,9},{9,10},{10,1... | collective-permute-start | bytes 1548296 | tf_op jit(solution)/shard_map/ppermute | solution.py:24
  4.3 14.2 %collective-permute-start.2 = (bf16[448,576]{1,0:T(8,128)(2,1)S(1)}, bf16[448,576]{1,0:T(8,128)(2,1)S(1)}, u32[]{:S(2)}, u32[]{:S(2)}) collective-permute-start(bf16[448,576]{1,0:T(8,128)(2,1)S(1)} %pad_maximum_fusion.5), channel_id=1, source_target_pairs={{0,3},{1,0},{2,1},{3,2},{4,7},{5,4},{6,5},{7,6},{8,11},{9,8},{10,9... | collective-permute-start | bytes 1548296 | tf_op jit(solution)/shard_map/ppermute | solution.py:24
  21.1 13.6 %collective-permute-start.3 = (bf16[336,576]{1,0:T(8,128)(2,1)S(1)}, bf16[336,576]{1,0:T(8,128)(2,1)S(1)}, u32[]{:S(2)}, u32[]{:S(2)}) collective-permute-start(bf16[336,576]{1,0:T(8,128)(2,1)S(1)} %get-tuple-element.62), channel_id=1, source_target_pairs={{0,1},{1,2},{2,3},{3,0},{4,5},{5,6},{6,7},{7,4},{8,9},{9,10},{10,1... | collective-permute-start | bytes 1161224 | tf_op jit(solution)/shard_map/ppermute | solution.py:24
  22.8 12.0 %collective-permute-start.4 = (bf16[336,576]{1,0:T(8,128)(2,1)S(1)}, bf16[336,576]{1,0:T(8,128)(2,1)S(1)}, u32[]{:S(2)}, u32[]{:S(2)}) collective-permute-start(bf16[336,576]{1,0:T(8,128)(2,1)S(1)} %get-tuple-element.61), channel_id=1, source_target_pairs={{0,3},{1,0},{2,1},{3,2},{4,7},{5,4},{6,5},{7,6},{8,11},{9,8},{10,9... | collective-permute-start | bytes 1161224 | tf_op jit(solution)/shard_map/ppermute | solution.py:24
  25.0 20.2 %collective-permute-start.9 = (bf16[224,576]{1,0:T(8,128)(2,1)S(1)}, bf16[224,576]{1,0:T(8,128)(2,1)}, u32[]{:S(2)}, u32[]{:S(2)}) collective-permute-start(bf16[224,576]{1,0:T(8,128)(2,1)S(1)} %get-tuple-element.46), channel_id=1, source_target_pairs={{0,4},{4,0},{1,5},{5,1},{2,6},{6,2},{3,7},{7,3},{8,12},{12,8},{9,1... | collective-permute-start | bytes 774152 | tf_op jit(solution)/shard_map/ppermute | solution.py:28
  36.0 10.8 %collective-permute-start.10 = (bf16[224,576]{1,0:T(8,128)(2,1)}, bf16[224,576]{1,0:T(8,128)(2,1)}, u32[]{:S(2)}, u32[]{:S(2)}) collective-permute-start(bf16[224,576]{1,0:T(8,128)(2,1)} %pad_maximum_fusion.11), channel_id=1, source_target_pairs={{0,4},{4,0},{1,5},{5,1},{2,6},{6,2},{3,7},{7,3},{8,12},{12,8},{9,1... | collective-permute-start | bytes 774152 | tf_op jit(solution)/shard_map/ppermute | solution.py:28
  36.6 30.1 %all-to-all-start = ((bf16[8,56,896]{2,1,0:T(8,128)(2,1)}), bf16[8,56,896]{2,1,0:T(8,128)(2,1)S(1)}, u32[]{:S(2)}, u32[]{:S(2)}) async-start(bf16[8,56,896]{2,1,0:T(8,128)(2,1)} %bitcast.2), calls=%async_computation | async-start | bytes 1605632 | tf_op jit(solution)/shard_map/all_to_all | solution.py:108
  50.7 10.6 %collective-permute-start.11 = (bf16[448,896]{1,0:T(8,128)(2,1)S(1)}, bf16[448,896]{1,0:T(8,128)(2,1)S(1)}, u32[]{:S(2)}, u32[]{:S(2)}) collective-permute-start(bf16[448,896]{1,0:T(8,128)(2,1)S(1)} %fusion.10), channel_id=1, source_target_pairs={{0,8},{8,0},{1,9},{9,1},{2,10},{10,2},{3,11},{11,3},{4,12},{12,4},... | collective-permute-start | bytes 2408456 | tf_op jit(solution)/shard_map/ppermute | solution.py:28
  50.8 10.5 %collective-permute-start.7 = (bf16[224,576]{1,0:T(8,128)(2,1)S(1)}, bf16[224,576]{1,0:T(8,128)(2,1)S(1)}, u32[]{:S(2)}, u32[]{:S(2)}) collective-permute-start(bf16[224,576]{1,0:T(8,128)(2,1)S(1)} %get-tuple-element.43), channel_id=1, source_target_pairs={{0,1},{1,2},{2,3},{3,0},{4,5},{5,6},{6,7},{7,4},{8,9},{9,10},{10,1... | collective-permute-start | bytes 774152 | tf_op jit(solution)/shard_map/ppermute | solution.py:24
  66.7 28.3 %all-to-all-start.1 = ((bf16[8,56,896]{2,1,0:T(8,128)(2,1)}), bf16[8,56,896]{2,1,0:T(8,128)(2,1)S(1)}, u32[]{:S(2)}, u32[]{:S(2)}) async-start(bf16[8,56,896]{2,1,0:T(8,128)(2,1)} %bitcast.21), calls=%async_computation.1 | async-start | bytes 1605632 | tf_op jit(solution)/shard_map/all_to_all | solution.py:108
  78.1 13.4 %collective-permute-start.14 = (bf16[56,896]{1,0:T(8,128)(2,1)S(1)}, bf16[56,896]{1,0:T(8,128)(2,1)S(1)}, u32[]{:S(2)}, u32[]{:S(2)}) collective-permute-start(bf16[56,896]{1,0:T(8,128)(2,1)S(1)} %add_convert_fusion.1), channel_id=1, source_target_pairs={{0,32},{32,64},{64,96},{96,128},{128,160},{160,192},{192,224},{224... | collective-permute-start | bytes 301064 | tf_op jit(solution)/shard_map/ppermute | solution.py:24
  79.7 18.6 %collective-permute-start.16 = (bf16[56,896]{1,0:T(8,128)(2,1)S(1)}, bf16[56,896]{1,0:T(8,128)(2,1)S(1)}, u32[]{:S(2)}, u32[]{:S(2)}) collective-permute-start(bf16[56,896]{1,0:T(8,128)(2,1)S(1)} %add_convert_fusion.1), channel_id=1, source_target_pairs={{0,224},{32,0},{64,32},{96,64},{128,96},{160,128},{192,160},{224,1... | collective-permute-start | bytes 301064 | tf_op jit(solution)/shard_map/ppermute | solution.py:24
  106.1 17.0 %collective-permute-start.18 = (bf16[56,1792]{1,0:T(8,128)(2,1)S(1)}, bf16[56,1792]{1,0:T(8,128)(2,1)S(1)}, u32[]{:S(2)}, u32[]{:S(2)}) collective-permute-start(bf16[56,1792]{1,0:T(8,128)(2,1)S(1)} %constant_dynamic-update-slice_fusion.5), channel_id=1, source_target_pairs={{0,32},{32,64},{64,96},{96,128},{128,160},{160,192},{192,224},{224... | collective-permute-start | bytes 602120 | tf_op jit(solution)/shard_map/ppermute | solution.py:24
  107.4 16.6 %collective-permute-start.20 = (bf16[56,1792]{1,0:T(8,128)(2,1)S(1)}, bf16[56,1792]{1,0:T(8,128)(2,1)S(1)}, u32[]{:S(2)}, u32[]{:S(2)}) collective-permute-start(bf16[56,1792]{1,0:T(8,128)(2,1)S(1)} %constant_dynamic-update-slice_fusion.5), channel_id=1, source_target_pairs={{0,64},{32,96},{64,128},{96,160},{128,192},{160,224},{192,0},{224,... | collective-permute-start | bytes 602120 | tf_op jit(solution)/shard_map/ppermute | solution.py:24
  109.8 10.1 %collective-permute-start.19 = (bf16[56,1792]{1,0:T(8,128)(2,1)S(1)}, bf16[56,1792]{1,0:T(8,128)(2,1)S(1)}, u32[]{:S(2)}, u32[]{:S(2)}) collective-permute-start(bf16[56,1792]{1,0:T(8,128)(2,1)S(1)} %constant_dynamic-update-slice_fusion.7), channel_id=1, source_target_pairs={{0,224},{32,0},{64,32},{96,64},{128,96},{160,128},{192,160},{224,1... | collective-permute-start | bytes 602120 | tf_op jit(solution)/shard_map/ppermute | solution.py:24
  109.9 14.1 %collective-permute-start.21 = (bf16[56,1792]{1,0:T(8,128)(2,1)S(1)}, bf16[56,1792]{1,0:T(8,128)(2,1)S(1)}, u32[]{:S(2)}, u32[]{:S(2)}) collective-permute-start(bf16[56,1792]{1,0:T(8,128)(2,1)S(1)} %constant_dynamic-update-slice_fusion.7), channel_id=1, source_target_pairs={{0,192},{32,224},{64,0},{96,32},{128,64},{160,96},{192,128},{224,1... | collective-permute-start | bytes 602120 | tf_op jit(solution)/shard_map/ppermute | solution.py:24
  137.4 15.1 %collective-permute-start.25 = (bf16[448,576]{1,0:T(8,128)(2,1)S(1)}, bf16[448,576]{1,0:T(8,128)(2,1)S(1)}, u32[]{:S(2)}, u32[]{:S(2)}) collective-permute-start(bf16[448,576]{1,0:T(8,128)(2,1)S(1)} %pad_maximum_fusion.6), channel_id=1, source_target_pairs={{0,4},{4,0},{1,5},{5,1},{2,6},{6,2},{3,7},{7,3},{8,12},{12,8},{9,1... | collective-permute-start | bytes 1548296 | tf_op jit(solution)/shard_map/ppermute | solution.py:28
  139.0 15.9 %collective-permute-start.26 = (bf16[448,576]{1,0:T(8,128)(2,1)S(1)}, bf16[448,576]{1,0:T(8,128)(2,1)S(1)}, u32[]{:S(2)}, u32[]{:S(2)}) collective-permute-start(bf16[448,576]{1,0:T(8,128)(2,1)S(1)} %pad_maximum_fusion.6), channel_id=1, source_target_pairs={{0,1},{1,2},{2,3},{3,0},{4,5},{5,6},{6,7},{7,4},{8,9},{9,10},{10,1... | collective-permute-start | bytes 1548296 | tf_op jit(solution)/shard_map/ppermute | solution.py:24
  140.1 14.8 %collective-permute-start.27 = (bf16[448,576]{1,0:T(8,128)(2,1)S(1)}, bf16[448,576]{1,0:T(8,128)(2,1)S(1)}, u32[]{:S(2)}, u32[]{:S(2)}) collective-permute-start(bf16[448,576]{1,0:T(8,128)(2,1)S(1)} %pad_maximum_fusion.6), channel_id=1, source_target_pairs={{0,3},{1,0},{2,1},{3,2},{4,7},{5,4},{6,5},{7,6},{8,11},{9,8},{10,9... | collective-permute-start | bytes 1548296 | tf_op jit(solution)/shard_map/ppermute | solution.py:24
  155.1 14.1 %collective-permute-start.28 = (bf16[336,576]{1,0:T(8,128)(2,1)S(1)}, bf16[336,576]{1,0:T(8,128)(2,1)S(1)}, u32[]{:S(2)}, u32[]{:S(2)}) collective-permute-start(bf16[336,576]{1,0:T(8,128)(2,1)S(1)} %get-tuple-element.60), channel_id=1, source_target_pairs={{0,1},{1,2},{2,3},{3,0},{4,5},{5,6},{6,7},{7,4},{8,9},{9,10},{10,1... | collective-permute-start | bytes 1161224 | tf_op jit(solution)/shard_map/ppermute | solution.py:24
  156.3 12.9 %collective-permute-start.29 = (bf16[336,576]{1,0:T(8,128)(2,1)S(1)}, bf16[336,576]{1,0:T(8,128)(2,1)S(1)}, u32[]{:S(2)}, u32[]{:S(2)}) collective-permute-start(bf16[336,576]{1,0:T(8,128)(2,1)S(1)} %get-tuple-element.59), channel_id=1, source_target_pairs={{0,3},{1,0},{2,1},{3,2},{4,7},{5,4},{6,5},{7,6},{8,11},{9,8},{10,9... | collective-permute-start | bytes 1161224 | tf_op jit(solution)/shard_map/ppermute | solution.py:24
  159.1 15.3 %collective-permute-start.33 = (bf16[224,576]{1,0:T(8,128)(2,1)S(1)}, bf16[224,576]{1,0:T(8,128)(2,1)S(1)}, u32[]{:S(2)}, u32[]{:S(2)}) collective-permute-start(bf16[224,576]{1,0:T(8,128)(2,1)S(1)} %get-tuple-element.36), channel_id=1, source_target_pairs={{0,4},{4,0},{1,5},{5,1},{2,6},{6,2},{3,7},{7,3},{8,12},{12,8},{9,1... | collective-permute-start | bytes 774152 | tf_op jit(solution)/shard_map/ppermute | solution.py:28
  160.7 18.2 %collective-permute-start.31 = (bf16[224,576]{1,0:T(8,128)(2,1)S(1)}, bf16[224,576]{1,0:T(8,128)(2,1)S(1)}, u32[]{:S(2)}, u32[]{:S(2)}) collective-permute-start(bf16[224,576]{1,0:T(8,128)(2,1)S(1)} %get-tuple-element.39), channel_id=1, source_target_pairs={{0,1},{1,2},{2,3},{3,0},{4,5},{5,6},{6,7},{7,4},{8,9},{9,10},{10,1... | collective-permute-start | bytes 774152 | tf_op jit(solution)/shard_map/ppermute | solution.py:24
  (36 other events, 206.2 us)
